TPU v7x, 512 devices: a whole 4x4x16 slice. The times are simulated.
512 devices in a mesh: req: 64 (over z, y), tensor: 8 (over x, core).
Axes of the slice: x: 4, y: 4, z: 16, core: 2. Of those that a mesh axis runs over, the one named last changes fastest.
Arguments:
- tokens: bfloat16 [16384, 2048], P('req', 'tensor'), may hold values from -6 to 6
- segment_ids: int32 [16384], P('req'), may hold values from 0 to 42, as said below
- prefix_lengths: int32 [43], replicated, may hold values from 0 to 256, as said below
- page_owner: int32 [4096, 1], P('req'), may hold values from 0 to 63; in each aligned block of 64 rows (0 to 63, 64 to 127, ...) at most 2 rows name the same one
- slot_perm: int32 [64, 128], P('req'), may hold values from 0 to 127, each once within a row
- ln_gain: float32 [2048], replicated, may hold values from 0.1 to 1.9
- ln_bias: float32 [2048], replicated, may hold values from -3 to 3
- qkv_weight: bfloat16 [2048, 3, 2048], P('req', None, 'tensor')
- qkv_bias: float32 [3, 2048], P(None, 'tensor'), may hold values from -3 to 3
- dense_weight: bfloat16 [2048, 2048], P('tensor', 'req'), may hold values from -0.375 to 0.375
- dense_bias: float32 [2048], P('tensor'), may hold values from -3 to 3
- fc1_weight: bfloat16 [2048, 4096], P('req', 'tensor'), may hold values from -0.125 to 0.125
- fc1_bias: float32 [4096], P('tensor'), may hold values from -3 to 3
- fc2_weight: bfloat16 [4096, 2048], P('tensor', 'req'), may hold values from -0.25 to 0.25
- fc2_bias: float32 [2048], P('tensor'), may hold values from -3 to 3
- prefix_cache: bfloat16 [16384, 2, 2048], P('req', None, 'tensor'), may hold values from -9 to 9
- cache_pool: bfloat16 [32768, 2, 2048], P('req', None, 'tensor'), may hold values from -6 to 6
Outputs:
- layer_out: bfloat16 [16384, 2048], P('req', 'tensor')
- new_pool: bfloat16 [32768, 2, 2048], P('req', None, 'tensor')
Inputs may be any that keep to these rules, and one draw needn't show every extreme that they name: `segment_ids`: labels 1 to 42 appear in order, each as one run of 257 to 512 rows, together filling all rows before the padding; segment 1 is 512 rows long; the last 128 rows are 0. `prefix_lengths`: entry 0 is 0 and entry 1 is 256. `page_owner`: among the pages of one index of req no owner appears more than 2 times, and some owner appears exactly 2 times. `slot_perm`: each row is a permutation of 0 to 127.
All inputs are finite; a program needn't handle non-finite values.
Results may differ from a plain program's by a relative error of at most 0.006.
The roundings to bfloat16 on the way count: a program that leaves them out, or rounds other values in their place, can miss the bound.
Values may be sent and summed in bfloat16 or wider, within the bound.
A program may use at most 64 MiB of HBM per device.

v0:
```python
import jax
import jax.numpy as jnp
from jax import lax
from jax.sharding import PartitionSpec as P

HEAD_DIM = 64
ROT = 32
SPAN = 2
SINKS = 4
PAGE = 4
WINDOW = 512


EPSILON = 1e-05


def from_behind(value, axis, steps):
    count = lax.axis_size(axis)
    leading, last = (max(0, -steps), min(count, count - steps))
    return lax.ppermute(value, axis, [(source, source + steps) for source in range(leading, last)])


def norm_rows(widened, gain, offset_bias):
    average = jnp.mean(widened, axis=-1, keepdims=True)
    centred = widened - average
    spread = jnp.mean(centred * centred, axis=-1, keepdims=True)
    return (centred * lax.rsqrt(spread + EPSILON) * gain + offset_bias).astype(jnp.bfloat16)


def label_rows(places, starts, prefix_lengths):
    labels = jnp.arange(starts.shape[0], dtype=jnp.int32)
    passed = (starts[None, :] <= places[:, None]) & (labels[None, :] >= 1)
    counted = jnp.sum(passed.astype(jnp.int32), axis=1)
    segment = jnp.where(places >= starts[0], 0, counted)
    segment = jnp.where(places < 0, -2, segment)
    onehot = segment[:, None] == labels[None, :]
    earliest = jnp.sum(jnp.where(onehot, starts[None, :], 0), axis=1)
    offset = jnp.sum(jnp.where(onehot, prefix_lengths[None, :], 0), axis=1)
    return (segment, offset + places - earliest)


def prefix_rows(block_id, rows_dev, prefix_count, starts, prefix_lengths):
    labels = jnp.arange(starts.shape[0], dtype=jnp.int32)
    located = (starts >= block_id * rows_dev) & (starts < (block_id + 1) * rows_dev) & (labels >= 1)
    owner_label = jnp.sum(jnp.where(located, labels, 0))
    length = jnp.sum(jnp.where(located, prefix_lengths, 0))
    places = jnp.arange(prefix_count, dtype=jnp.int32)
    usable = jnp.any(located) & (places < length)
    return (jnp.where(usable, owner_label, -2), places)


def rotate_heads(values, position):
    half_rot = ROT // 2
    frequency = 10000.0 ** (-2.0 * jnp.arange(half_rot, dtype=jnp.float32) / ROT)
    angles = position.astype(jnp.float32)[:, None] * frequency[None, :]
    cosine = jnp.cos(angles)[:, None, :]
    sine_vals = jnp.sin(angles)[:, None, :]
    lower = values[..., :half_rot]
    upper = values[..., half_rot:ROT]
    return jnp.concatenate(
        [lower * cosine - upper * sine_vals, upper * cosine + lower * sine_vals, values[..., ROT:]],
        axis=-1,
    )


def head_attention(query_rows, key_rows, value_rows, allowed):
    head_count = query_rows.shape[1] // HEAD_DIM
    score_scale = HEAD_DIM ** (-0.5)

    def one_head(head_index):
        query_cols = lax.dynamic_slice_in_dim(query_rows, head_index * HEAD_DIM, HEAD_DIM, 1)
        key_cols = lax.dynamic_slice_in_dim(key_rows, head_index * HEAD_DIM, HEAD_DIM, 1)
        value_cols = lax.dynamic_slice_in_dim(value_rows, head_index * HEAD_DIM, HEAD_DIM, 1)
        scores = (
            lax.dot_general(
                query_cols, key_cols, (((1,), (1,)), ((), ())), preferred_element_type=jnp.float32
            )
            * score_scale
        )
        masked = jnp.where(allowed, scores, -1e30)
        highest = jnp.max(masked, axis=1, keepdims=True)
        expo = jnp.where(allowed, jnp.exp(masked - highest), 0.0)
        denom = jnp.sum(expo, axis=1, keepdims=True)
        mixed = (
            jnp.dot(expo.astype(jnp.bfloat16), value_cols, preferred_element_type=jnp.float32)
            / denom
        )
        return mixed.astype(jnp.bfloat16)

    outcome = lax.map(one_head, jnp.arange(head_count, dtype=jnp.int32))
    return jnp.transpose(outcome, (1, 0, 2)).reshape(query_rows.shape[0], head_count * HEAD_DIM)


def shards(
    tokens,
    segment_ids,
    prefix_lengths,
    page_owner,
    slot_perm,
    ln_gain,
    ln_bias,
    qkv_weight,
    qkv_bias,
    dense_weight,
    dense_bias,
    fc1_weight,
    fc1_bias,
    fc2_weight,
    fc2_bias,
    prefix_cache,
    cache_pool,
):
    req_count = lax.axis_size("req")
    req_index = lax.axis_index("req")
    tok_rows = tokens.shape[0]
    prefix_count = prefix_cache.shape[0]
    head_cols = qkv_weight.shape[2]
    pool_count = slot_perm.shape[1]
    page_cap = pool_count // req_count
    gathered = lax.all_gather(tokens, "tensor", axis=1, tiled=True)
    normed = norm_rows(gathered.astype(jnp.float32), ln_gain, ln_bias)
    row_ids = jnp.arange(tok_rows, dtype=jnp.int32)
    places = req_index * tok_rows + row_ids
    labels = jnp.arange(prefix_lengths.shape[0], dtype=jnp.int32)
    beyond = tok_rows * req_count
    earliest_rows = jnp.min(
        jnp.where(segment_ids[:, None] == labels[None, :], places[:, None], beyond), axis=0
    )
    starts = lax.pmin(earliest_rows, "req")

    def add_rows(portion):
        return jnp.dot(normed, portion, preferred_element_type=jnp.float32)

    qkv_local = qkv_weight.reshape(qkv_weight.shape[0], 3 * head_cols)
    projected = add_rows(lax.all_gather(qkv_local, "req", axis=0, tiled=True))
    lifted = add_rows(lax.all_gather(fc1_weight, "req", axis=0, tiled=True))
    projected = (projected + qkv_bias.reshape(1, 3 * head_cols)).reshape(
        tok_rows, 3, head_cols // HEAD_DIM, HEAD_DIM
    )
    segment, position = label_rows(places, starts, prefix_lengths)
    queries = (
        rotate_heads(projected[:, 0], position).astype(jnp.bfloat16).reshape(tok_rows, head_cols)
    )
    new_keys = (
        rotate_heads(projected[:, 1], position).astype(jnp.bfloat16).reshape(tok_rows, head_cols)
    )
    new_values = projected[:, 2].astype(jnp.bfloat16).reshape(tok_rows, head_cols)
    key_value = jnp.stack([new_keys, new_values], axis=1)
    pages_here = tok_rows // PAGE
    pages = key_value.reshape(pages_here, PAGE * 2 * head_cols)
    owners = page_owner[:, 0]
    onehot = (owners[:, None] == jnp.arange(req_count, dtype=jnp.int32)[None, :]).astype(jnp.int32)
    earlier = jnp.cumsum(onehot, axis=0) - onehot
    earlier_count = jnp.sum(earlier * onehot, axis=1)
    target = owners * page_cap + earlier_count
    selecting = (target[None, :] == jnp.arange(pool_count, dtype=jnp.int32)[:, None]).astype(
        jnp.bfloat16
    )
    outgoing = jnp.dot(selecting, pages, preferred_element_type=jnp.float32).astype(jnp.bfloat16)
    filled = jnp.sum(selecting, axis=1)
    incoming, incoming_filled = (
        lax.all_to_all(
            outgoing.reshape(req_count, page_cap, PAGE * 2 * head_cols),
            "req",
            split_axis=0,
            concat_axis=0,
            tiled=True,
        ),
        lax.all_to_all(
            filled.reshape(req_count, page_cap), "req", split_axis=0, concat_axis=0, tiled=True
        ),
    )
    slot_ids = slot_perm[0]
    placing = (slot_ids[None, :] == jnp.arange(pool_count, dtype=jnp.int32)[:, None]) & (
        incoming_filled.reshape(pool_count)[None, :] > 0
    )
    written = jnp.dot(
        placing.astype(jnp.bfloat16),
        incoming.reshape(pool_count, PAGE * 2 * head_cols),
        preferred_element_type=jnp.float32,
    ).astype(jnp.bfloat16)
    written_mask = jnp.any(placing, axis=1)
    pool_pages = cache_pool.reshape(pool_count, PAGE * 2 * head_cols)
    new_pool = jnp.where(written_mask[:, None], written, pool_pages).reshape(cache_pool.shape)
    local_keys = jnp.concatenate([key_value, prefix_cache], axis=0)
    blocks = [local_keys]
    for shift_by in range(1, SPAN + 1):
        blocks.append(from_behind(local_keys, "req", shift_by))
    key_segs = []
    key_poss = []
    for step_back in range(SPAN + 1):
        block_id = req_index - step_back
        seg_new, pos_new = label_rows(block_id * tok_rows + row_ids, starts, prefix_lengths)
        seg_old, pos_old = prefix_rows(block_id, tok_rows, prefix_count, starts, prefix_lengths)
        key_segs.extend([seg_new, seg_old])
        key_poss.extend([pos_new, pos_old])
    key_segment = jnp.concatenate(key_segs)
    key_position = jnp.concatenate(key_poss)
    allowed = (key_segment[None, :] == segment[:, None]) & (
        key_position[None, :] <= position[:, None]
    )
    allowed = allowed & (
        (position[:, None] - key_position[None, :] < WINDOW) | (key_position[None, :] < SINKS)
    )
    all_keys = jnp.concatenate(blocks, axis=0)
    attended = head_attention(queries, all_keys[:, 0, :], all_keys[:, 1, :], allowed)
    hidden = jax.nn.gelu(lifted + fc1_bias, approximate=True).astype(jnp.bfloat16)
    attn_part = jnp.dot(
        attended,
        lax.all_gather(dense_weight, "req", axis=1, tiled=True),
        preferred_element_type=jnp.float32,
    )
    mlp_part = jnp.dot(
        hidden,
        lax.all_gather(fc2_weight, "req", axis=1, tiled=True),
        preferred_element_type=jnp.float32,
    )
    branches = attn_part + mlp_part
    summed = lax.psum_scatter(branches, "tensor", scatter_dimension=1, tiled=True)
    layer_out = (tokens.astype(jnp.float32) + summed + dense_bias + fc2_bias).astype(jnp.bfloat16)
    return (layer_out, new_pool)


def solution(mesh):
    placed = (
        P("req", "tensor"),
        P("req"),
        P(),
        P("req", None),
        P("req", None),
        P(),
        P(),
        P("req", None, "tensor"),
        P(None, "tensor"),
        P("tensor", "req"),
        P("tensor"),
        P("req", "tensor"),
        P("tensor"),
        P("tensor", "req"),
        P("tensor"),
        P("req", None, "tensor"),
        P("req", None, "tensor"),
    )
    return jax.shard_map(
        shards,
        mesh=mesh,
        in_specs=placed,
        out_specs=(P("req", "tensor"), P("req", None, "tensor")),
        check_vma=False,
    )
```

profile of v0, /device:TPU:6, one launch (start us, length us, event | category | flops | bytes accessed | tf_op | source)
XLA Modules:
  0.0 680.2 jit_solution(15321426984740319894)
XLA Ops:
  12.2 34.2 %pmin.7 = s32[43]{0:T(128)S(1)} all-reduce(s32[43]{0:T(128)S(1)} %select_reduce_fusion.6), channel_id=1, replica_groups=mesh['req'=64,'tensor'=8] {'req'}, use_global_device_ids=true, to_apply=%region_3.4 | all-reduce | flops 43 | bytes 344 | tf_op jit(solution)/shard_map/pmin | solution.py:129
  47.1 1.4 select_reduce_fusion.9
  49.4 1.9 constant_dynamic-update-slice_fusion.8
  51.3 1.9 constant_dynamic-update-slice_fusion.4
  56.2 1.5 convert_reduce_fusion
  57.7 1.6 fusion.23
  59.4 134.8 %all-gather.8.cloned.1.call-done = bf16[2048,768]{1,0:T(8,128)(2,1)} async-done(((bf16[32,768]{1,0:T(8,128)(2,1)}), bf16[2048,768]{1,0:T(8,128)(2,1)}) %all-gather.8.cloned.1.call-update) | async-done | bytes 3145744 | tf_op jit(solution)/shard_map/all_gather | solution.py:135
  194.2 3.0 convolution_add_fusion.1
  197.7 1.9 collective-permute-start
  199.6 4.1 collective-permute-start.1
  203.7 1.9 constant_dynamic-update-slice_fusion
  205.7 2.8 collective-permute-done
  208.5 5.8 collective-permute-done.1
  214.5 15.9 %while.11 = (s32[]{:T(128)}, bf16[4,256,64]{1,2,0:T(8,128)(2,1)S(1)}, s32[4]{0:T(128)S(1)}, bf16[256,256]{0,1:T(8,128)(2,1)S(1)}, bf16[1536,256]{0,1:T(8,128)(2,...) while((s32[]{:T(128)}, ...), condition=%wide.region_25.26_spmd.clone, body=%wide.region_22.25_spmd.clone.sunk | while | flops 112492032 | bytes 5240527 | solution.py:90
  230.4 100.3 %all-gather.10.cloned.1.call-done = bf16[256,2048]{0,1:T(8,128)(2,1)} async-done(((bf16[256,32]{0,1:T(8,128)(2,1)}), bf16[256,2048]{0,1:T(8,128)(2,1)}) %all-gather.10.cloned.1.call-update) | async-done | bytes 1048592 | tf_op jit(solution)/shard_map/all_gather | solution.py:210
  330.7 1.7 fusion.59
  332.5 138.2 %all-gather.12.cloned.1.call-done = bf16[2048,512]{1,0:T(8,128)(2,1)} async-done(((bf16[32,512]{1,0:T(8,128)(2,1)}), bf16[2048,512]{1,0:T(8,128)(2,1)}) %all-gather.12.cloned.1.call-update) | async-done | bytes 2097168 | tf_op jit(solution)/shard_map/all_gather | solution.py:136
  470.6 139.8 %all-gather.14.cloned.1.call-done = bf16[512,2048]{0,1:T(8,128)(2,1)} async-done(((bf16[512,32]{0,1:T(8,128)(2,1)}), bf16[512,2048]{0,1:T(8,128)(2,1)}) %all-gather.14.cloned.1.call-update) | async-done | bytes 2097168 | tf_op jit(solution)/shard_map/all_gather | solution.py:215
  610.4 5.1 convolution_add_fusion
  617.5 10.3 %all-to-all-start = ((bf16[64,1,2]{2,1,0:T(2,128)(2,1)}), bf16[64,1,2]{2,1,0:T(2,128)(2,1)S(1)}, u32[]{:S(2)}, u32[]{:S(2)}) async-start(bf16[64,1,2]{2,1,0:T(2,128)(2,1)} %all_to_all.12), calls=%async_computation.1 | async-start | bytes 65536 | tf_op jit(solution)/shard_map/all_to_all | solution.py:169
  629.7 12.6 %all-to-all-done = bf16[64,1,2]{2,1,0:T(2,128)(2,1)S(1)} async-done(((bf16[64,1,2]{2,1,0:T(2,128)(2,1)}), bf16[64,1,2]{2,1,0:T(2,128)(2,1)S(1)}, u32[]{:S(2)}, u32[]{:S(2)}) %all-to-all-start) | async-done | bytes 288 | tf_op jit(solution)/shard_map/all_to_all | solution.py:169
  642.3 4.6 all-to-all-start.1
  647.8 22.2 %all-to-all-done.1 = bf16[64,2,2048]{2,1,0:T(2,128)(2,1)S(1)} async-done(((bf16[64,2,2048]{2,1,0:T(2,128)(2,1)}), bf16[64,2,2048]{2,1,0:T(2,128)(2,1)S(1)}, u32[]{:S(2)}, u32[]{:S(2)}) %all-to-all-start.1) | async-done | bytes 524320 | tf_op jit(solution)/shard_map/all_to_all | solution.py:162
  671.7 1.7 add_convert_fusion
  (109 shorter events, 29.5 us)
Async XLA Ops:
  7.2 187.0 %copy-start.9 = (f32[2048]{0:T(1024)S(1)}, f32[2048]{0:T(1024)}, u32[]{:S(2)}) copy-start(f32[2048]{0:T(1024)} %param.24) | copy-start | bytes 24580
  7.2 187.0 %copy-start.7 = (f32[2048]{0:T(1024)S(1)}, f32[2048]{0:T(1024)}, u32[]{:S(2)}) copy-start(f32[2048]{0:T(1024)} %param.25) | copy-start | bytes 24580
  7.2 49.0 %all-gather.6.cloned.1.call-start = ((), (), s32[]{:S(2)}) async-start(), calls=%async_computation.3 | async-start | bytes 1179648 | tf_op jit(solution)/shard_map/all_gather | solution.py:120
  7.9 186.2 %all-gather.8.cloned.1.call-start = ((), (), s32[]{:S(2)}) async-start(), calls=%async_computation.4 | async-start | bytes 3194880 | tf_op jit(solution)/shard_map/all_gather | solution.py:135
  9.4 321.3 %all-gather.10.cloned.1.call-start = ((), (), s32[]{:S(2)}) async-start(), calls=%async_computation.5 | async-start | bytes 1064960 | tf_op jit(solution)/shard_map/all_gather | solution.py:210
  10.2 460.5 %all-gather.12.cloned.1.call-start = ((), (), s32[]{:S(2)}) async-start(), calls=%async_computation.6 | async-start | bytes 2129920 | tf_op jit(solution)/shard_map/all_gather | solution.py:136
  10.7 599.7 %all-gather.14.cloned.1.call-start = ((), (), s32[]{:S(2)}) async-start(), calls=%async_computation.7 | async-start | bytes 2129920 | tf_op jit(solution)/shard_map/all_gather | solution.py:215
  11.3 660.3 %reduce-scatter.2.cloned.1.call-start = ((), (), s32[]{:S(2)}) async-start(), calls=%async_computation.8 | async-start | bytes 2359296 | tf_op jit(solution)/shard_map/reduce_scatter | solution.py:219
  56.1 138.0 %copy-start = (bf16[256,2048]{1,0:T(8,128)(2,1)S(1)}, bf16[256,2048]{1,0:T(8,128)(2,1)}, u32[]{:S(2)}) copy-start(bf16[256,2048]{1,0:T(8,128)(2,1)} %all-gather.6.cloned.1.call-done) | copy-start | bytes 3145732
  197.7 10.8 %collective-permute-start = (bf16[512,2,256]{0,2,1:T(8,128)(2,1)S(1)}, bf16[512,2,256]{0,2,1:T(8,128)(2,1)S(1)}, u32[]{:S(2)}, u32[]{:S(2)}) collective-permute-start(bf16[512,2,256]{0,2,1:T(8,128)(2,1)S(1)} %pad_maximum_fusion.1), channel_id=1, source_target_pairs={{0,8},{8,16},{16,24},{24,32},{32,40},{40,48},{48,56},{56,64},{64,7... | collective-permute-start | bytes 1572872 | tf_op jit(solution)/shard_map/ppermute | solution.py:20
  199.6 14.6 %collective-permute-start.1 = (bf16[512,2,256]{0,2,1:T(8,128)(2,1)S(1)}, bf16[512,2,256]{0,2,1:T(8,128)(2,1)S(1)}, u32[]{:S(2)}, u32[]{:S(2)}) collective-permute-start(bf16[512,2,256]{0,2,1:T(8,128)(2,1)S(1)} %pad_maximum_fusion.1), channel_id=1, source_target_pairs={{0,16},{8,24},{16,32},{24,40},{32,48},{40,56},{48,64},{56,72},{64,... | collective-permute-start | bytes 1572872 | tf_op jit(solution)/shard_map/ppermute | solution.py:20
  230.4 380.0 %copy-start.8 = (f32[2048]{0:T(1024)S(1)}, f32[2048]{0:T(1024)}, u32[]{:S(2)}) copy-start(f32[2048]{0:T(1024)} %param.25) | copy-start | bytes 24580
  615.5 0.7 copy-start.3
  617.5 24.9 %all-to-all-start = ((bf16[64,1,2]{2,1,0:T(2,128)(2,1)}), bf16[64,1,2]{2,1,0:T(2,128)(2,1)S(1)}, u32[]{:S(2)}, u32[]{:S(2)}) async-start(bf16[64,1,2]{2,1,0:T(2,128)(2,1)} %all_to_all.12), calls=%async_computation.1 | async-start | bytes 65536 | tf_op jit(solution)/shard_map/all_to_all | solution.py:169
  627.8 19.2 %copy-start.1 = (bf16[512,2,256]{2,1,0:T(2,128)(2,1)S(1)}, bf16[512,2,256]{2,1,0:T(2,128)(2,1)}, u32[]{:S(2)}) copy-start(bf16[512,2,256]{2,1,0:T(2,128)(2,1)} %param.35) | copy-start | bytes 1572868
  628.1 19.5 %copy-start.6 = (s32[1,128]{1,0:T(1,128)S(1)}, s32[1,128]{1,0:T(1,128)}, u32[]{:S(2)}) copy-start(s32[1,128]{1,0:T(1,128)} %param.23) | copy-start | bytes 1540
  642.3 27.6 %all-to-all-start.1 = ((bf16[64,2,2048]{2,1,0:T(2,128)(2,1)}), bf16[64,2,2048]{2,1,0:T(2,128)(2,1)S(1)}, u32[]{:S(2)}, u32[]{:S(2)}) async-start(bf16[64,2,2048]{2,1,0:T(2,128)(2,1)} %reshape.254), calls=%async_computation.2 | async-start | bytes 1048576 | tf_op jit(solution)/shard_map/all_to_all | solution.py:162
  647.4 24.3 %copy-start.2 = (bf16[256,256]{1,0:T(8,128)(2,1)S(1)}, bf16[256,256]{1,0:T(8,128)(2,1)}, u32[]{:S(2)}) copy-start(bf16[256,256]{1,0:T(8,128)(2,1)} %param.19) | copy-start | bytes 393220
  647.4 24.3 %copy-start.4 = (f32[256]{0:T(256)S(1)}, f32[256]{0:T(256)}, u32[]{:S(2)}) copy-start(f32[256]{0:T(256)} %param.33) | copy-start | bytes 3076
  647.4 24.3 %copy-start.5 = (f32[256]{0:T(256)S(1)}, f32[256]{0:T(256)}, u32[]{:S(2)}) copy-start(f32[256]{0:T(256)} %param.29) | copy-start | bytes 3076
Sparse Core Ops, SparseCore 0:
  10.1 34.7 all-gather.5
  48.5 145.6 all-gather.7
  197.1 133.5 all-gather.9
  333.5 137.0 all-gather.11
  473.4 136.9 all-gather.13
  615.7 34.3 reduce-scatter.1
where the time goes:
time: 681 us; the launch traced here: 680 us
  waiting for transfers between devices  559 us (82%)
  blocking collectives  34.2 us (5%)
  starting transfers between devices  21.1 us (3%)
  other arithmetic  20 us (3%)
  matrix products  17.7 us (3%)
  between operations  14.6 us (2%)
  local copies, waits for them, and re-layouts  10.9 us (2%)
    all_gather x1, waiting for transfers between devices, shards(): lax.all_gather(fc2_weight, 'req', axis=1, tiled=True)  140 us
    all_gather x1, waiting for transfers between devices, shards(): lifted = add_rows(lax.all_gather(fc1_weight, 'req', axis=0, tiled=True))  138 us
    all_gather x1, waiting for transfers between devices, shards(): projected = add_rows(lax.all_gather(qkv_local, 'req', axis=0, tiled=True))  135 us
    all_gather x1, waiting for transfers between devices, shards(): lax.all_gather(dense_weight, 'req', axis=1, tiled=True)  100 us
    pmin x1, blocking collectives, shards(): starts = lax.pmin(earliest_rows, 'req')  34.2 us
    all_to_all x1, waiting for transfers between devices, shards(): lax.all_to_all(outgoing.reshape(req_count, page_cap, PAGE * 2 * head_cols...  22.2 us
  transfers between devices with their start and end apart: 10, of which 8 were waited for; matrix products, arithmetic and copies ran while one was open for 6% of the time, Pallas kernels for 0%

commit v1 on v0

--- a/solution.py
+++ b/solution.py
@@ -122,18 +122,42 @@
     row_ids = jnp.arange(tok_rows, dtype=jnp.int32)
     places = req_index * tok_rows + row_ids
     labels = jnp.arange(prefix_lengths.shape[0], dtype=jnp.int32)
+    label_count = labels.shape[0]
     beyond = tok_rows * req_count
     earliest_rows = jnp.min(
         jnp.where(segment_ids[:, None] == labels[None, :], places[:, None], beyond), axis=0
     )
-    starts = lax.pmin(earliest_rows, "req")
+    weight_rows = qkv_weight.shape[0]
+    digit_cols = 128
+    digits = jnp.concatenate([earliest_rows // 128, earliest_rows % 128]).astype(jnp.bfloat16)
+    digits = jnp.pad(digits, (0, weight_rows * digit_cols - 2 * label_count)).reshape(
+        weight_rows, digit_cols
+    )
+    qkv_local = qkv_weight.reshape(weight_rows, 3 * head_cols)
+    fc1_cols = fc1_weight.shape[1]
+    dense_cols = dense_weight.shape[0]
+    fc2_cols = fc2_weight.shape[0]
+    packed = jnp.concatenate(
+        [qkv_local, fc1_weight, dense_weight.T, fc2_weight.T, digits], axis=1
+    )
+    everything = lax.all_gather(packed, "req", axis=0, tiled=True)
+    edges = [0]
+    for width in (3 * head_cols, fc1_cols, dense_cols, fc2_cols, digit_cols):
+        edges.append(edges[-1] + width)
+    qkv_full, fc1_full, dense_full_t, fc2_full_t, digits_full = [
+        everything[:, edges[i] : edges[i + 1]] for i in range(5)
+    ]
+    digit_table = digits_full.reshape(req_count, weight_rows * digit_cols)[:, : 2 * label_count]
+    digit_table = digit_table.astype(jnp.int32)
+    starts = jnp.min(
+        digit_table[:, :label_count] * 128 + digit_table[:, label_count:], axis=0
+    )
 
     def add_rows(portion):
         return jnp.dot(normed, portion, preferred_element_type=jnp.float32)
 
-    qkv_local = qkv_weight.reshape(qkv_weight.shape[0], 3 * head_cols)
-    projected = add_rows(lax.all_gather(qkv_local, "req", axis=0, tiled=True))
-    lifted = add_rows(lax.all_gather(fc1_weight, "req", axis=0, tiled=True))
+    projected = add_rows(qkv_full)
+    lifted = add_rows(fc1_full)
     projected = (projected + qkv_bias.reshape(1, 3 * head_cols)).reshape(
         tok_rows, 3, head_cols // HEAD_DIM, HEAD_DIM
     )
@@ -147,7 +171,8 @@
     new_values = projected[:, 2].astype(jnp.bfloat16).reshape(tok_rows, head_cols)
     key_value = jnp.stack([new_keys, new_values], axis=1)
     pages_here = tok_rows // PAGE
-    pages = key_value.reshape(pages_here, PAGE * 2 * head_cols)
+    page_width = PAGE * 2 * head_cols
+    pages = key_value.reshape(pages_here, page_width)
     owners = page_owner[:, 0]
     onehot = (owners[:, None] == jnp.arange(req_count, dtype=jnp.int32)[None, :]).astype(jnp.int32)
     earlier = jnp.cumsum(onehot, axis=0) - onehot
@@ -158,29 +183,31 @@
     )
     outgoing = jnp.dot(selecting, pages, preferred_element_type=jnp.float32).astype(jnp.bfloat16)
     filled = jnp.sum(selecting, axis=1)
-    incoming, incoming_filled = (
-        lax.all_to_all(
-            outgoing.reshape(req_count, page_cap, PAGE * 2 * head_cols),
-            "req",
-            split_axis=0,
-            concat_axis=0,
-            tiled=True,
-        ),
-        lax.all_to_all(
-            filled.reshape(req_count, page_cap), "req", split_axis=0, concat_axis=0, tiled=True
-        ),
-    )
+    flag_cols = 128
+    flagged = jnp.concatenate(
+        [outgoing, jnp.broadcast_to(filled[:, None], (pool_count, flag_cols)).astype(jnp.bfloat16)],
+        axis=1,
+    )
+    arrived = lax.all_to_all(
+        flagged.reshape(req_count, page_cap, page_width + flag_cols),
+        "req",
+        split_axis=0,
+        concat_axis=0,
+        tiled=True,
+    ).reshape(pool_count, page_width + flag_cols)
+    incoming = arrived[:, :page_width]
+    incoming_filled = arrived[:, page_width]
     slot_ids = slot_perm[0]
     placing = (slot_ids[None, :] == jnp.arange(pool_count, dtype=jnp.int32)[:, None]) & (
-        incoming_filled.reshape(pool_count)[None, :] > 0
+        incoming_filled[None, :] > 0
     )
     written = jnp.dot(
         placing.astype(jnp.bfloat16),
-        incoming.reshape(pool_count, PAGE * 2 * head_cols),
+        incoming,
         preferred_element_type=jnp.float32,
     ).astype(jnp.bfloat16)
     written_mask = jnp.any(placing, axis=1)
-    pool_pages = cache_pool.reshape(pool_count, PAGE * 2 * head_cols)
+    pool_pages = cache_pool.reshape(pool_count, page_width)
     new_pool = jnp.where(written_mask[:, None], written, pool_pages).reshape(cache_pool.shape)
     local_keys = jnp.concatenate([key_value, prefix_cache], axis=0)
     blocks = [local_keys]
@@ -205,15 +232,12 @@
     all_keys = jnp.concatenate(blocks, axis=0)
     attended = head_attention(queries, all_keys[:, 0, :], all_keys[:, 1, :], allowed)
     hidden = jax.nn.gelu(lifted + fc1_bias, approximate=True).astype(jnp.bfloat16)
-    attn_part = jnp.dot(
-        attended,
-        lax.all_gather(dense_weight, "req", axis=1, tiled=True),
-        preferred_element_type=jnp.float32,
-    )
-    mlp_part = jnp.dot(
-        hidden,
-        lax.all_gather(fc2_weight, "req", axis=1, tiled=True),
-        preferred_element_type=jnp.float32,
+    contract_rows = (((1,), (1,)), ((), ()))
+    attn_part = lax.dot_general(
+        attended, dense_full_t, contract_rows, preferred_element_type=jnp.float32
+    )
+    mlp_part = lax.dot_general(
+        hidden, fc2_full_t, contract_rows, preferred_element_type=jnp.float32
     )
     branches = attn_part + mlp_part
     summed = lax.psum_scatter(branches, "tensor", scatter_dimension=1, tiled=True)

time: 681 us -> 321 us (0.47)
  waiting for transfers between devices: 559 us -> 234 us
  blocking collectives: 34.2 us -> 0 us
    all_gather x4 -> x1, waiting for transfers between devices: 513 us -> 161 us  [shards(): everything = lax.all_gather(packed, 'req', axis=0, tiled=True)]
    pmin x1 -> x0, blocking collectives: 34.2 us -> none  [shards(): starts = lax.pmin(earliest_rows, 'req')]
    all_gather x1, waiting for transfers between devices: 0.02 us -> 30.4 us  [shards(): gathered = lax.all_gather(tokens, 'tensor', axis=1, tiled=True)]
    all_to_all x2 -> x1, waiting for transfers between devices: 34.8 us -> 30.7 us  [shards(): lax.all_to_all(flagged.reshape(req_count, page_cap, page_width + flag_col...]
    all_to_all x2 -> x1, starting transfers between devices: 14.9 us -> 12.5 us  [shards(): lax.all_to_all(flagged.reshape(req_count, page_cap, page_width + flag_col...]
  transfers between devices with their start and end apart: 10 -> 6, of which waited for: 8 -> 5; matrix products, arithmetic and copies ran while one was open for 6% -> 5% of each run, Pallas kernels for 0% -> 0%
where the time goes in v1:
time: 321 us; the launch traced here: 320 us
  waiting for transfers between devices  234 us (73%)
  other arithmetic  18.5 us (6%)
  starting transfers between devices  18.3 us (6%)
  matrix products  17.8 us (6%)
  local copies, waits for them, and re-layouts  14.5 us (5%)
  between operations  14.3 us (4%)
    all_gather x1, waiting for transfers between devices, shards(): everything = lax.all_gather(packed, 'req', axis=0, tiled=True)  161 us
    all_to_all x1, waiting for transfers between devices, shards(): lax.all_to_all(flagged.reshape(req_count, page_cap, page_width + flag_col...  30.7 us
    all_gather x1, waiting for transfers between devices, shards(): gathered = lax.all_gather(tokens, 'tensor', axis=1, tiled=True)  30.4 us
    all_to_all x1, starting transfers between devices, shards(): lax.all_to_all(flagged.reshape(req_count, page_cap, page_width + flag_col...  12.5 us
    ppermute x2, waiting for transfers between devices, from_behind(): lax.ppermute(value, axis, [(source, source + steps) for source in range(l...  10.9 us
  transfers between devices with their start and end apart: 6, of which 5 were waited for; matrix products, arithmetic and copies ran while one was open for 5% of the time, Pallas kernels for 0%

profile of v1, /device:TPU:6, one launch (start us, length us, event | category | flops | bytes accessed | tf_op | source)
XLA Modules:
  0.0 319.7 jit_solution(9198134115274271958)
XLA Ops:
  13.4 1.1 copy.42
  14.5 30.4 %all-gather.3.cloned.1.call-done = bf16[256,2048]{1,0:T(8,128)(2,1)} async-done(((bf16[256,256]{1,0:T(8,128)(2,1)}), bf16[256,2048]{1,0:T(8,128)(2,1)}) %all-gather.3.cloned.1.call-update) | async-done | bytes 1048592 | tf_op jit(solution)/shard_map/all_gather | solution.py:120
  45.0 1.5 convert_reduce_fusion
  46.5 1.6 fusion.25
  48.1 160.8 %all-gather.5.cloned.1.call-done = bf16[2048,2176]{1,0:T(8,128)(2,1)} async-done(((bf16[32,2176]{1,0:T(8,128)(2,1)}), bf16[2048,2176]{1,0:T(8,128)(2,1)}) %all-gather.5.cloned.1.call-update) | async-done | bytes 8912912 | tf_op jit(solution)/shard_map/all_gather | solution.py:143
  209.0 3.0 fusion.32
  215.6 1.7 constant_dynamic-update-slice_fusion.14
  217.4 1.9 constant_dynamic-update-slice_fusion.8
  219.8 3.6 %collective-permute-start.1 = (bf16[512,2,256]{0,2,1:T(8,128)(2,1)S(1)}, bf16[512,2,256]{0,2,1:T(8,128)(2,1)S(1)}, u32[]{:S(2)}, u32[]{:S(2)}) collective-permute-start(bf16[512,2,256]{0,2,1:T(8,128)(2,1)S(1)} %pad_maximum_fusion.2), channel_id=1, source_target_pairs={{0,16},{8,24},{16,32},{24,40},{32,48},{40,56},{48,64},{56,72},{64,... | collective-permute-start | bytes 1572872 | tf_op jit(solution)/shard_map/ppermute | solution.py:20
  223.4 2.0 collective-permute-start
  225.5 1.8 constant_dynamic-update-slice_fusion.6
  227.4 5.3 %collective-permute-done.1 = bf16[512,2,256]{0,2,1:T(8,128)(2,1)S(1)} collective-permute-done((bf16[512,2,256]{0,2,1:T(8,128)(2,1)S(1)}, bf16[512,2,256]{0,2,1:T(8,128)(2,1)S(1)}, u32[]{:S(2)}, u32[]{:S(2)}) %collective-permute-start.1) | collective-permute-done | bytes 524320 | tf_op jit(solution)/shard_map/ppermute | solution.py:20
  232.7 5.6 %collective-permute-done = bf16[512,2,256]{0,2,1:T(8,128)(2,1)S(1)} collective-permute-done((bf16[512,2,256]{0,2,1:T(8,128)(2,1)S(1)}, bf16[512,2,256]{0,2,1:T(8,128)(2,1)S(1)}, u32[]{:S(2)}, u32[]{:S(2)}) %collective-permute-start) | collective-permute-done | bytes 524320 | tf_op jit(solution)/shard_map/ppermute | solution.py:20
  239.3 15.9 %while.11 = (s32[]{:T(128)}, bf16[4,256,64]{1,2,0:T(8,128)(2,1)S(1)}, s32[4]{0:T(128)S(1)}, bf16[256,256]{0,1:T(8,128)(2,1)S(1)}, bf16[1536,256]{0,1:T(8,128)(2,...) while((s32[]{:T(128)}, ...), condition=%wide.region_25.26_spmd.clone, body=%wide.region_22.25_spmd.clone.sunk | while | flops 112492032 | bytes 5240535 | solution.py:90
  241.5 0.9 fusion.96
  245.4 0.9 fusion.96
  249.4 0.9 fusion.96
  255.9 1.8 fusion.38
  257.7 5.1 %convolution_add_fusion = f32[256,2048]{1,0:T(8,128)} fusion(f32[256,2048]{1,0:T(8,128)S(1)} %fusion.38, bf16[2048,2176]{1,0:T(8,128)(2,1)} %all-gather.5.cloned.1.call-done, f32[512]{0:T(512)S(1)} %copy-done.13, bf16[256,2048]{1,0:T(8,128)(2,1)S(1)} %copy-done, f32[2048]{0:T(1024)S(1)} %copy-done.11, f32[2048]{0:T(1024)S(1)} %copy-done.12, ...), kind=kOutput, calls=%fused_computation.23 | convolution fusion | flops 1078722560 | bytes 9457664 | tf_op jit(solution)/shard_map/dot_general | solution.py:239
  264.9 1.0 reshape.258
  265.9 12.5 %all-to-all-start = ((bf16[64,2,2176]{2,1,0:T(2,128)(2,1)}), bf16[64,2,2176]{2,1,0:T(2,128)(2,1)S(1)}, u32[]{:S(2)}, u32[]{:S(2)}) async-start(bf16[64,2,2176]{2,1,0:T(2,128)(2,1)} %reshape.258), calls=%async_computation.1 | async-start | bytes 1114112 | tf_op jit(solution)/shard_map/all_to_all | solution.py:191
  278.9 30.7 %all-to-all-done = bf16[64,2,2176]{2,1,0:T(2,128)(2,1)S(1)} async-done(((bf16[64,2,2176]{2,1,0:T(2,128)(2,1)}), bf16[64,2,2176]{2,1,0:T(2,128)(2,1)S(1)}, u32[]{:S(2)}, u32[]{:S(2)}) %all-to-all-start) | async-done | bytes 557088 | tf_op jit(solution)/shard_map/all_to_all | solution.py:191
  310.3 1.2 reshape.261
  311.5 1.6 add_convert_fusion
  (116 shorter events, 25.4 us)
Async XLA Ops:
  7.2 201.8 %copy-start.11 = (f32[2048]{0:T(1024)S(1)}, f32[2048]{0:T(1024)}, u32[]{:S(2)}) copy-start(f32[2048]{0:T(1024)} %param.25) | copy-start | bytes 24580
  7.2 201.8 %copy-start.12 = (f32[2048]{0:T(1024)S(1)}, f32[2048]{0:T(1024)}, u32[]{:S(2)}) copy-start(f32[2048]{0:T(1024)} %param.24) | copy-start | bytes 24580
  7.2 37.8 %all-gather.3.cloned.1.call-start = ((), (), s32[]{:S(2)}) async-start(), calls=%async_computation.2 | async-start | bytes 1179648 | tf_op jit(solution)/shard_map/all_gather | solution.py:120
  7.9 201.0 %all-gather.5.cloned.1.call-start = ((), (), s32[]{:S(2)}) async-start(), calls=%async_computation.3 | async-start | bytes 9052160 | tf_op jit(solution)/shard_map/all_gather | solution.py:143
  11.9 0.7 copy-start.3
  12.6 298.9 %reduce-scatter.2.cloned.1.call-start = ((), (), s32[]{:S(2)}) async-start(), calls=%async_computation.4 | async-start | bytes 2359296 | tf_op jit(solution)/shard_map/reduce_scatter | solution.py:243
  45.0 164.0 %copy-start = (bf16[256,2048]{1,0:T(8,128)(2,1)S(1)}, bf16[256,2048]{1,0:T(8,128)(2,1)}, u32[]{:S(2)}) copy-start(bf16[256,2048]{1,0:T(8,128)(2,1)} %all-gather.3.cloned.1.call-done) | copy-start | bytes 3145732
  212.0 1.0 slice-start
  212.3 1.8 copy-start.7
  219.8 12.9 %collective-permute-start.1 = (bf16[512,2,256]{0,2,1:T(8,128)(2,1)S(1)}, bf16[512,2,256]{0,2,1:T(8,128)(2,1)S(1)}, u32[]{:S(2)}, u32[]{:S(2)}) collective-permute-start(bf16[512,2,256]{0,2,1:T(8,128)(2,1)S(1)} %pad_maximum_fusion.2), channel_id=1, source_target_pairs={{0,16},{8,24},{16,32},{24,40},{32,48},{40,56},{48,64},{56,72},{64,... | collective-permute-start | bytes 1572872 | tf_op jit(solution)/shard_map/ppermute | solution.py:20
  223.4 14.9 %collective-permute-start = (bf16[512,2,256]{0,2,1:T(8,128)(2,1)S(1)}, bf16[512,2,256]{0,2,1:T(8,128)(2,1)S(1)}, u32[]{:S(2)}, u32[]{:S(2)}) collective-permute-start(bf16[512,2,256]{0,2,1:T(8,128)(2,1)S(1)} %pad_maximum_fusion.2), channel_id=1, source_target_pairs={{0,8},{8,16},{16,24},{24,32},{32,40},{40,48},{48,56},{56,64},{64,7... | collective-permute-start | bytes 1572872 | tf_op jit(solution)/shard_map/ppermute | solution.py:20
  238.4 0.9 copy-start.4
  255.2 0.7 copy-start.5
  255.2 2.4 copy-start.13
  262.8 0.7 copy-start.6
  264.3 14.1 %copy-start.1 = (bf16[512,2,256]{2,1,0:T(2,128)(2,1)S(1)}, bf16[512,2,256]{2,1,0:T(2,128)(2,1)}, u32[]{:S(2)}) copy-start(bf16[512,2,256]{2,1,0:T(2,128)(2,1)} %param.35) | copy-start | bytes 1572868
  264.9 45.0 %copy-start.10 = (s32[1,128]{1,0:T(1,128)S(1)}, s32[1,128]{1,0:T(1,128)}, u32[]{:S(2)}) copy-start(s32[1,128]{1,0:T(1,128)} %param.23) | copy-start | bytes 1540
  265.9 43.7 %all-to-all-start = ((bf16[64,2,2176]{2,1,0:T(2,128)(2,1)}), bf16[64,2,2176]{2,1,0:T(2,128)(2,1)S(1)}, u32[]{:S(2)}, u32[]{:S(2)}) async-start(bf16[64,2,2176]{2,1,0:T(2,128)(2,1)} %reshape.258), calls=%async_computation.1 | async-start | bytes 1114112 | tf_op jit(solution)/shard_map/all_to_all | solution.py:191
  278.8 32.7 %copy-start.2 = (bf16[256,256]{1,0:T(8,128)(2,1)S(1)}, bf16[256,256]{1,0:T(8,128)(2,1)}, u32[]{:S(2)}) copy-start(bf16[256,256]{1,0:T(8,128)(2,1)} %param.19) | copy-start | bytes 393220
  278.8 32.7 %copy-start.8 = (f32[256]{0:T(256)S(1)}, f32[256]{0:T(256)}, u32[]{:S(2)}) copy-start(f32[256]{0:T(256)} %param.33) | copy-start | bytes 3076
  278.9 32.7 %copy-start.9 = (f32[256]{0:T(256)S(1)}, f32[256]{0:T(256)}, u32[]{:S(2)}) copy-start(f32[256]{0:T(256)} %param.29) | copy-start | bytes 3076
Sparse Core Ops, SparseCore 0:
  10.1 34.7 all-gather.2
  48.5 160.4 all-gather.4
  262.9 36.6 reduce-scatter.1

commit v2 on v1

--- a/solution.py
+++ b/solution.py
@@ -1,6 +1,10 @@
+import functools
+
 import jax
 import jax.numpy as jnp
 from jax import lax
+from jax.experimental import pallas as pl
+from jax.experimental.pallas import tpu as pltpu
 from jax.sharding import PartitionSpec as P
 
 HEAD_DIM = 64
@@ -9,6 +13,99 @@
 SINKS = 4
 PAGE = 4
 WINDOW = 512
+INNER = 4
+
+
+MESH_IDS = pl.DeviceIdType.MESH
+
+
+def ring_gather_kernel(inner, outer, block_ref, out_ref, own_sem, send_sems, recv_sems):
+    req_index = lax.axis_index("req")
+    tensor_index = lax.axis_index("tensor")
+    here_outer = req_index // inner
+    here_inner = req_index % inner
+
+    def device(outer_at, inner_at):
+        outer_at = lax.rem(outer_at + outer, outer)
+        inner_at = lax.rem(inner_at + inner, inner)
+        return (outer_at * inner + inner_at, tensor_index)
+
+    neighbours = (
+        device(here_outer, here_inner + 1),
+        device(here_outer, here_inner - 1),
+        device(here_outer + 1, here_inner),
+        device(here_outer - 1, here_inner),
+    )
+    barrier = pltpu.get_barrier_semaphore()
+    for neighbour in neighbours:
+        pl.semaphore_signal(barrier, inc=1, device_id=neighbour, device_id_type=MESH_IDS)
+    pl.semaphore_wait(barrier, len(neighbours))
+
+    own = pltpu.make_async_copy(block_ref, out_ref.at[here_outer, here_inner], own_sem)
+    own.start()
+    sent = []
+
+    def run_ring(stage, count, place, first_source, step_to):
+        plans = [(0, 1, count // 2), (1, -1, (count - 1) // 2)]
+        pending = [None, None]
+        for step in range(1, count // 2 + 1):
+            for direction, sign, steps in plans:
+                if step > steps:
+                    continue
+                origin = -sign * (step - 1)
+                if step > 1:
+                    pending[direction].wait_recv()
+                source = first_source if step == 1 else place(origin)
+                copy = pltpu.make_async_remote_copy(
+                    src_ref=source,
+                    dst_ref=place(origin),
+                    send_sem=send_sems.at[stage, direction, step - 1],
+                    recv_sem=recv_sems.at[stage, direction, step - 1],
+                    device_id=step_to(sign),
+                    device_id_type=MESH_IDS,
+                )
+                copy.start()
+                sent.append(copy)
+                pending[direction] = pltpu.make_async_remote_copy(
+                    src_ref=source,
+                    dst_ref=place(-sign * step),
+                    send_sem=send_sems.at[stage, direction, step - 1],
+                    recv_sem=recv_sems.at[stage, direction, step - 1],
+                    device_id=step_to(sign),
+                    device_id_type=MESH_IDS,
+                )
+        for waiting in pending:
+            if waiting is not None:
+                waiting.wait_recv()
+
+    def inner_place(offset):
+        return out_ref.at[here_outer, lax.rem(here_inner + offset + inner, inner)]
+
+    def outer_place(offset):
+        return out_ref.at[lax.rem(here_outer + offset + outer, outer)]
+
+    run_ring(0, inner, inner_place, block_ref, lambda sign: device(here_outer, here_inner + sign))
+    own.wait()
+    run_ring(1, outer, outer_place, out_ref.at[here_outer], lambda sign: device(here_outer + sign, here_inner))
+    for copy in sent:
+        copy.wait_send()
+
+
+def ring_gather(block, inner, outer):
+    rows, cols = block.shape
+    most_steps = max(inner, outer) // 2
+    return pl.pallas_call(
+        functools.partial(ring_gather_kernel, inner, outer),
+        out_shape=jax.ShapeDtypeStruct((outer, inner, rows, cols), block.dtype),
+        in_specs=[pl.BlockSpec(memory_space=pl.ANY)],
+        out_specs=pl.BlockSpec(memory_space=pl.ANY),
+        scratch_shapes=[
+            pltpu.SemaphoreType.DMA(()),
+            pltpu.SemaphoreType.DMA((2, 2, most_steps)),
+            pltpu.SemaphoreType.DMA((2, 2, most_steps)),
+        ],
+        compiler_params=pltpu.CompilerParams(collective_id=0, has_side_effects=True),
+    )(block).reshape(outer * inner * rows, cols)
 
 
 EPSILON = 1e-05
@@ -140,7 +237,7 @@
     packed = jnp.concatenate(
         [qkv_local, fc1_weight, dense_weight.T, fc2_weight.T, digits], axis=1
     )
-    everything = lax.all_gather(packed, "req", axis=0, tiled=True)
+    everything = ring_gather(packed, INNER, req_count // INNER)
     edges = [0]
     for width in (3 * head_cols, fc1_cols, dense_cols, fc2_cols, digit_cols):
         edges.append(edges[-1] + width)

time: 321 us -> 252 us (0.79)
  waiting for transfers between devices: 234 us -> 46.3 us
  Pallas kernels: 0 us -> 119 us
    all_gather x1 -> x0, waiting for transfers between devices: 161 us -> none  [shards(): everything = lax.all_gather(packed, 'req', axis=0, tiled=True)]
    pallas_call x0 -> x1, Pallas kernels: none -> 119 us  [ring_gather(): pl.pallas_call(functools.partial(ring_gather_kernel, inner, outer), out_s...]
    all_gather x1, waiting for transfers between devices: 30.4 us -> 0.02 us  [shards(): gathered = lax.all_gather(tokens, 'tensor', axis=1, tiled=True)]
  transfers between devices with their start and end apart: 6 -> 5, of which waited for: 5 -> 3; matrix products, arithmetic and copies ran while one was open for 5% -> 7% of each run, Pallas kernels for 0% -> 48%
where the time goes in v2:
time: 252 us; the launch traced here: 251 us
  Pallas kernels  119 us (47%)
  waiting for transfers between devices  46.3 us (18%)
  starting transfers between devices  19.5 us (8%)
  other arithmetic  18.6 us (7%)
  matrix products  17.8 us (7%)
  between operations  14.6 us (6%)
  local copies, waits for them, and re-layouts  11.9 us (5%)
  loops' own time  2.71 us (1%)
    pallas_call x1, Pallas kernels, ring_gather(): pl.pallas_call(functools.partial(ring_gather_kernel, inner, outer), out_s...  119 us
    all_to_all x1, waiting for transfers between devices, shards(): lax.all_to_all(flagged.reshape(req_count, page_cap, page_width + flag_col...  33 us
    all_to_all x1, starting transfers between devices, shards(): lax.all_to_all(flagged.reshape(req_count, page_cap, page_width + flag_col...  14.2 us
    ppermute x2, waiting for transfers between devices, from_behind(): lax.ppermute(value, axis, [(source, source + steps) for source in range(l...  12.5 us
    ppermute x2, starting transfers between devices, from_behind(): lax.ppermute(value, axis, [(source, source + steps) for source in range(l...  5.29 us
    dot_general x1, matrix products, shards(): lax.dot_general(hidden, fc2_full_t, contract_rows, preferred_element_type...  5.16 us
  transfers between devices with their start and end apart: 5, of which 3 were waited for; matrix products, arithmetic and copies ran while one was open for 7% of the time, Pallas kernels for 48%

profile of v2, /device:TPU:6, one launch (start us, length us, event | category | flops | bytes accessed | tf_op | source)
XLA Modules:
  0.0 250.9 jit_solution(16731718445129282967)
XLA Ops:
  12.6 119.4 %shard_map.176 = bf16[16,4,32,2176]{3,2,1,0:T(8,128)(2,1)} custom-call(bf16[32,2176]{1,0:T(8,128)(2,1)} %copy-done.4), custom_call_target="tpu_custom_call" | custom-call | tf_op jit(solution)/shard_map/pallas_call | solution.py:97
  132.1 1.1 slice.97
  135.8 1.8 constant_dynamic-update-slice_fusion.14
  137.7 1.9 constant_dynamic-update-slice_fusion.8
  140.2 1.5 convert_reduce_fusion
  141.8 1.6 fusion.25
  143.4 3.0 %fusion.32 = f32[256,768]{1,0:T(8,128)S(1)} fusion(bf16[2048,2176]{1,0:T(8,128)(2,1)} %bitcast.43, f32[768]{0:T(1024)S(1)} %add.197, bf16[256,2048]{1,0:T(8,128)(2,1)S(1)} %copy-done, f32[2048]{0:T(1024)S(1)} %copy-done.11, f32[2048]{0:T(1024)S(1)} %copy-done.13, f32[256]{0:T(256)S(1)} %add_rsqrt_fusion, f32[256]{0:T(256)S(1)} %broadcast_multiply_fusion), kind=kOutput, calls=%fused_computation.39 | convolution fusion | flops 808648704 | bytes 5002240 | tf_op jit(solution)/shard_map/dot_general | solution.py:254
  147.0 4.0 %collective-permute-start.1 = (bf16[512,2,256]{0,2,1:T(8,128)(2,1)S(1)}, bf16[512,2,256]{0,2,1:T(8,128)(2,1)S(1)}, u32[]{:S(2)}, u32[]{:S(2)}) collective-permute-start(bf16[512,2,256]{0,2,1:T(8,128)(2,1)S(1)} %pad_maximum_fusion.2), channel_id=1, source_target_pairs={{0,16},{8,24},{16,32},{24,40},{32,48},{40,56},{48,64},{56,72},{64,... | collective-permute-start | bytes 1572872 | tf_op jit(solution)/shard_map/ppermute | solution.py:117
  150.9 1.3 collective-permute-start
  152.3 1.8 constant_dynamic-update-slice_fusion.6
  154.2 6.9 %collective-permute-done.1 = bf16[512,2,256]{0,2,1:T(8,128)(2,1)S(1)} collective-permute-done((bf16[512,2,256]{0,2,1:T(8,128)(2,1)S(1)}, bf16[512,2,256]{0,2,1:T(8,128)(2,1)S(1)}, u32[]{:S(2)}, u32[]{:S(2)}) %collective-permute-start.1) | collective-permute-done | bytes 524320 | tf_op jit(solution)/shard_map/ppermute | solution.py:117
  161.0 5.6 %collective-permute-done = bf16[512,2,256]{0,2,1:T(8,128)(2,1)S(1)} collective-permute-done((bf16[512,2,256]{0,2,1:T(8,128)(2,1)S(1)}, bf16[512,2,256]{0,2,1:T(8,128)(2,1)S(1)}, u32[]{:S(2)}, u32[]{:S(2)}) %collective-permute-start) | collective-permute-done | bytes 524320 | tf_op jit(solution)/shard_map/ppermute | solution.py:117
  166.9 15.9 %while.11 = (s32[]{:T(128)}, bf16[4,256,64]{1,2,0:T(8,128)(2,1)S(1)}, s32[4]{0:T(128)S(1)}, bf16[256,256]{0,1:T(8,128)(2,1)S(1)}, bf16[1536,256]{0,1:T(8,128)(2,...) while((s32[]{:T(128)}, ...), condition=%wide.region_25.26_spmd.clone, body=%wide.region_22.25_spmd.clone.sunk | while | flops 112492032 | bytes 5240535 | solution.py:187
  169.0 0.9 fusion.96
  173.0 0.9 fusion.96
  177.0 0.9 fusion.96
  181.0 0.9 fusion.96
  182.8 1.7 fusion.38
  184.6 5.2 %convolution_add_fusion = f32[256,2048]{1,0:T(8,128)} fusion(f32[256,2048]{1,0:T(8,128)S(1)} %fusion.38, bf16[2048,2176]{1,0:T(8,128)(2,1)} %bitcast.45, f32[512]{0:T(512)} %param.31, bf16[256,2048]{1,0:T(8,128)(2,1)S(1)} %copy-done, f32[2048]{0:T(1024)S(1)} %copy-done.12, f32[2048]{0:T(1024)} %param.24, f32[256]{0:T(256)S(1)} %add_rsqrt_fusion, ...), kind=kOutput, calls=%fused_computation.23 | convolution fusion | flops 1078722560 | bytes 9457664 | tf_op jit(solution)/shard_map/dot_general | solution.py:336
  191.8 1.0 reshape.262
  192.8 14.2 %all-to-all-start = ((bf16[64,2,2176]{2,1,0:T(2,128)(2,1)}), bf16[64,2,2176]{2,1,0:T(2,128)(2,1)S(1)}, u32[]{:S(2)}, u32[]{:S(2)}) async-start(bf16[64,2,2176]{2,1,0:T(2,128)(2,1)} %reshape.262), calls=%async_computation.1 | async-start | bytes 1114112 | tf_op jit(solution)/shard_map/all_to_all | solution.py:288
  207.4 33.0 %all-to-all-done = bf16[64,2,2176]{2,1,0:T(2,128)(2,1)S(1)} async-done(((bf16[64,2,2176]{2,1,0:T(2,128)(2,1)}), bf16[64,2,2176]{2,1,0:T(2,128)(2,1)S(1)}, u32[]{:S(2)}, u32[]{:S(2)}) %all-to-all-start) | async-done | bytes 557088 | tf_op jit(solution)/shard_map/all_to_all | solution.py:288
  241.2 1.2 reshape.265
  242.4 1.6 add_convert_fusion
  (113 shorter events, 21.9 us)
Async XLA Ops:
  7.2 133.0 %all-gather.2.cloned.1.call-start = ((), (), s32[]{:S(2)}) async-start(), calls=%async_computation.2 | async-start | bytes 1179648 | tf_op jit(solution)/shard_map/all_gather | solution.py:217
  7.9 234.5 %reduce-scatter.2.cloned.1.call-start = ((), (), s32[]{:S(2)}) async-start(), calls=%async_computation.3 | async-start | bytes 2359296 | tf_op jit(solution)/shard_map/reduce_scatter | solution.py:340
  11.9 0.7 copy-start.4
  12.6 119.4 %copy-start.5 = (f32[3,256]{1,0:T(4,128)S(1)}, f32[3,256]{1,0:T(4,128)}, u32[]{:S(2)}) copy-start(f32[3,256]{1,0:T(4,128)} %param.27) | copy-start | bytes 9220
  132.0 2.2 copy-start.7
  132.1 7.7 %copy-start.3 = (bf16[256,2,256]{2,1,0:T(2,128)(2,1)S(1)}, bf16[256,2,256]{2,1,0:T(2,128)(2,1)}, u32[]{:S(2)}) copy-start(bf16[256,2,256]{2,1,0:T(2,128)(2,1)} %param.34) | copy-start | bytes 786436
  133.2 10.2 %copy-start.11 = (f32[2048]{0:T(1024)S(1)}, f32[2048]{0:T(1024)}, u32[]{:S(2)}) copy-start(f32[2048]{0:T(1024)} %param.25) | copy-start | bytes 24580
  133.2 10.2 %copy-start.13 = (f32[2048]{0:T(1024)S(1)}, f32[2048]{0:T(1024)}, u32[]{:S(2)}) copy-start(f32[2048]{0:T(1024)} %param.24) | copy-start | bytes 24580
  140.2 3.2 %copy-start = (bf16[256,2048]{1,0:T(8,128)(2,1)S(1)}, bf16[256,2048]{1,0:T(8,128)(2,1)}, u32[]{:S(2)}) copy-start(bf16[256,2048]{1,0:T(8,128)(2,1)} %all-gather.2.cloned.1.call-done) | copy-start | bytes 3145732
  147.0 14.1 %collective-permute-start.1 = (bf16[512,2,256]{0,2,1:T(8,128)(2,1)S(1)}, bf16[512,2,256]{0,2,1:T(8,128)(2,1)S(1)}, u32[]{:S(2)}, u32[]{:S(2)}) collective-permute-start(bf16[512,2,256]{0,2,1:T(8,128)(2,1)S(1)} %pad_maximum_fusion.2), channel_id=1, source_target_pairs={{0,16},{8,24},{16,32},{24,40},{32,48},{40,56},{48,64},{56,72},{64,... | collective-permute-start | bytes 1572872 | tf_op jit(solution)/shard_map/ppermute | solution.py:117
  150.9 15.7 %collective-permute-start = (bf16[512,2,256]{0,2,1:T(8,128)(2,1)S(1)}, bf16[512,2,256]{0,2,1:T(8,128)(2,1)S(1)}, u32[]{:S(2)}, u32[]{:S(2)}) collective-permute-start(bf16[512,2,256]{0,2,1:T(8,128)(2,1)S(1)} %pad_maximum_fusion.2), channel_id=1, source_target_pairs={{0,8},{8,16},{16,24},{24,32},{32,40},{40,48},{48,56},{56,64},{64,7... | collective-permute-start | bytes 1572872 | tf_op jit(solution)/shard_map/ppermute | solution.py:117
  182.8 1.7 copy-start.12
  189.7 0.7 copy-start.6
  191.2 15.8 %copy-start.1 = (bf16[512,2,256]{2,1,0:T(2,128)(2,1)S(1)}, bf16[512,2,256]{2,1,0:T(2,128)(2,1)}, u32[]{:S(2)}) copy-start(bf16[512,2,256]{2,1,0:T(2,128)(2,1)} %param.35) | copy-start | bytes 1572868
  191.8 49.0 %copy-start.10 = (s32[1,128]{1,0:T(1,128)S(1)}, s32[1,128]{1,0:T(1,128)}, u32[]{:S(2)}) copy-start(s32[1,128]{1,0:T(1,128)} %param.23) | copy-start | bytes 1540
  192.8 47.7 %all-to-all-start = ((bf16[64,2,2176]{2,1,0:T(2,128)(2,1)}), bf16[64,2,2176]{2,1,0:T(2,128)(2,1)S(1)}, u32[]{:S(2)}, u32[]{:S(2)}) async-start(bf16[64,2,2176]{2,1,0:T(2,128)(2,1)} %reshape.262), calls=%async_computation.1 | async-start | bytes 1114112 | tf_op jit(solution)/shard_map/all_to_all | solution.py:288
  207.4 35.0 %copy-start.2 = (bf16[256,256]{1,0:T(8,128)(2,1)S(1)}, bf16[256,256]{1,0:T(8,128)(2,1)}, u32[]{:S(2)}) copy-start(bf16[256,256]{1,0:T(8,128)(2,1)} %param.19) | copy-start | bytes 393220
  207.4 35.0 %copy-start.8 = (f32[256]{0:T(256)S(1)}, f32[256]{0:T(256)}, u32[]{:S(2)}) copy-start(f32[256]{0:T(256)} %param.33) | copy-start | bytes 3076
  207.4 35.0 %copy-start.9 = (f32[256]{0:T(256)S(1)}, f32[256]{0:T(256)}, u32[]{:S(2)}) copy-start(f32[256]{0:T(256)} %param.29) | copy-start | bytes 3076
Sparse Core Ops, SparseCore 0:
  10.1 34.7 all-gather.1
  189.9 38.3 reduce-scatter.1

commit v3 on v2

--- a/solution.py
+++ b/solution.py
@@ -106,6 +106,88 @@
         ],
         compiler_params=pltpu.CompilerParams(collective_id=0, has_side_effects=True),
     )(block).reshape(outer * inner * rows, cols)
+
+
+def exchange_kernel(count, outgoing_ref, keys_ref, incoming_ref, behind_ref, own_sem, send_sems,
+                    recv_sems, shift_send, shift_recv):
+    here = lax.axis_index("req")
+    tensor_index = lax.axis_index("tensor")
+
+    def device(offset):
+        return (lax.rem(here + offset + count, count), tensor_index)
+
+    barrier = pltpu.get_barrier_semaphore()
+
+    def greet(offset, carry):
+        pl.semaphore_signal(barrier, inc=1, device_id=device(offset), device_id_type=MESH_IDS)
+        return carry
+
+    lax.fori_loop(1, count, greet, 0)
+    pl.semaphore_wait(barrier, count - 1)
+
+    own = pltpu.make_async_copy(outgoing_ref.at[here], incoming_ref.at[here], own_sem)
+    own.start()
+
+    def shift_copy(step):
+        return pltpu.make_async_remote_copy(
+            src_ref=keys_ref,
+            dst_ref=behind_ref.at[step],
+            send_sem=shift_send.at[step],
+            recv_sem=shift_recv.at[step],
+            device_id=device(step + 1),
+            device_id_type=MESH_IDS,
+        )
+
+    for step in range(2):
+        shift_copy(step).start()
+
+    def page_copy(offset, source_at, target_at):
+        return pltpu.make_async_remote_copy(
+            src_ref=outgoing_ref.at[source_at],
+            dst_ref=incoming_ref.at[target_at],
+            send_sem=send_sems.at[offset],
+            recv_sem=recv_sems.at[offset],
+            device_id=device(offset),
+            device_id_type=MESH_IDS,
+        )
+
+    def push(offset, carry):
+        page_copy(offset, lax.rem(here + offset, count), here).start()
+        return carry
+
+    lax.fori_loop(1, count, push, 0)
+
+    def settle(offset, carry):
+        page_copy(offset, lax.rem(here + offset, count), here).wait_send()
+        page_copy(offset, here, lax.rem(here - offset + count, count)).wait_recv()
+        return carry
+
+    lax.fori_loop(1, count, settle, 0)
+    for step in range(2):
+        shift_copy(step).wait_send()
+        shift_copy(step).wait_recv()
+    own.wait()
+
+
+def exchange(outgoing, keys):
+    count = outgoing.shape[0]
+    return pl.pallas_call(
+        functools.partial(exchange_kernel, count),
+        out_shape=(
+            jax.ShapeDtypeStruct(outgoing.shape, outgoing.dtype),
+            jax.ShapeDtypeStruct((2,) + keys.shape, keys.dtype),
+        ),
+        in_specs=[pl.BlockSpec(memory_space=pl.ANY)] * 2,
+        out_specs=(pl.BlockSpec(memory_space=pl.ANY), pl.BlockSpec(memory_space=pl.ANY)),
+        scratch_shapes=[
+            pltpu.SemaphoreType.DMA(()),
+            pltpu.SemaphoreType.DMA((count,)),
+            pltpu.SemaphoreType.DMA((count,)),
+            pltpu.SemaphoreType.DMA((2,)),
+            pltpu.SemaphoreType.DMA((2,)),
+        ],
+        compiler_params=pltpu.CompilerParams(collective_id=1, has_side_effects=True),
+    )(outgoing, keys)
 
 
 EPSILON = 1e-05
@@ -285,13 +367,11 @@
         [outgoing, jnp.broadcast_to(filled[:, None], (pool_count, flag_cols)).astype(jnp.bfloat16)],
         axis=1,
     )
-    arrived = lax.all_to_all(
-        flagged.reshape(req_count, page_cap, page_width + flag_cols),
-        "req",
-        split_axis=0,
-        concat_axis=0,
-        tiled=True,
-    ).reshape(pool_count, page_width + flag_cols)
+    local_keys = jnp.concatenate([key_value, prefix_cache], axis=0)
+    arrived, behind = exchange(
+        flagged.reshape(req_count, page_cap, page_width + flag_cols), local_keys
+    )
+    arrived = arrived.reshape(pool_count, page_width + flag_cols)
     incoming = arrived[:, :page_width]
     incoming_filled = arrived[:, page_width]
     slot_ids = slot_perm[0]
@@ -306,10 +386,7 @@
     written_mask = jnp.any(placing, axis=1)
     pool_pages = cache_pool.reshape(pool_count, page_width)
     new_pool = jnp.where(written_mask[:, None], written, pool_pages).reshape(cache_pool.shape)
-    local_keys = jnp.concatenate([key_value, prefix_cache], axis=0)
-    blocks = [local_keys]
-    for shift_by in range(1, SPAN + 1):
-        blocks.append(from_behind(local_keys, "req", shift_by))
+    blocks = [local_keys] + [behind[step] for step in range(SPAN)]
     key_segs = []
     key_poss = []
     for step_back in range(SPAN + 1):

time: 252 us -> 318 us (1.26); the launches traced: 251 us -> 314 us
  Pallas kernels: 119 us -> 182 us
  other arithmetic: 18.6 us -> 43.4 us
  starting transfers between devices: 19.5 us -> 0.08 us
  waiting for transfers between devices: 46.3 us -> 34.2 us
  local copies, waits for them, and re-layouts: 11.9 us -> 16.7 us
    pallas_call x0 -> x1, Pallas kernels: none -> 63.1 us  [exchange(): pl.pallas_call(functools.partial(exchange_kernel, count), out_shape=(jax....]
    reduce_scatter x1, waiting for transfers between devices: 0.01 us -> 33.5 us  [shards(): lax.psum_scatter(branches, 'tensor', scatter_dimension=1, tiled=True)]
    all_to_all x1 -> x0, waiting for transfers between devices: 33 us -> none  [shards(): lax.all_to_all(flagged.reshape(req_count, page_cap, page_width + flag_col...]
    concatenate x1, other arithmetic: 0.1 us -> 22.2 us  [shards(): all_keys = jnp.concatenate(blocks, axis=0)]
    all_to_all x1 -> x0, starting transfers between devices: 14.2 us -> none  [shards(): lax.all_to_all(flagged.reshape(req_count, page_cap, page_width + flag_col...]
    ppermute x2 -> x0, waiting for transfers between devices: 12.5 us -> none  [from_behind(): lax.ppermute(value, axis, [(source, source + steps) for source in range(l...]
    ppermute x2 -> x0, starting transfers between devices: 5.29 us -> none  [from_behind(): lax.ppermute(value, axis, [(source, source + steps) for source in range(l...]
  transfers between devices with their start and end apart: 5 -> 2, of which waited for: 3 -> 1; matrix products, arithmetic and copies ran while one was open for 7% -> 5% of each run, Pallas kernels for 48% -> 38%
where the time goes in v3:
time: 318 us; the launch traced here: 314 us
  Pallas kernels  182 us (57%)
  other arithmetic  43.4 us (14%)
  waiting for transfers between devices  34.2 us (11%)
  matrix products  19.2 us (6%)
  local copies, waits for them, and re-layouts  16.7 us (5%)
  between operations  14.6 us (5%)
    pallas_call x1, Pallas kernels, ring_gather(): pl.pallas_call(functools.partial(ring_gather_kernel, inner, outer), out_s...  119 us
    pallas_call x1, Pallas kernels, exchange(): pl.pallas_call(functools.partial(exchange_kernel, count), out_shape=(jax....  63.1 us
    reduce_scatter x1, waiting for transfers between devices, shards(): lax.psum_scatter(branches, 'tensor', scatter_dimension=1, tiled=True)  33.5 us
    concatenate x1, other arithmetic, shards(): all_keys = jnp.concatenate(blocks, axis=0)  22.2 us
  transfers between devices with their start and end apart: 2, of which 1 were waited for; matrix products, arithmetic and copies ran while one was open for 5% of the time, Pallas kernels for 38%

profile of v3, /device:TPU:6, one launch (start us, length us, event | category | flops | bytes accessed | tf_op | source)
XLA Modules:
  0.0 313.5 jit_solution(10584047134357920363)
XLA Ops:
  13.3 119.3 %shard_map.176 = bf16[16,4,32,2176]{3,2,1,0:T(8,128)(2,1)} custom-call(bf16[32,2176]{1,0:T(8,128)(2,1)} %copy-done.5), custom_call_target="tpu_custom_call" | custom-call | tf_op jit(solution)/shard_map/pallas_call | solution.py:97
  132.7 1.1 slice.105
  136.4 1.9 constant_dynamic-update-slice_fusion.14
  138.3 1.9 constant_dynamic-update-slice_fusion.8
  140.6 1.8 constant_dynamic-update-slice_fusion.6
  142.8 1.5 convert_reduce_fusion
  144.4 1.6 fusion.25
  146.1 3.0 fusion.32
  152.3 1.6 pad_maximum_fusion.2.keys_ref
  153.9 63.1 %shard_map.177 = (bf16[64,2,2176]{2,1,0:T(2,128)(2,1)}, bf16[2,512,2,256]{3,2,1,0:T(2,128)(2,1)}) custom-call(bf16[64,2,2176]{2,1,0:T(2,128)(2,1)} %reshape.261.outgoing_ref, bf16[512,2,256]{2,1,0:T(2,128)(2,1)} %pad_maximum_fusion.2.keys_ref), custom_call_target="tpu_custom_call" | custom-call | tf_op jit(solution)/shard_map/pallas_call | solution.py:174
  217.0 1.9 slice_bitcast_fusion.1
  218.9 22.2 %pad_maximum_fusion = bf16[1536,2,256]{2,1,0:T(2,128)(2,1)S(1)} fusion(bf16[512,2,256]{2,1,0:T(2,128)(2,1)S(1)} %get-tuple-element.156, bf16[512,2,256]{2,1,0:T(2,128)(2,1)S(1)} %get-tuple-element.155, bf16[256,2,256]{2,1,0:T(2,128)(2,1)S(1)} %copy-done.1, bf16[256,1,256]{2,1,0:T(2,128)(2,1)S(1)} %copy.33, bf16[256,1,256]{2,1,0:T(2,128)(2,1)S(1)} %copy.32), kind=kLoop, calls=%fused_computation.38 | loop fusion | flops 7864320 | bytes 3145728 | tf_op jit(solution)/shard_map/concatenate | solution.py:406
  241.1 2.2 fusion.86
  243.7 17.6 %while.11 = (s32[]{:T(128)}, bf16[4,256,64]{1,2,0:T(8,128)(2,1)S(1)}, s32[4]{0:T(128)S(1)}, bf16[256,256]{0,1:T(8,128)(2,1)S(1)}, bf16[1536,256]{1,0:T(8,128)(2,...) while((s32[]{:T(128)}, ...), condition=%wide.region_28.29_spmd.clone, body=%wide.region_25.28_spmd.clone.sunk | while | flops 112492032 | bytes 5633751 | solution.py:269
  245.0 1.1 fusion.96
  247.0 1.0 fusion.98
  249.3 1.1 fusion.96
  253.6 1.1 fusion.96
  258.0 1.1 fusion.96
  261.3 1.7 fusion.38
  263.0 5.1 %convolution_add_fusion = f32[256,2048]{1,0:T(8,128)} fusion(f32[256,2048]{1,0:T(8,128)S(1)} %fusion.38, bf16[2048,2176]{1,0:T(8,128)(2,1)} %bitcast.52, f32[512]{0:T(512)S(1)} %copy-done.14, bf16[256,2048]{1,0:T(8,128)(2,1)S(1)} %copy-done, f32[2048]{0:T(1024)S(1)} %copy-done.12, f32[2048]{0:T(1024)S(1)} %copy-done.13, f32[256]{0:T(256)S(1)} %add_rsqrt_fusion, ...), kind=kOutput, calls=%fused_computation.23 | convolution fusion | flops 1078722560 | bytes 9457664 | tf_op jit(solution)/shard_map/dot_general | solution.py:413
  270.4 1.2 reshape.265
  271.6 33.5 %reduce-scatter.2.cloned.1.call-done = f32[256,256]{1,0:T(8,128)} async-done(((f32[256,2048]{1,0:T(8,128)}), f32[256,256]{1,0:T(8,128)}) %reduce-scatter.2.cloned.1.call-update) | async-done | bytes 262160 | tf_op jit(solution)/shard_map/reduce_scatter | solution.py:417
  305.0 1.6 add_convert_fusion
  (114 shorter events, 24.1 us)
Async XLA Ops:
  7.2 135.7 %all-gather.2.cloned.1.call-start = ((), (), s32[]{:S(2)}) async-start(), calls=%async_computation.1 | async-start | bytes 1179648 | tf_op jit(solution)/shard_map/all_gather | solution.py:299
  7.9 297.1 %reduce-scatter.2.cloned.1.call-start = ((), (), s32[]{:S(2)}) async-start(), calls=%async_computation.2 | async-start | bytes 2359296 | tf_op jit(solution)/shard_map/reduce_scatter | solution.py:417
  12.7 0.7 copy-start.5
  132.6 2.2 copy-start.8
  132.6 7.8 %copy-start.6 = (f32[3,256]{1,0:T(4,128)S(1)}, f32[3,256]{1,0:T(4,128)}, u32[]{:S(2)}) copy-start(f32[3,256]{1,0:T(4,128)} %param.27) | copy-start | bytes 9220
  132.7 9.7 %copy-start.7 = (s32[64,1]{0,1:T(1,128)S(1)}, s32[64,1]{0,1:T(1,128)}, u32[]{:S(2)}) copy-start(s32[64,1]{0,1:T(1,128)} %param.22) | copy-start | bytes 772
  132.7 13.4 %copy-start.12 = (f32[2048]{0:T(1024)S(1)}, f32[2048]{0:T(1024)}, u32[]{:S(2)}) copy-start(f32[2048]{0:T(1024)} %param.25) | copy-start | bytes 24580
  132.7 13.4 %copy-start.13 = (f32[2048]{0:T(1024)S(1)}, f32[2048]{0:T(1024)}, u32[]{:S(2)}) copy-start(f32[2048]{0:T(1024)} %param.24) | copy-start | bytes 24580
  142.8 3.2 %copy-start = (bf16[256,2048]{1,0:T(8,128)(2,1)S(1)}, bf16[256,2048]{1,0:T(8,128)(2,1)}, u32[]{:S(2)}) copy-start(bf16[256,2048]{1,0:T(8,128)(2,1)} %all-gather.2.cloned.1.call-done) | copy-start | bytes 3145732
  149.9 2.4 copy-start.1
  261.3 1.7 copy-start.14
  268.2 1.0 copy-start.3
  268.2 1.5 copy-start.2
  268.2 1.8 copy-start.11
  269.6 35.5 %copy-start.4 = (bf16[256,256]{1,0:T(8,128)(2,1)S(1)}, bf16[256,256]{1,0:T(8,128)(2,1)}, u32[]{:S(2)}) copy-start(bf16[256,256]{1,0:T(8,128)(2,1)} %param.19) | copy-start | bytes 393220
  269.6 35.4 %copy-start.9 = (f32[256]{0:T(256)S(1)}, f32[256]{0:T(256)}, u32[]{:S(2)}) copy-start(f32[256]{0:T(256)} %param.33) | copy-start | bytes 3076
  269.6 35.4 %copy-start.10 = (f32[256]{0:T(256)S(1)}, f32[256]{0:T(256)}, u32[]{:S(2)}) copy-start(f32[256]{0:T(256)} %param.29) | copy-start | bytes 3076
Sparse Core Ops, SparseCore 0:
  10.1 34.7 all-gather.1
  268.3 36.6 reduce-scatter.1

commit v4 on v2

--- a/solution.py
+++ b/solution.py
@@ -14,6 +14,7 @@
 PAGE = 4
 WINDOW = 512
 INNER = 4
+RING_COST = 40
 
 
 MESH_IDS = pl.DeviceIdType.MESH
@@ -91,9 +92,10 @@
         copy.wait_send()
 
 
-def ring_gather(block, inner, outer):
+def ring_gather(block, inner, outer, kernel_id):
     rows, cols = block.shape
     most_steps = max(inner, outer) // 2
+    gathered_bytes = outer * inner * rows * cols * block.dtype.itemsize
     return pl.pallas_call(
         functools.partial(ring_gather_kernel, inner, outer),
         out_shape=jax.ShapeDtypeStruct((outer, inner, rows, cols), block.dtype),
@@ -104,7 +106,10 @@
             pltpu.SemaphoreType.DMA((2, 2, most_steps)),
             pltpu.SemaphoreType.DMA((2, 2, most_steps)),
         ],
-        compiler_params=pltpu.CompilerParams(collective_id=0, has_side_effects=True),
+        compiler_params=pltpu.CompilerParams(collective_id=kernel_id, has_side_effects=True),
+        cost_estimate=pl.CostEstimate(
+            flops=0, transcendentals=0, bytes_accessed=RING_COST * gathered_bytes
+        ),
     )(block).reshape(outer * inner * rows, cols)
 
 
@@ -234,16 +239,10 @@
     fc1_cols = fc1_weight.shape[1]
     dense_cols = dense_weight.shape[0]
     fc2_cols = fc2_weight.shape[0]
-    packed = jnp.concatenate(
-        [qkv_local, fc1_weight, dense_weight.T, fc2_weight.T, digits], axis=1
-    )
-    everything = ring_gather(packed, INNER, req_count // INNER)
-    edges = [0]
-    for width in (3 * head_cols, fc1_cols, dense_cols, fc2_cols, digit_cols):
-        edges.append(edges[-1] + width)
-    qkv_full, fc1_full, dense_full_t, fc2_full_t, digits_full = [
-        everything[:, edges[i] : edges[i + 1]] for i in range(5)
-    ]
+    first_pack = jnp.concatenate([qkv_local, digits], axis=1)
+    qkv_full, digits_full = jnp.split(
+        ring_gather(first_pack, INNER, req_count // INNER, 0), [3 * head_cols], axis=1
+    )
     digit_table = digits_full.reshape(req_count, weight_rows * digit_cols)[:, : 2 * label_count]
     digit_table = digit_table.astype(jnp.int32)
     starts = jnp.min(
@@ -254,7 +253,6 @@
         return jnp.dot(normed, portion, preferred_element_type=jnp.float32)
 
     projected = add_rows(qkv_full)
-    lifted = add_rows(fc1_full)
     projected = (projected + qkv_bias.reshape(1, 3 * head_cols)).reshape(
         tok_rows, 3, head_cols // HEAD_DIM, HEAD_DIM
     )
@@ -285,6 +283,13 @@
         [outgoing, jnp.broadcast_to(filled[:, None], (pool_count, flag_cols)).astype(jnp.bfloat16)],
         axis=1,
     )
+    second_pack = jnp.concatenate([fc1_weight, dense_weight.T, fc2_weight.T], axis=1)
+    second_pack, flagged = lax.optimization_barrier((second_pack, flagged))
+    fc1_full, dense_full_t, fc2_full_t = jnp.split(
+        ring_gather(second_pack, INNER, req_count // INNER, 1),
+        [fc1_cols, fc1_cols + dense_cols],
+        axis=1,
+    )
     arrived = lax.all_to_all(
         flagged.reshape(req_count, page_cap, page_width + flag_cols),
         "req",
@@ -292,6 +297,8 @@
         concat_axis=0,
         tiled=True,
     ).reshape(pool_count, page_width + flag_cols)
+    fc1_full, arrived = lax.optimization_barrier((fc1_full, arrived))
+    lifted = add_rows(fc1_full)
     incoming = arrived[:, :page_width]
     incoming_filled = arrived[:, page_width]
     slot_ids = slot_perm[0]

time: 252 us -> 300 us (1.19)
  Pallas kernels: 119 us -> 162 us
  waiting for transfers between devices: 46.3 us -> 39.9 us
  other arithmetic: 18.6 us -> 23.9 us
  matrix products: 17.8 us -> 22.8 us
  starting transfers between devices: 19.5 us -> 16.5 us
    pallas_call x1 -> x2, Pallas kernels: 119 us -> 162 us  [ring_gather(): pl.pallas_call(functools.partial(ring_gather_kernel, inner, outer), out_s...]
    reduce_scatter x1, waiting for transfers between devices: 0.01 us -> 39.2 us  [shards(): lax.psum_scatter(branches, 'tensor', scatter_dimension=1, tiled=True)]
    all_to_all x1, waiting for transfers between devices: 33 us -> 0.01 us  [shards(): lax.all_to_all(flagged.reshape(req_count, page_cap, page_width + flag_col...]
    ppermute x2, waiting for transfers between devices: 12.5 us -> 0.01 us  [from_behind(): lax.ppermute(value, axis, [(source, source + steps) for source in range(l...]
    split x0 -> x2, local copies, waits for them, and re-layouts: none -> 4.23 us  [the longest x1 3.1 us: shards(): jnp.split(ring_gather(second_pack, INNER, req_count // INNER, 1), [fc1_co...]
    all_to_all x1, starting transfers between devices: 14.2 us -> 10.3 us  [shards(): lax.all_to_all(flagged.reshape(req_count, page_cap, page_width + flag_col...]
    dot_general x4, matrix products: 3.57 us -> 6.59 us  [one_head(): lax.dot_general(query_cols, key_cols, (((1,), (1,)), ((), ())), preferred...]
  transfers between devices with their start and end apart: 5 -> 5, of which waited for: 3 -> 1; matrix products, arithmetic and copies ran while one was open for 7% -> 15% of each run, Pallas kernels for 48% -> 55%
where the time goes in v4:
time: 300 us; the launch traced here: 296 us
  Pallas kernels  162 us (54%)
  waiting for transfers between devices  39.9 us (13%)
  other arithmetic  23.9 us (8%)
  matrix products  22.8 us (8%)
  starting transfers between devices  16.5 us (6%)
  between operations  14.8 us (5%)
  local copies, waits for them, and re-layouts  14 us (5%)
    pallas_call x2, Pallas kernels, ring_gather(): pl.pallas_call(functools.partial(ring_gather_kernel, inner, outer), out_s...  162 us
    reduce_scatter x1, waiting for transfers between devices, shards(): lax.psum_scatter(branches, 'tensor', scatter_dimension=1, tiled=True)  39.2 us
    all_to_all x1, starting transfers between devices, shards(): lax.all_to_all(flagged.reshape(req_count, page_cap, page_width + flag_col...  10.3 us
    dot_general x4, matrix products, one_head(): lax.dot_general(query_cols, key_cols, (((1,), (1,)), ((), ())), preferred...  6.59 us
  transfers between devices with their start and end apart: 5, of which 1 were waited for; matrix products, arithmetic and copies ran while one was open for 15% of the time, Pallas kernels for 55%

profile of v4, /device:TPU:6, one launch (start us, length us, event | category | flops | bytes accessed | tf_op | source)
XLA Modules:
  0.0 296.0 jit_solution(17384512709706158831)
XLA Ops:
  11.0 72.9 %shard_map.176 = bf16[16,4,32,896]{3,2,1,0:T(8,128)(2,1)} custom-call(bf16[32,896]{1,0:T(8,128)(2,1)} %pad_maximum_fusion.7.block_ref), custom_call_target="tpu_custom_call" | custom-call | bytes 146800640 | tf_op jit(solution)/shard_map/pallas_call | solution.py:99
  84.0 1.1 split.21
  87.8 1.9 constant_dynamic-update-slice_fusion.8
  89.7 1.9 constant_dynamic-update-slice_fusion.4
  92.2 1.8 constant_dynamic-update-slice_fusion
  96.2 1.5 convert_reduce_fusion
  97.8 1.6 fusion.25
  100.1 3.0 %fusion.30 = f32[256,768]{1,0:T(8,128)S(1)} fusion(bf16[2048,896]{1,0:T(8,128)(2,1)} %bitcast.44, f32[768]{0:T(1024)S(1)} %add.197, bf16[256,2048]{1,0:T(8,128)(2,1)S(1)} %copy-done, f32[2048]{0:T(1024)S(1)} %copy-done.28, f32[2048]{0:T(1024)S(1)} %copy-done.30, f32[256]{0:T(256)S(1)} %add_rsqrt_fusion, f32[256]{0:T(256)S(1)} %broadcast_multiply_fusion), kind=kOutput, calls=%fused_computation.37 | convolution fusion | flops 808648704 | bytes 5002240 | tf_op jit(solution)/shard_map/dot_general | solution.py:253
  104.2 3.8 %collective-permute-start.1 = (bf16[512,2,256]{0,2,1:T(8,128)(2,1)S(1)}, bf16[512,2,256]{0,2,1:T(8,128)(2,1)S(1)}, u32[]{:S(2)}, u32[]{:S(2)}) collective-permute-start(bf16[512,2,256]{0,2,1:T(8,128)(2,1)S(1)} %pad_maximum_fusion.2), channel_id=1, source_target_pairs={{0,16},{8,24},{16,32},{24,40},{32,48},{40,56},{48,64},{56,72},{64,... | collective-permute-start | bytes 1572872 | tf_op jit(solution)/shard_map/ppermute | solution.py:122
  108.0 2.1 collective-permute-start
  112.1 10.3 %all-to-all-start = ((bf16[64,2,2176]{2,1,0:T(2,128)(2,1)}), bf16[64,2,2176]{2,1,0:T(2,128)(2,1)S(1)}, u32[]{:S(2)}, u32[]{:S(2)}) async-start(bf16[64,2,2176]{2,1,0:T(2,128)(2,1)} %reshape.266), calls=%async_computation | async-start | bytes 1114112 | tf_op jit(solution)/shard_map/all_to_all | solution.py:293
  122.6 88.6 %shard_map.177 = bf16[16,4,32,1280]{3,2,1,0:T(8,128)(2,1)} custom-call(bf16[32,1280]{1,0:T(8,128)(2,1)} %pad_maximum_fusion.6.block_ref), custom_call_target="tpu_custom_call" | custom-call | bytes 209715200 | tf_op jit(solution)/shard_map/pallas_call | solution.py:99
  211.2 3.1 %split.23 = bf16[2048,512]{1,0:T(8,128)(2,1)} slice(bf16[2048,1280]{1,0:T(8,128)(2,1)} %bitcast.40), slice={[0:2048], [0:512]} | slice | bytes 4194304 | tf_op jit(solution)/shard_map/split | solution.py:288
  215.0 1.1 pad_maximum_fusion
  217.1 18.9 %while.11 = (s32[]{:T(128)}, bf16[4,256,64]{1,2,0:T(8,128)(2,1)S(1)}, s32[4]{0:T(128)S(1)}, bf16[256,256]{0,1:T(8,128)(2,1)}, bf16[1536,256]{0,1:T(8,128)(2,1)S(...) while((s32[]{:T(128)}, ...), condition=%wide.region_25.26_spmd.clone, body=%wide.region_22.25_spmd.clone.sunk | while | flops 112492032 | bytes 5240535 | solution.py:192
  218.3 1.6 fusion.85
  223.1 1.6 fusion.85
  227.8 1.6 fusion.85
  232.5 1.7 fusion.85
  236.1 3.1 %fusion.33 = f32[256,2048]{1,0:T(8,128)} fusion(bf16[256,256]{0,1:T(8,128)(2,1)S(1)} %bitcast.54, bf16[2048,1280]{1,0:T(8,128)(2,1)} %bitcast.41), kind=kOutput, calls=%fused_computation.39 | convolution fusion | flops 268435456 | bytes 3276800 | tf_op jit(solution)/shard_map/dot_general | solution.py:340
  239.4 5.8 %convolution_add_fusion = f32[256,2048]{1,0:T(8,128)} fusion(f32[256,2048]{1,0:T(8,128)} %fusion.33, bf16[2048,1280]{1,0:T(8,128)(2,1)} %bitcast.42, bf16[2048,512]{1,0:T(8,128)(2,1)} %split.23, f32[512]{0:T(512)S(1)} %copy-done.32, bf16[256,2048]{1,0:T(8,128)(2,1)S(1)} %copy-done, f32[2048]{0:T(1024)S(1)} %copy-done.29, f32[2048]{0:T(1024)S(1)} %copy-done.31, ...), kind=kOutput, calls=%fused_computation.23 | convolution fusion | flops 1078722560 | bytes 9457664 | tf_op jit(solution)/shard_map/dot_general | solution.py:343
  247.2 1.2 reshape.269
  248.3 39.2 %reduce-scatter.2.cloned.1.call-done = f32[256,256]{1,0:T(8,128)} async-done(((f32[256,2048]{1,0:T(8,128)}), f32[256,256]{1,0:T(8,128)}) %reduce-scatter.2.cloned.1.call-update) | async-done | bytes 262160 | tf_op jit(solution)/shard_map/reduce_scatter | solution.py:347
  287.5 1.6 add_convert_fusion
  (151 shorter events, 26.2 us)
Async XLA Ops:
  7.2 89.1 %all-gather.2.cloned.1.call-start = ((), (), s32[]{:S(2)}) async-start(), calls=%async_computation.2 | async-start | bytes 1179648 | tf_op jit(solution)/shard_map/all_gather | solution.py:222
  11.0 75.2 %copy-start.19 = (s32[43]{0:T(128)S(1)}, s32[43]{0:T(128)}, u32[]{:S(2)}) copy-start(s32[43]{0:T(128)} %param.21) | copy-start | bytes 520
  11.0 80.8 %copy-start.15 = (f32[3,256]{1,0:T(4,128)S(1)}, f32[3,256]{1,0:T(4,128)}, u32[]{:S(2)}) copy-start(f32[3,256]{1,0:T(4,128)} %param.27) | copy-start | bytes 9220
  84.0 8.0 %copy-start.3 = (bf16[256,2,256]{2,1,0:T(2,128)(2,1)S(1)}, bf16[256,2,256]{2,1,0:T(2,128)(2,1)}, u32[]{:S(2)}) copy-start(bf16[256,2,256]{2,1,0:T(2,128)(2,1)} %param.34) | copy-start | bytes 786436
  84.0 10.1 %copy-start.18 = (s32[64,1]{0,1:T(1,128)S(1)}, s32[64,1]{0,1:T(1,128)}, u32[]{:S(2)}) copy-start(s32[64,1]{0,1:T(1,128)} %param.22) | copy-start | bytes 772
  84.0 11.6 %copy-start.12 = (bf16[512,32]{0,1:T(8,128)(2,1)S(1)}, bf16[512,32]{0,1:T(8,128)(2,1)}, u32[]{:S(2)}) copy-start(bf16[512,32]{0,1:T(8,128)(2,1)} %param.32) | copy-start | bytes 98308
  84.0 11.6 %copy-start.13 = (bf16[32,512]{1,0:T(8,128)(2,1)S(1)}, bf16[32,512]{1,0:T(8,128)(2,1)}, u32[]{:S(2)}) copy-start(bf16[32,512]{1,0:T(8,128)(2,1)} %param.30) | copy-start | bytes 98308
  84.0 11.6 %copy-start.14 = (bf16[256,32]{0,1:T(8,128)(2,1)S(1)}, bf16[256,32]{0,1:T(8,128)(2,1)}, u32[]{:S(2)}) copy-start(bf16[256,32]{0,1:T(8,128)(2,1)} %param.28) | copy-start | bytes 49156
  85.1 14.9 %copy-start.28 = (f32[2048]{0:T(1024)S(1)}, f32[2048]{0:T(1024)}, u32[]{:S(2)}) copy-start(f32[2048]{0:T(1024)} %param.25) | copy-start | bytes 24580
  85.2 14.9 %copy-start.30 = (f32[2048]{0:T(1024)S(1)}, f32[2048]{0:T(1024)}, u32[]{:S(2)}) copy-start(f32[2048]{0:T(1024)} %param.24) | copy-start | bytes 24580
  87.7 4.1 %copy-start.8 = (s32[256]{0:T(256)}, s32[256]{0:T(256)S(1)}, u32[]{:S(2)}) copy-start(s32[256]{0:T(256)S(1)} %get-tuple-element.263) | copy-start | bytes 3076
  91.8 4.5 %copy-start.10 = (s32[256]{0:T(256)}, s32[256]{0:T(256)S(1)}, u32[]{:S(2)}) copy-start(s32[256]{0:T(256)S(1)} %get-tuple-element.266) | copy-start | bytes 3076
  94.2 8.8 %copy-start.26 = (s32[64]{0:T(128)}, s32[64]{0:T(128)S(1)}, u32[]{:S(2)}) copy-start(s32[64]{0:T(128)S(1)} %multiply_add_fusion) | copy-start | bytes 772
  96.2 3.8 %copy-start = (bf16[256,2048]{1,0:T(8,128)(2,1)S(1)}, bf16[256,2048]{1,0:T(8,128)(2,1)}, u32[]{:S(2)}) copy-start(bf16[256,2048]{1,0:T(8,128)(2,1)} %all-gather.2.cloned.1.call-done) | copy-start | bytes 3145732
  103.4 7.1 %copy-start.27 = (s32[64]{0:T(128)S(1)}, s32[64]{0:T(128)}, u32[]{:S(2)}) copy-start(s32[64]{0:T(128)} %copy-done.26) | copy-start | bytes 772
  103.5 7.5 %copy-start.25 = (bf16[128]{0:T(256)(128)(2,1)S(1)}, bf16[128]{0:T(256)(128)(2,1)}, u32[]{:S(2)}) copy-start(bf16[128]{0:T(256)(128)(2,1)} %fusion.57) | copy-start | bytes 772
  104.2 110.8 %collective-permute-start.1 = (bf16[512,2,256]{0,2,1:T(8,128)(2,1)S(1)}, bf16[512,2,256]{0,2,1:T(8,128)(2,1)S(1)}, u32[]{:S(2)}, u32[]{:S(2)}) collective-permute-start(bf16[512,2,256]{0,2,1:T(8,128)(2,1)S(1)} %pad_maximum_fusion.2), channel_id=1, source_target_pairs={{0,16},{8,24},{16,32},{24,40},{32,48},{40,56},{48,64},{56,72},{64,... | collective-permute-start | bytes 1572872 | tf_op jit(solution)/shard_map/ppermute | solution.py:122
  108.0 107.0 %collective-permute-start = (bf16[512,2,256]{0,2,1:T(8,128)(2,1)S(1)}, bf16[512,2,256]{0,2,1:T(8,128)(2,1)}, u32[]{:S(2)}, u32[]{:S(2)}) collective-permute-start(bf16[512,2,256]{0,2,1:T(8,128)(2,1)S(1)} %pad_maximum_fusion.2), channel_id=1, source_target_pairs={{0,8},{8,16},{16,24},{24,32},{32,40},{40,48},{48,56},{56,64},{64,7... | collective-permute-start | bytes 1572872 | tf_op jit(solution)/shard_map/ppermute | solution.py:122
  112.1 127.1 %all-to-all-start = ((bf16[64,2,2176]{2,1,0:T(2,128)(2,1)}), bf16[64,2,2176]{2,1,0:T(2,128)(2,1)S(1)}, u32[]{:S(2)}, u32[]{:S(2)}) async-start(bf16[64,2,2176]{2,1,0:T(2,128)(2,1)} %reshape.266), calls=%async_computation | async-start | bytes 1114112 | tf_op jit(solution)/shard_map/all_to_all | solution.py:293
  122.4 165.1 %reduce-scatter.2.cloned.1.call-start = ((), (), s32[]{:S(2)}) async-start(), calls=%async_computation.3 | async-start | bytes 2359296 | tf_op jit(solution)/shard_map/reduce_scatter | solution.py:347
  236.0 3.4 %copy-start.17 = (f32[256]{0:T(256)S(1)}, f32[256]{0:T(256)}, u32[]{:S(2)}) copy-start(f32[256]{0:T(256)} %copy-done.16) | copy-start | bytes 3076
  246.2 41.3 %copy-start.2 = (bf16[256,256]{1,0:T(8,128)(2,1)S(1)}, bf16[256,256]{1,0:T(8,128)(2,1)}, u32[]{:S(2)}) copy-start(bf16[256,256]{1,0:T(8,128)(2,1)} %param.19) | copy-start | bytes 393220
  246.2 41.3 %copy-start.20 = (f32[256]{0:T(256)S(1)}, f32[256]{0:T(256)}, u32[]{:S(2)}) copy-start(f32[256]{0:T(256)} %param.33) | copy-start | bytes 3076
  246.2 41.3 %copy-start.21 = (f32[256]{0:T(256)S(1)}, f32[256]{0:T(256)}, u32[]{:S(2)}) copy-start(f32[256]{0:T(256)} %param.29) | copy-start | bytes 3076
  (14 other events, 28.2 us)
Sparse Core Ops, SparseCore 0:
  10.1 34.7 all-gather.1
  245.3 42.1 reduce-scatter.1

commit v5 on v2

--- a/solution.py
+++ b/solution.py
@@ -292,20 +292,6 @@
         concat_axis=0,
         tiled=True,
     ).reshape(pool_count, page_width + flag_cols)
-    incoming = arrived[:, :page_width]
-    incoming_filled = arrived[:, page_width]
-    slot_ids = slot_perm[0]
-    placing = (slot_ids[None, :] == jnp.arange(pool_count, dtype=jnp.int32)[:, None]) & (
-        incoming_filled[None, :] > 0
-    )
-    written = jnp.dot(
-        placing.astype(jnp.bfloat16),
-        incoming,
-        preferred_element_type=jnp.float32,
-    ).astype(jnp.bfloat16)
-    written_mask = jnp.any(placing, axis=1)
-    pool_pages = cache_pool.reshape(pool_count, page_width)
-    new_pool = jnp.where(written_mask[:, None], written, pool_pages).reshape(cache_pool.shape)
     local_keys = jnp.concatenate([key_value, prefix_cache], axis=0)
     blocks = [local_keys]
     for shift_by in range(1, SPAN + 1):
@@ -328,6 +314,21 @@
     )
     all_keys = jnp.concatenate(blocks, axis=0)
     attended = head_attention(queries, all_keys[:, 0, :], all_keys[:, 1, :], allowed)
+    attended, arrived = lax.optimization_barrier((attended, arrived))
+    incoming = arrived[:, :page_width]
+    incoming_filled = arrived[:, page_width]
+    slot_ids = slot_perm[0]
+    placing = (slot_ids[None, :] == jnp.arange(pool_count, dtype=jnp.int32)[:, None]) & (
+        incoming_filled[None, :] > 0
+    )
+    written = jnp.dot(
+        placing.astype(jnp.bfloat16),
+        incoming,
+        preferred_element_type=jnp.float32,
+    ).astype(jnp.bfloat16)
+    written_mask = jnp.any(placing, axis=1)
+    pool_pages = cache_pool.reshape(pool_count, page_width)
+    new_pool = jnp.where(written_mask[:, None], written, pool_pages).reshape(cache_pool.shape)
     hidden = jax.nn.gelu(lifted + fc1_bias, approximate=True).astype(jnp.bfloat16)
     contract_rows = (((1,), (1,)), ((), ()))
     attn_part = lax.dot_general(

time: 252 us -> 272 us (1.079); the launches traced: 251 us -> 268 us
  waiting for transfers between devices: 46.3 us -> 54.8 us
  matrix products: 17.8 us -> 22.8 us
  other arithmetic: 18.6 us -> 22.7 us
  starting transfers between devices: 19.5 us -> 16.4 us
    reduce_scatter x1, waiting for transfers between devices: 0.01 us -> 46.6 us  [shards(): lax.psum_scatter(branches, 'tensor', scatter_dimension=1, tiled=True)]
    all_to_all x1, waiting for transfers between devices: 33 us -> 6.09 us  [shards(): lax.all_to_all(flagged.reshape(req_count, page_cap, page_width + flag_col...]
    ppermute x2, waiting for transfers between devices: 12.5 us -> 1.35 us  [from_behind(): lax.ppermute(value, axis, [(source, source + steps) for source in range(l...]
    all_to_all x1, starting transfers between devices: 14.2 us -> 10.1 us  [shards(): lax.all_to_all(flagged.reshape(req_count, page_cap, page_width + flag_col...]
    dot_general x4, matrix products: 3.57 us -> 6.59 us  [one_head(): lax.dot_general(query_cols, key_cols, (((1,), (1,)), ((), ())), preferred...]
    unnamed x35 -> x65, local copies, waits for them, and re-layouts: 3.79 us -> 5.94 us
  transfers between devices with their start and end apart: 5 -> 5, of which waited for: 3 -> 3; matrix products, arithmetic and copies ran while one was open for 7% -> 14% of each run, Pallas kernels for 48% -> 45%
where the time goes in v5:
time: 272 us; the launch traced here: 268 us
  Pallas kernels  119 us (44%)
  waiting for transfers between devices  54.8 us (20%)
  matrix products  22.8 us (8%)
  other arithmetic  22.7 us (8%)
  starting transfers between devices  16.4 us (6%)
  between operations  14.7 us (5%)
  local copies, waits for them, and re-layouts  14.2 us (5%)
    pallas_call x1, Pallas kernels, ring_gather(): pl.pallas_call(functools.partial(ring_gather_kernel, inner, outer), out_s...  119 us
    reduce_scatter x1, waiting for transfers between devices, shards(): lax.psum_scatter(branches, 'tensor', scatter_dimension=1, tiled=True)  46.6 us
    all_to_all x1, starting transfers between devices, shards(): lax.all_to_all(flagged.reshape(req_count, page_cap, page_width + flag_col...  10.1 us
    dot_general x4, matrix products, one_head(): lax.dot_general(query_cols, key_cols, (((1,), (1,)), ((), ())), preferred...  6.59 us
    all_to_all x1, waiting for transfers between devices, shards(): lax.all_to_all(flagged.reshape(req_count, page_cap, page_width + flag_col...  6.09 us
    ppermute x2, starting transfers between devices, from_behind(): lax.ppermute(value, axis, [(source, source + steps) for source in range(l...  6.07 us
    unnamed x65, local copies, waits for them, and re-layouts  5.94 us
    dot_general x1, matrix products, shards(): lax.dot_general(hidden, fc2_full_t, contract_rows, preferred_element_type...  5.77 us
  transfers between devices with their start and end apart: 5, of which 3 were waited for; matrix products, arithmetic and copies ran while one was open for 14% of the time, Pallas kernels for 45%

profile of v5, /device:TPU:6, one launch (start us, length us, event | category | flops | bytes accessed | tf_op | source)
XLA Modules:
  0.0 267.6 jit_solution(5913903938945580701)
XLA Ops:
  12.6 119.3 %shard_map.176 = bf16[16,4,32,2176]{3,2,1,0:T(8,128)(2,1)} custom-call(bf16[32,2176]{1,0:T(8,128)(2,1)} %copy-done.4), custom_call_target="tpu_custom_call" | custom-call | tf_op jit(solution)/shard_map/pallas_call | solution.py:97
  135.7 1.9 constant_dynamic-update-slice_fusion.14
  137.6 1.9 constant_dynamic-update-slice_fusion.8
  140.5 1.8 constant_dynamic-update-slice_fusion.6
  143.9 1.5 convert_reduce_fusion
  145.4 1.6 fusion.25
  147.7 3.0 %fusion.32 = f32[256,768]{1,0:T(8,128)S(1)} fusion(bf16[2048,2176]{1,0:T(8,128)(2,1)} %bitcast.43, f32[768]{0:T(1024)S(1)} %add.197, bf16[256,2048]{1,0:T(8,128)(2,1)S(1)} %copy-done, f32[2048]{0:T(1024)S(1)} %copy-done.24, f32[2048]{0:T(1024)S(1)} %copy-done.26, f32[256]{0:T(256)S(1)} %add_rsqrt_fusion, f32[256]{0:T(256)S(1)} %broadcast_multiply_fusion), kind=kOutput, calls=%fused_computation.39 | convolution fusion | flops 808648704 | bytes 5002240 | tf_op jit(solution)/shard_map/dot_general | solution.py:254
  151.8 4.0 %collective-permute-start.1 = (bf16[512,2,256]{0,2,1:T(8,128)(2,1)S(1)}, bf16[512,2,256]{0,2,1:T(8,128)(2,1)S(1)}, u32[]{:S(2)}, u32[]{:S(2)}) collective-permute-start(bf16[512,2,256]{0,2,1:T(8,128)(2,1)S(1)} %pad_maximum_fusion.2), channel_id=1, source_target_pairs={{0,16},{8,24},{16,32},{24,40},{32,48},{40,56},{48,64},{56,72},{64,... | collective-permute-start | bytes 1572872 | tf_op jit(solution)/shard_map/ppermute | solution.py:117
  155.7 2.1 collective-permute-start
  159.9 10.1 %all-to-all-start = ((bf16[64,2,2176]{2,1,0:T(2,128)(2,1)}), bf16[64,2,2176]{2,1,0:T(2,128)(2,1)S(1)}, u32[]{:S(2)}, u32[]{:S(2)}) async-start(bf16[64,2,2176]{2,1,0:T(2,128)(2,1)} %reshape.262), calls=%async_computation | async-start | bytes 1114112 | tf_op jit(solution)/shard_map/all_to_all | solution.py:288
  170.2 1.4 pad_maximum_fusion.4
  171.7 1.3 collective-permute-done
  173.0 1.1 pad_maximum_fusion
  175.1 18.9 %while.11 = (s32[]{:T(128)}, bf16[4,256,64]{1,2,0:T(8,128)(2,1)S(1)}, s32[4]{0:T(128)S(1)}, bf16[256,256]{0,1:T(8,128)(2,1)}, bf16[1536,256]{0,1:T(8,128)(2,1)S(...) while((s32[]{:T(128)}, ...), condition=%wide.region_25.26_spmd.clone, body=%wide.region_22.25_spmd.clone.sunk | while | flops 112492032 | bytes 5240535 | solution.py:187
  176.4 1.6 fusion.95
  181.1 1.7 fusion.95
  185.8 1.6 fusion.95
  190.5 1.7 fusion.95
  194.1 6.1 %all-to-all-done = bf16[64,2,2176]{2,1,0:T(2,128)(2,1)S(1)} async-done(((bf16[64,2,2176]{2,1,0:T(2,128)(2,1)}), bf16[64,2,2176]{2,1,0:T(2,128)(2,1)S(1)}, u32[]{:S(2)}, u32[]{:S(2)}) %all-to-all-start) | async-done | bytes 557088 | tf_op jit(solution)/shard_map/all_to_all | solution.py:288
  200.4 3.1 %fusion.38 = f32[256,2048]{1,0:T(8,128)} fusion(bf16[256,256]{0,1:T(8,128)(2,1)S(1)} %bitcast.55, bf16[2048,2176]{1,0:T(8,128)(2,1)} %bitcast.44), kind=kOutput, calls=%fused_computation.41 | convolution fusion | flops 268435456 | bytes 3276800 | tf_op jit(solution)/shard_map/dot_general | solution.py:334
  203.5 5.8 %convolution_add_fusion = f32[256,2048]{1,0:T(8,128)} fusion(f32[256,2048]{1,0:T(8,128)} %fusion.38, bf16[2048,2176]{1,0:T(8,128)(2,1)} %bitcast.45, f32[512]{0:T(512)S(1)} %copy-done.28, bf16[256,2048]{1,0:T(8,128)(2,1)S(1)} %copy-done, f32[2048]{0:T(1024)S(1)} %copy-done.25, f32[2048]{0:T(1024)S(1)} %copy-done.27, f32[256]{0:T(256)S(1)} %copy-done.19, ...), kind=kOutput, calls=%fused_computation.23 | convolution fusion | flops 1078722560 | bytes 9457664 | tf_op jit(solution)/shard_map/dot_general | solution.py:337
  211.3 1.2 reshape.265
  212.4 46.6 %reduce-scatter.2.cloned.1.call-done = f32[256,256]{1,0:T(8,128)} async-done(((f32[256,2048]{1,0:T(8,128)}), f32[256,256]{1,0:T(8,128)}) %reduce-scatter.2.cloned.1.call-update) | async-done | bytes 262160 | tf_op jit(solution)/shard_map/reduce_scatter | solution.py:341
  259.1 1.6 add_convert_fusion
  (143 shorter events, 28.0 us)
Async XLA Ops:
  7.2 136.7 %all-gather.2.cloned.1.call-start = ((), (), s32[]{:S(2)}) async-start(), calls=%async_computation.2 | async-start | bytes 1179648 | tf_op jit(solution)/shard_map/all_gather | solution.py:217
  131.8 2.2 copy-start.14
  131.8 2.3 copy-start.15
  131.9 7.9 %copy-start.11 = (f32[3,256]{1,0:T(4,128)S(1)}, f32[3,256]{1,0:T(4,128)}, u32[]{:S(2)}) copy-start(f32[3,256]{1,0:T(4,128)} %param.27) | copy-start | bytes 9220
  131.9 8.3 %copy-start.3 = (bf16[256,2,256]{2,1,0:T(2,128)(2,1)S(1)}, bf16[256,2,256]{2,1,0:T(2,128)(2,1)}, u32[]{:S(2)}) copy-start(bf16[256,2,256]{2,1,0:T(2,128)(2,1)} %param.34) | copy-start | bytes 786436
  133.0 14.6 %copy-start.24 = (f32[2048]{0:T(1024)S(1)}, f32[2048]{0:T(1024)}, u32[]{:S(2)}) copy-start(f32[2048]{0:T(1024)} %param.25) | copy-start | bytes 24580
  133.0 14.6 %copy-start.26 = (f32[2048]{0:T(1024)S(1)}, f32[2048]{0:T(1024)}, u32[]{:S(2)}) copy-start(f32[2048]{0:T(1024)} %param.24) | copy-start | bytes 24580
  135.7 4.1 %copy-start.7 = (s32[256]{0:T(256)}, s32[256]{0:T(256)S(1)}, u32[]{:S(2)}) copy-start(s32[256]{0:T(256)S(1)} %get-tuple-element.259) | copy-start | bytes 3076
  142.5 2.9 %copy-start.22 = (s32[64]{0:T(128)}, s32[64]{0:T(128)S(1)}, u32[]{:S(2)}) copy-start(s32[64]{0:T(128)S(1)} %multiply_add_fusion) | copy-start | bytes 772
  143.9 3.8 %copy-start = (bf16[256,2048]{1,0:T(8,128)(2,1)S(1)}, bf16[256,2048]{1,0:T(8,128)(2,1)}, u32[]{:S(2)}) copy-start(bf16[256,2048]{1,0:T(8,128)(2,1)} %all-gather.2.cloned.1.call-done) | copy-start | bytes 3145732
  151.0 7.2 %copy-start.23 = (s32[64]{0:T(128)S(1)}, s32[64]{0:T(128)}, u32[]{:S(2)}) copy-start(s32[64]{0:T(128)} %copy-done.22) | copy-start | bytes 772
  151.0 7.6 %copy-start.21 = (bf16[128]{0:T(256)(128)(2,1)S(1)}, bf16[128]{0:T(256)(128)(2,1)}, u32[]{:S(2)}) copy-start(bf16[128]{0:T(256)(128)(2,1)} %fusion.68) | copy-start | bytes 772
  151.8 19.9 %collective-permute-start.1 = (bf16[512,2,256]{0,2,1:T(8,128)(2,1)S(1)}, bf16[512,2,256]{0,2,1:T(8,128)(2,1)S(1)}, u32[]{:S(2)}, u32[]{:S(2)}) collective-permute-start(bf16[512,2,256]{0,2,1:T(8,128)(2,1)S(1)} %pad_maximum_fusion.2), channel_id=1, source_target_pairs={{0,16},{8,24},{16,32},{24,40},{32,48},{40,56},{48,64},{56,72},{64,... | collective-permute-start | bytes 1572872 | tf_op jit(solution)/shard_map/ppermute | solution.py:117
  155.7 17.3 %collective-permute-start = (bf16[512,2,256]{0,2,1:T(8,128)(2,1)S(1)}, bf16[512,2,256]{0,2,1:T(8,128)(2,1)}, u32[]{:S(2)}, u32[]{:S(2)}) collective-permute-start(bf16[512,2,256]{0,2,1:T(8,128)(2,1)S(1)} %pad_maximum_fusion.2), channel_id=1, source_target_pairs={{0,8},{8,16},{16,24},{24,32},{32,40},{40,48},{48,56},{56,64},{64,7... | collective-permute-start | bytes 1572872 | tf_op jit(solution)/shard_map/ppermute | solution.py:117
  159.9 40.3 %all-to-all-start = ((bf16[64,2,2176]{2,1,0:T(2,128)(2,1)}), bf16[64,2,2176]{2,1,0:T(2,128)(2,1)S(1)}, u32[]{:S(2)}, u32[]{:S(2)}) async-start(bf16[64,2,2176]{2,1,0:T(2,128)(2,1)} %reshape.262), calls=%async_computation | async-start | bytes 1114112 | tf_op jit(solution)/shard_map/all_to_all | solution.py:288
  170.0 89.1 %reduce-scatter.2.cloned.1.call-start = ((), (), s32[]{:S(2)}) async-start(), calls=%async_computation.3 | async-start | bytes 2359296 | tf_op jit(solution)/shard_map/reduce_scatter | solution.py:341
  194.0 9.5 %copy-start.13 = (f32[256]{0:T(256)S(1)}, f32[256]{0:T(256)}, u32[]{:S(2)}) copy-start(f32[256]{0:T(256)} %copy-done.12) | copy-start | bytes 3076
  194.0 9.4 %copy-start.19 = (f32[256]{0:T(256)S(1)}, f32[256]{0:T(256)}, u32[]{:S(2)}) copy-start(f32[256]{0:T(256)} %copy-done.18) | copy-start | bytes 3076
  194.0 9.4 %copy-start.25 = (f32[2048]{0:T(1024)S(1)}, f32[2048]{0:T(1024)}, u32[]{:S(2)}) copy-start(f32[2048]{0:T(1024)} %param.25) | copy-start | bytes 24580
  194.1 9.4 %copy-start.27 = (f32[2048]{0:T(1024)S(1)}, f32[2048]{0:T(1024)}, u32[]{:S(2)}) copy-start(f32[2048]{0:T(1024)} %param.24) | copy-start | bytes 24580
  194.1 9.4 %copy-start.28 = (f32[512]{0:T(512)S(1)}, f32[512]{0:T(512)}, u32[]{:S(2)}) copy-start(f32[512]{0:T(512)} %param.31) | copy-start | bytes 6148
  210.3 48.7 %copy-start.2 = (bf16[256,256]{1,0:T(8,128)(2,1)S(1)}, bf16[256,256]{1,0:T(8,128)(2,1)}, u32[]{:S(2)}) copy-start(bf16[256,256]{1,0:T(8,128)(2,1)} %param.19) | copy-start | bytes 393220
  210.3 48.8 %copy-start.16 = (f32[256]{0:T(256)S(1)}, f32[256]{0:T(256)}, u32[]{:S(2)}) copy-start(f32[256]{0:T(256)} %param.33) | copy-start | bytes 3076
  210.3 48.8 %copy-start.17 = (f32[256]{0:T(256)S(1)}, f32[256]{0:T(256)}, u32[]{:S(2)}) copy-start(f32[256]{0:T(256)} %param.29) | copy-start | bytes 3076
  (10 other events, 9.5 us)
Sparse Core Ops, SparseCore 0:
  10.1 34.7 all-gather.1
  209.4 49.5 reduce-scatter.1

commit v6 on v5

--- a/solution.py
+++ b/solution.py
@@ -338,7 +338,9 @@
         hidden, fc2_full_t, contract_rows, preferred_element_type=jnp.float32
     )
     branches = attn_part + mlp_part
-    summed = lax.psum_scatter(branches, "tensor", scatter_dimension=1, tiled=True)
+    summed = lax.psum_scatter(
+        branches.astype(jnp.bfloat16), "tensor", scatter_dimension=1, tiled=True
+    ).astype(jnp.float32)
     layer_out = (tokens.astype(jnp.float32) + summed + dense_bias + fc2_bias).astype(jnp.bfloat16)
     return (layer_out, new_pool)
 

time: 272 us -> 270 us (level)
  no operation moved by 1% of the time
where the time goes in v6:
time: 270 us; the launch traced here: 266 us
  Pallas kernels  119 us (44%)
  waiting for transfers between devices  54.2 us (20%)
  other arithmetic  22.7 us (8%)
  matrix products  22.4 us (8%)
  starting transfers between devices  16.4 us (6%)
  between operations  14.7 us (5%)
  local copies, waits for them, and re-layouts  13.3 us (5%)
  loops' own time  2.7 us (1%)
    pallas_call x1, Pallas kernels, ring_gather(): pl.pallas_call(functools.partial(ring_gather_kernel, inner, outer), out_s...  119 us
    reduce_scatter x1, waiting for transfers between devices, shards(): lax.psum_scatter(branches.astype(jnp.bfloat16), 'tensor', scatter_dimensi...  46 us
    all_to_all x1, starting transfers between devices, shards(): lax.all_to_all(flagged.reshape(req_count, page_cap, page_width + flag_col...  10.1 us
    dot_general x4, matrix products, one_head(): lax.dot_general(query_cols, key_cols, (((1,), (1,)), ((), ())), preferred...  6.59 us
    all_to_all x1, waiting for transfers between devices, shards(): lax.all_to_all(flagged.reshape(req_count, page_cap, page_width + flag_col...  6.09 us
    ppermute x2, starting transfers between devices, from_behind(): lax.ppermute(value, axis, [(source, source + steps) for source in range(l...  6.07 us
    dot_general x1, matrix products, shards(): lax.dot_general(hidden, fc2_full_t, contract_rows, preferred_element_type...  5.41 us
  transfers between devices with their start and end apart: 5, of which 3 were waited for; matrix products, arithmetic and copies ran while one was open for 14% of the time, Pallas kernels for 45%

profile of v6, /device:TPU:6, one launch (start us, length us, event | category | flops | bytes accessed | tf_op | source)
XLA Modules:
  0.0 265.7 jit_solution(881487822561822255)
XLA Ops:
  12.6 119.3 %shard_map.176 = bf16[16,4,32,2176]{3,2,1,0:T(8,128)(2,1)} custom-call(bf16[32,2176]{1,0:T(8,128)(2,1)} %copy-done.4), custom_call_target="tpu_custom_call" | custom-call | tf_op jit(solution)/shard_map/pallas_call | solution.py:97
  135.7 1.9 constant_dynamic-update-slice_fusion.14
  137.6 1.9 constant_dynamic-update-slice_fusion.8
  140.5 1.8 constant_dynamic-update-slice_fusion.6
  143.9 1.5 convert_reduce_fusion
  145.4 1.6 fusion.26
  147.7 3.0 %fusion.33 = f32[256,768]{1,0:T(8,128)S(1)} fusion(bf16[2048,2176]{1,0:T(8,128)(2,1)} %bitcast.43, f32[768]{0:T(1024)S(1)} %add.197, bf16[256,2048]{1,0:T(8,128)(2,1)S(1)} %copy-done, f32[2048]{0:T(1024)S(1)} %copy-done.24, f32[2048]{0:T(1024)S(1)} %copy-done.26, f32[256]{0:T(256)S(1)} %add_rsqrt_fusion, f32[256]{0:T(256)S(1)} %broadcast_multiply_fusion), kind=kOutput, calls=%fused_computation.40 | convolution fusion | flops 808648704 | bytes 5002240 | tf_op jit(solution)/shard_map/dot_general | solution.py:254
  151.8 4.0 %collective-permute-start.1 = (bf16[512,2,256]{0,2,1:T(8,128)(2,1)S(1)}, bf16[512,2,256]{0,2,1:T(8,128)(2,1)S(1)}, u32[]{:S(2)}, u32[]{:S(2)}) collective-permute-start(bf16[512,2,256]{0,2,1:T(8,128)(2,1)S(1)} %pad_maximum_fusion.2), channel_id=1, source_target_pairs={{0,16},{8,24},{16,32},{24,40},{32,48},{40,56},{48,64},{56,72},{64,... | collective-permute-start | bytes 1572872 | tf_op jit(solution)/shard_map/ppermute | solution.py:117
  155.7 2.1 collective-permute-start
  159.9 10.1 %all-to-all-start = ((bf16[64,2,2176]{2,1,0:T(2,128)(2,1)}), bf16[64,2,2176]{2,1,0:T(2,128)(2,1)S(1)}, u32[]{:S(2)}, u32[]{:S(2)}) async-start(bf16[64,2,2176]{2,1,0:T(2,128)(2,1)} %reshape.262), calls=%async_computation | async-start | bytes 1114112 | tf_op jit(solution)/shard_map/all_to_all | solution.py:288
  170.2 1.4 pad_maximum_fusion.4
  171.7 1.3 collective-permute-done
  173.0 1.1 pad_maximum_fusion
  175.1 18.9 %while.11 = (s32[]{:T(128)}, bf16[4,256,64]{1,2,0:T(8,128)(2,1)S(1)}, s32[4]{0:T(128)S(1)}, bf16[256,256]{0,1:T(8,128)(2,1)}, bf16[1536,256]{0,1:T(8,128)(2,1)S(...) while((s32[]{:T(128)}, ...), condition=%wide.region_25.26_spmd.clone, body=%wide.region_22.25_spmd.clone.sunk | while | flops 112492032 | bytes 5240535 | solution.py:187
  176.4 1.6 fusion.96
  181.1 1.7 fusion.96
  185.8 1.6 fusion.96
  190.5 1.7 fusion.96
  194.1 6.1 %all-to-all-done = bf16[64,2,2176]{2,1,0:T(2,128)(2,1)S(1)} async-done(((bf16[64,2,2176]{2,1,0:T(2,128)(2,1)}), bf16[64,2,2176]{2,1,0:T(2,128)(2,1)S(1)}, u32[]{:S(2)}, u32[]{:S(2)}) %all-to-all-start) | async-done | bytes 557088 | tf_op jit(solution)/shard_map/all_to_all | solution.py:288
  200.4 3.1 %fusion.39 = f32[256,2048]{1,0:T(8,128)} fusion(bf16[256,256]{0,1:T(8,128)(2,1)S(1)} %bitcast.55, bf16[2048,2176]{1,0:T(8,128)(2,1)} %bitcast.44), kind=kOutput, calls=%fused_computation.42 | convolution fusion | flops 268435456 | bytes 3276800 | tf_op jit(solution)/shard_map/dot_general | solution.py:334
  203.5 5.4 %fusion.22 = bf16[256,2048]{1,0:T(8,128)(2,1)} fusion(f32[256,2048]{1,0:T(8,128)} %fusion.39, bf16[2048,2176]{1,0:T(8,128)(2,1)} %bitcast.45, f32[512]{0:T(512)S(1)} %copy-done.28, bf16[256,2048]{1,0:T(8,128)(2,1)S(1)} %copy-done, f32[2048]{0:T(1024)S(1)} %copy-done.25, f32[2048]{0:T(1024)S(1)} %copy-done.27, f32[256]{0:T(256)S(1)} %copy-done.19, ...), kind=kOutput, calls=%fused_computation.26 | convolution fusion | flops 1079246848 | bytes 8409088 | tf_op jit(solution)/shard_map/dot_general | solution.py:337
  210.0 1.2 reshape.265
  211.2 46.0 %reduce-scatter.2.cloned.1.call-done = bf16[256,256]{1,0:T(8,128)(2,1)} async-done(((bf16[256,2048]{1,0:T(8,128)(2,1)}), bf16[256,256]{1,0:T(8,128)(2,1)}) %reduce-scatter.2.cloned.1.call-update) | async-done | bytes 131088 | tf_op jit(solution)/shard_map/reduce_scatter | solution.py:341
  257.2 1.6 add_convert_fusion
  (143 shorter events, 27.1 us)
Async XLA Ops:
  7.2 136.7 %all-gather.2.cloned.1.call-start = ((), (), s32[]{:S(2)}) async-start(), calls=%async_computation.2 | async-start | bytes 1179648 | tf_op jit(solution)/shard_map/all_gather | solution.py:217
  131.8 2.3 copy-start.15
  131.9 7.9 %copy-start.11 = (f32[3,256]{1,0:T(4,128)S(1)}, f32[3,256]{1,0:T(4,128)}, u32[]{:S(2)}) copy-start(f32[3,256]{1,0:T(4,128)} %param.27) | copy-start | bytes 9220
  131.9 8.3 %copy-start.3 = (bf16[256,2,256]{2,1,0:T(2,128)(2,1)S(1)}, bf16[256,2,256]{2,1,0:T(2,128)(2,1)}, u32[]{:S(2)}) copy-start(bf16[256,2,256]{2,1,0:T(2,128)(2,1)} %param.34) | copy-start | bytes 786436
  133.0 14.6 %copy-start.24 = (f32[2048]{0:T(1024)S(1)}, f32[2048]{0:T(1024)}, u32[]{:S(2)}) copy-start(f32[2048]{0:T(1024)} %param.25) | copy-start | bytes 24580
  133.0 14.6 %copy-start.26 = (f32[2048]{0:T(1024)S(1)}, f32[2048]{0:T(1024)}, u32[]{:S(2)}) copy-start(f32[2048]{0:T(1024)} %param.24) | copy-start | bytes 24580
  135.7 4.1 %copy-start.7 = (s32[256]{0:T(256)}, s32[256]{0:T(256)S(1)}, u32[]{:S(2)}) copy-start(s32[256]{0:T(256)S(1)} %get-tuple-element.259) | copy-start | bytes 3076
  142.5 2.9 %copy-start.22 = (s32[64]{0:T(128)}, s32[64]{0:T(128)S(1)}, u32[]{:S(2)}) copy-start(s32[64]{0:T(128)S(1)} %multiply_add_fusion) | copy-start | bytes 772
  143.9 3.8 %copy-start = (bf16[256,2048]{1,0:T(8,128)(2,1)S(1)}, bf16[256,2048]{1,0:T(8,128)(2,1)}, u32[]{:S(2)}) copy-start(bf16[256,2048]{1,0:T(8,128)(2,1)} %all-gather.2.cloned.1.call-done) | copy-start | bytes 3145732
  151.0 7.2 %copy-start.23 = (s32[64]{0:T(128)S(1)}, s32[64]{0:T(128)}, u32[]{:S(2)}) copy-start(s32[64]{0:T(128)} %copy-done.22) | copy-start | bytes 772
  151.0 7.6 %copy-start.21 = (bf16[128]{0:T(256)(128)(2,1)S(1)}, bf16[128]{0:T(256)(128)(2,1)}, u32[]{:S(2)}) copy-start(bf16[128]{0:T(256)(128)(2,1)} %fusion.69) | copy-start | bytes 772
  151.8 19.9 %collective-permute-start.1 = (bf16[512,2,256]{0,2,1:T(8,128)(2,1)S(1)}, bf16[512,2,256]{0,2,1:T(8,128)(2,1)S(1)}, u32[]{:S(2)}, u32[]{:S(2)}) collective-permute-start(bf16[512,2,256]{0,2,1:T(8,128)(2,1)S(1)} %pad_maximum_fusion.2), channel_id=1, source_target_pairs={{0,16},{8,24},{16,32},{24,40},{32,48},{40,56},{48,64},{56,72},{64,... | collective-permute-start | bytes 1572872 | tf_op jit(solution)/shard_map/ppermute | solution.py:117
  155.7 17.3 %collective-permute-start = (bf16[512,2,256]{0,2,1:T(8,128)(2,1)S(1)}, bf16[512,2,256]{0,2,1:T(8,128)(2,1)}, u32[]{:S(2)}, u32[]{:S(2)}) collective-permute-start(bf16[512,2,256]{0,2,1:T(8,128)(2,1)S(1)} %pad_maximum_fusion.2), channel_id=1, source_target_pairs={{0,8},{8,16},{16,24},{24,32},{32,40},{40,48},{48,56},{56,64},{64,7... | collective-permute-start | bytes 1572872 | tf_op jit(solution)/shard_map/ppermute | solution.py:117
  159.9 40.3 %all-to-all-start = ((bf16[64,2,2176]{2,1,0:T(2,128)(2,1)}), bf16[64,2,2176]{2,1,0:T(2,128)(2,1)S(1)}, u32[]{:S(2)}, u32[]{:S(2)}) async-start(bf16[64,2,2176]{2,1,0:T(2,128)(2,1)} %reshape.262), calls=%async_computation | async-start | bytes 1114112 | tf_op jit(solution)/shard_map/all_to_all | solution.py:288
  170.0 87.2 %reduce-scatter.2.cloned.1.call-start = ((), (), s32[]{:S(2)}) async-start(), calls=%async_computation.3 | async-start | bytes 1179648 | tf_op jit(solution)/shard_map/reduce_scatter | solution.py:341
  194.0 9.5 %copy-start.13 = (f32[256]{0:T(256)S(1)}, f32[256]{0:T(256)}, u32[]{:S(2)}) copy-start(f32[256]{0:T(256)} %copy-done.12) | copy-start | bytes 3076
  194.0 9.4 %copy-start.19 = (f32[256]{0:T(256)S(1)}, f32[256]{0:T(256)}, u32[]{:S(2)}) copy-start(f32[256]{0:T(256)} %copy-done.18) | copy-start | bytes 3076
  194.0 9.4 %copy-start.25 = (f32[2048]{0:T(1024)S(1)}, f32[2048]{0:T(1024)}, u32[]{:S(2)}) copy-start(f32[2048]{0:T(1024)} %param.25) | copy-start | bytes 24580
  194.1 9.4 %copy-start.27 = (f32[2048]{0:T(1024)S(1)}, f32[2048]{0:T(1024)}, u32[]{:S(2)}) copy-start(f32[2048]{0:T(1024)} %param.24) | copy-start | bytes 24580
  194.1 9.4 %copy-start.28 = (f32[512]{0:T(512)S(1)}, f32[512]{0:T(512)}, u32[]{:S(2)}) copy-start(f32[512]{0:T(512)} %param.31) | copy-start | bytes 6148
  203.5 5.5 %copy-start.2 = (bf16[512,2,256]{2,1,0:T(2,128)(2,1)S(1)}, bf16[512,2,256]{2,1,0:T(2,128)(2,1)}, u32[]{:S(2)}) copy-start(bf16[512,2,256]{2,1,0:T(2,128)(2,1)} %param.35) | copy-start | bytes 1572868
  209.0 48.3 %copy-start.1 = (bf16[256,256]{1,0:T(8,128)(2,1)S(1)}, bf16[256,256]{1,0:T(8,128)(2,1)}, u32[]{:S(2)}) copy-start(bf16[256,256]{1,0:T(8,128)(2,1)} %param.19) | copy-start | bytes 393220
  209.0 48.2 %copy-start.16 = (f32[256]{0:T(256)S(1)}, f32[256]{0:T(256)}, u32[]{:S(2)}) copy-start(f32[256]{0:T(256)} %param.33) | copy-start | bytes 3076
  209.0 48.2 %copy-start.17 = (f32[256]{0:T(256)S(1)}, f32[256]{0:T(256)}, u32[]{:S(2)}) copy-start(f32[256]{0:T(256)} %param.29) | copy-start | bytes 3076
  (10 other events, 9.8 us)
Sparse Core Ops, SparseCore 0:
  10.1 34.7 all-gather.1
  209.1 48.0 reduce-scatter.1

commit v7 on v2

--- a/solution.py
+++ b/solution.py
@@ -19,7 +19,8 @@
 MESH_IDS = pl.DeviceIdType.MESH
 
 
-def ring_gather_kernel(inner, outer, block_ref, out_ref, own_sem, send_sems, recv_sems):
+def ring_gather_kernel(inner, outer, block_ref, out_ref, own_sem, inner_send_sems, inner_recv_sems,
+                       outer_send_sems, outer_recv_sems):
     req_index = lax.axis_index("req")
     tensor_index = lax.axis_index("tensor")
     here_outer = req_index // inner
@@ -29,6 +30,12 @@
         outer_at = lax.rem(outer_at + outer, outer)
         inner_at = lax.rem(inner_at + inner, inner)
         return (outer_at * inner + inner_at, tensor_index)
+
+    def inner_at(offset):
+        return lax.rem(here_inner + offset + inner, inner)
+
+    def outer_at(offset):
+        return lax.rem(here_outer + offset + outer, outer)
 
     neighbours = (
         device(here_outer, here_inner + 1),
@@ -45,55 +52,84 @@
     own.start()
     sent = []
 
-    def run_ring(stage, count, place, first_source, step_to):
-        plans = [(0, 1, count // 2), (1, -1, (count - 1) // 2)]
-        pending = [None, None]
-        for step in range(1, count // 2 + 1):
-            for direction, sign, steps in plans:
+    def remote(source, target, send_sem, recv_sem, toward):
+        return pltpu.make_async_remote_copy(
+            src_ref=source,
+            dst_ref=target,
+            send_sem=send_sem,
+            recv_sem=recv_sem,
+            device_id=toward,
+            device_id_type=MESH_IDS,
+        )
+
+    inner_plans = [(0, 1, inner // 2), (1, -1, (inner - 1) // 2)]
+    outer_plans = [(0, 1, outer // 2), (1, -1, (outer - 1) // 2)]
+
+    def inner_copy(direction, sign, step, arriving):
+        piece = -sign * step if arriving else -sign * (step - 1)
+        source = block_ref if step == 1 else out_ref.at[here_outer, inner_at(piece)]
+        return remote(
+            source,
+            out_ref.at[here_outer, inner_at(piece)],
+            inner_send_sems.at[direction, step - 1],
+            inner_recv_sems.at[direction, step - 1],
+            device(here_outer, here_inner + sign),
+        )
+
+    def outer_copy(column, slot, direction, sign, step, arriving):
+        piece = -sign * step if arriving else -sign * (step - 1)
+        if step == 1 and column == 0:
+            source = block_ref
+        else:
+            source = out_ref.at[outer_at(piece), inner_at(column)]
+        return remote(
+            source,
+            out_ref.at[outer_at(piece), inner_at(column)],
+            outer_send_sems.at[slot, direction, step - 1],
+            outer_recv_sems.at[slot, direction, step - 1],
+            device(here_outer + sign, here_inner),
+        )
+
+    def launch(copy):
+        copy.start()
+        sent.append(copy)
+
+    columns = [0]
+    for direction, sign, steps in inner_plans:
+        if steps:
+            launch(inner_copy(direction, sign, 1, False))
+    for direction, sign, steps in outer_plans:
+        if steps:
+            launch(outer_copy(0, 0, direction, sign, 1, False))
+    for step in range(1, inner // 2 + 1):
+        for direction, sign, steps in inner_plans:
+            if step > steps:
+                continue
+            inner_copy(direction, sign, step, True).wait_recv()
+            if step < steps:
+                launch(inner_copy(direction, sign, step + 1, False))
+            columns.append(-sign * step)
+            for outer_direction, outer_sign, outer_steps in outer_plans:
+                if outer_steps:
+                    launch(outer_copy(columns[-1], len(columns) - 1, outer_direction, outer_sign, 1, False))
+    for step in range(2, outer // 2 + 1):
+        for slot, column in enumerate(columns):
+            for direction, sign, steps in outer_plans:
                 if step > steps:
                     continue
-                origin = -sign * (step - 1)
-                if step > 1:
-                    pending[direction].wait_recv()
-                source = first_source if step == 1 else place(origin)
-                copy = pltpu.make_async_remote_copy(
-                    src_ref=source,
-                    dst_ref=place(origin),
-                    send_sem=send_sems.at[stage, direction, step - 1],
-                    recv_sem=recv_sems.at[stage, direction, step - 1],
-                    device_id=step_to(sign),
-                    device_id_type=MESH_IDS,
-                )
-                copy.start()
-                sent.append(copy)
-                pending[direction] = pltpu.make_async_remote_copy(
-                    src_ref=source,
-                    dst_ref=place(-sign * step),
-                    send_sem=send_sems.at[stage, direction, step - 1],
-                    recv_sem=recv_sems.at[stage, direction, step - 1],
-                    device_id=step_to(sign),
-                    device_id_type=MESH_IDS,
-                )
-        for waiting in pending:
-            if waiting is not None:
-                waiting.wait_recv()
-
-    def inner_place(offset):
-        return out_ref.at[here_outer, lax.rem(here_inner + offset + inner, inner)]
-
-    def outer_place(offset):
-        return out_ref.at[lax.rem(here_outer + offset + outer, outer)]
-
-    run_ring(0, inner, inner_place, block_ref, lambda sign: device(here_outer, here_inner + sign))
+                outer_copy(column, slot, direction, sign, step - 1, True).wait_recv()
+                launch(outer_copy(column, slot, direction, sign, step, False))
+    for slot, column in enumerate(columns):
+        for direction, sign, steps in outer_plans:
+            if steps:
+                outer_copy(column, slot, direction, sign, steps, True).wait_recv()
     own.wait()
-    run_ring(1, outer, outer_place, out_ref.at[here_outer], lambda sign: device(here_outer + sign, here_inner))
     for copy in sent:
         copy.wait_send()
 
 
 def ring_gather(block, inner, outer):
     rows, cols = block.shape
-    most_steps = max(inner, outer) // 2
     return pl.pallas_call(
         functools.partial(ring_gather_kernel, inner, outer),
         out_shape=jax.ShapeDtypeStruct((outer, inner, rows, cols), block.dtype),
@@ -101,8 +137,10 @@
         out_specs=pl.BlockSpec(memory_space=pl.ANY),
         scratch_shapes=[
             pltpu.SemaphoreType.DMA(()),
-            pltpu.SemaphoreType.DMA((2, 2, most_steps)),
-            pltpu.SemaphoreType.DMA((2, 2, most_steps)),
+            pltpu.SemaphoreType.DMA((2, max(1, inner // 2))),
+            pltpu.SemaphoreType.DMA((2, max(1, inner // 2))),
+            pltpu.SemaphoreType.DMA((inner, 2, max(1, outer // 2))),
+            pltpu.SemaphoreType.DMA((inner, 2, max(1, outer // 2))),
         ],
         compiler_params=pltpu.CompilerParams(collective_id=0, has_side_effects=True),
     )(block).reshape(outer * inner * rows, cols)

time: 252 us -> 249 us (0.988)
  Pallas kernels: 119 us -> 112 us
  waiting for transfers between devices: 46.3 us -> 51.5 us
    pallas_call x1, Pallas kernels: 119 us -> 112 us  [ring_gather(): pl.pallas_call(functools.partial(ring_gather_kernel, inner, outer), out_s...]
    ppermute x2, waiting for transfers between devices: 12.5 us -> 16.9 us  [from_behind(): lax.ppermute(value, axis, [(source, source + steps) for source in range(l...]
  transfers between devices with their start and end apart: 5 -> 5, of which waited for: 3 -> 3; matrix products, arithmetic and copies ran while one was open for 7% -> 7% of each run, Pallas kernels for 48% -> 45%
where the time goes in v7:
time: 249 us; the launch traced here: 248 us
  Pallas kernels  112 us (45%)
  waiting for transfers between devices  51.5 us (21%)
  starting transfers between devices  19.1 us (8%)
  other arithmetic  18.6 us (7%)
  matrix products  17.8 us (7%)
  between operations  14.6 us (6%)
  local copies, waits for them, and re-layouts  11.9 us (5%)
  loops' own time  2.71 us (1%)
    pallas_call x1, Pallas kernels, ring_gather(): pl.pallas_call(functools.partial(ring_gather_kernel, inner, outer), out_s...  112 us
    all_to_all x1, waiting for transfers between devices, shards(): lax.all_to_all(flagged.reshape(req_count, page_cap, page_width + flag_col...  33.9 us
    ppermute x2, waiting for transfers between devices, from_behind(): lax.ppermute(value, axis, [(source, source + steps) for source in range(l...  16.9 us
    all_to_all x1, starting transfers between devices, shards(): lax.all_to_all(flagged.reshape(req_count, page_cap, page_width + flag_col...  13.3 us
    ppermute x2, starting transfers between devices, from_behind(): lax.ppermute(value, axis, [(source, source + steps) for source in range(l...  5.74 us
    dot_general x1, matrix products, shards(): lax.dot_general(hidden, fc2_full_t, contract_rows, preferred_element_type...  5.16 us
  transfers between devices with their start and end apart: 5, of which 3 were waited for; matrix products, arithmetic and copies ran while one was open for 7% of the time, Pallas kernels for 45%

profile of v7, /device:TPU:6, one launch (start us, length us, event | category | flops | bytes accessed | tf_op | source)
XLA Modules:
  0.0 248.4 jit_solution(10307284025105436339)
XLA Ops:
  12.6 112.1 %shard_map.176 = bf16[16,4,32,2176]{3,2,1,0:T(8,128)(2,1)} custom-call(bf16[32,2176]{1,0:T(8,128)(2,1)} %copy-done.4), custom_call_target="tpu_custom_call" | custom-call | tf_op jit(solution)/shard_map/pallas_call | solution.py:133
  124.8 1.1 slice.97
  128.5 1.8 constant_dynamic-update-slice_fusion.14
  130.4 1.9 constant_dynamic-update-slice_fusion.8
  132.9 1.5 convert_reduce_fusion
  134.4 1.6 fusion.25
  136.1 3.0 %fusion.32 = f32[256,768]{1,0:T(8,128)S(1)} fusion(bf16[2048,2176]{1,0:T(8,128)(2,1)} %bitcast.43, f32[768]{0:T(1024)S(1)} %add.197, bf16[256,2048]{1,0:T(8,128)(2,1)S(1)} %copy-done, f32[2048]{0:T(1024)S(1)} %copy-done.11, f32[2048]{0:T(1024)S(1)} %copy-done.13, f32[256]{0:T(256)S(1)} %add_rsqrt_fusion, f32[256]{0:T(256)S(1)} %broadcast_multiply_fusion), kind=kOutput, calls=%fused_computation.39 | convolution fusion | flops 808648704 | bytes 5002240 | tf_op jit(solution)/shard_map/dot_general | solution.py:292
  139.6 3.1 %collective-permute-start.1 = (bf16[512,2,256]{0,2,1:T(8,128)(2,1)S(1)}, bf16[512,2,256]{0,2,1:T(8,128)(2,1)S(1)}, u32[]{:S(2)}, u32[]{:S(2)}) collective-permute-start(bf16[512,2,256]{0,2,1:T(8,128)(2,1)S(1)} %pad_maximum_fusion.2), channel_id=1, source_target_pairs={{0,16},{8,24},{16,32},{24,40},{32,48},{40,56},{48,64},{56,72},{64,... | collective-permute-start | bytes 1572872 | tf_op jit(solution)/shard_map/ppermute | solution.py:155
  142.8 2.6 %collective-permute-start = (bf16[512,2,256]{0,2,1:T(8,128)(2,1)S(1)}, bf16[512,2,256]{0,2,1:T(8,128)(2,1)S(1)}, u32[]{:S(2)}, u32[]{:S(2)}) collective-permute-start(bf16[512,2,256]{0,2,1:T(8,128)(2,1)S(1)} %pad_maximum_fusion.2), channel_id=1, source_target_pairs={{0,8},{8,16},{16,24},{24,32},{32,40},{40,48},{48,56},{56,64},{64,7... | collective-permute-start | bytes 1572872 | tf_op jit(solution)/shard_map/ppermute | solution.py:155
  145.4 1.8 constant_dynamic-update-slice_fusion.6
  147.3 7.9 %collective-permute-done.1 = bf16[512,2,256]{0,2,1:T(8,128)(2,1)S(1)} collective-permute-done((bf16[512,2,256]{0,2,1:T(8,128)(2,1)S(1)}, bf16[512,2,256]{0,2,1:T(8,128)(2,1)S(1)}, u32[]{:S(2)}, u32[]{:S(2)}) %collective-permute-start.1) | collective-permute-done | bytes 524320 | tf_op jit(solution)/shard_map/ppermute | solution.py:155
  155.1 9.0 %collective-permute-done = bf16[512,2,256]{0,2,1:T(8,128)(2,1)S(1)} collective-permute-done((bf16[512,2,256]{0,2,1:T(8,128)(2,1)S(1)}, bf16[512,2,256]{0,2,1:T(8,128)(2,1)S(1)}, u32[]{:S(2)}, u32[]{:S(2)}) %collective-permute-start) | collective-permute-done | bytes 524320 | tf_op jit(solution)/shard_map/ppermute | solution.py:155
  164.4 15.9 %while.11 = (s32[]{:T(128)}, bf16[4,256,64]{1,2,0:T(8,128)(2,1)S(1)}, s32[4]{0:T(128)S(1)}, bf16[256,256]{0,1:T(8,128)(2,1)S(1)}, bf16[1536,256]{0,1:T(8,128)(2,...) while((s32[]{:T(128)}, ...), condition=%wide.region_25.26_spmd.clone, body=%wide.region_22.25_spmd.clone.sunk | while | flops 112492032 | bytes 5240535 | solution.py:225
  166.5 0.9 fusion.96
  170.5 0.9 fusion.96
  174.5 0.9 fusion.96
  178.5 0.9 fusion.96
  180.3 1.7 fusion.38
  182.1 5.2 %convolution_add_fusion = f32[256,2048]{1,0:T(8,128)} fusion(f32[256,2048]{1,0:T(8,128)S(1)} %fusion.38, bf16[2048,2176]{1,0:T(8,128)(2,1)} %bitcast.45, f32[512]{0:T(512)} %param.31, bf16[256,2048]{1,0:T(8,128)(2,1)S(1)} %copy-done, f32[2048]{0:T(1024)S(1)} %copy-done.12, f32[2048]{0:T(1024)} %param.24, f32[256]{0:T(256)S(1)} %add_rsqrt_fusion, ...), kind=kOutput, calls=%fused_computation.23 | convolution fusion | flops 1078722560 | bytes 9457664 | tf_op jit(solution)/shard_map/dot_general | solution.py:374
  189.3 1.0 reshape.262
  190.3 13.3 %all-to-all-start = ((bf16[64,2,2176]{2,1,0:T(2,128)(2,1)}), bf16[64,2,2176]{2,1,0:T(2,128)(2,1)S(1)}, u32[]{:S(2)}, u32[]{:S(2)}) async-start(bf16[64,2,2176]{2,1,0:T(2,128)(2,1)} %reshape.262), calls=%async_computation.1 | async-start | bytes 1114112 | tf_op jit(solution)/shard_map/all_to_all | solution.py:326
  204.1 33.9 %all-to-all-done = bf16[64,2,2176]{2,1,0:T(2,128)(2,1)S(1)} async-done(((bf16[64,2,2176]{2,1,0:T(2,128)(2,1)}), bf16[64,2,2176]{2,1,0:T(2,128)(2,1)S(1)}, u32[]{:S(2)}, u32[]{:S(2)}) %all-to-all-start) | async-done | bytes 557088 | tf_op jit(solution)/shard_map/all_to_all | solution.py:326
  238.7 1.2 reshape.265
  239.9 1.6 add_convert_fusion
  (113 shorter events, 21.9 us)
Async XLA Ops:
  7.2 125.7 %all-gather.2.cloned.1.call-start = ((), (), s32[]{:S(2)}) async-start(), calls=%async_computation.2 | async-start | bytes 1179648 | tf_op jit(solution)/shard_map/all_gather | solution.py:255
  7.9 232.0 %reduce-scatter.2.cloned.1.call-start = ((), (), s32[]{:S(2)}) async-start(), calls=%async_computation.3 | async-start | bytes 2359296 | tf_op jit(solution)/shard_map/reduce_scatter | solution.py:378
  11.9 0.7 copy-start.4
  12.6 112.1 %copy-start.5 = (f32[3,256]{1,0:T(4,128)S(1)}, f32[3,256]{1,0:T(4,128)}, u32[]{:S(2)}) copy-start(f32[3,256]{1,0:T(4,128)} %param.27) | copy-start | bytes 9220
  124.7 2.2 copy-start.7
  124.7 7.7 %copy-start.3 = (bf16[256,2,256]{2,1,0:T(2,128)(2,1)S(1)}, bf16[256,2,256]{2,1,0:T(2,128)(2,1)}, u32[]{:S(2)}) copy-start(bf16[256,2,256]{2,1,0:T(2,128)(2,1)} %param.34) | copy-start | bytes 786436
  125.9 10.2 %copy-start.11 = (f32[2048]{0:T(1024)S(1)}, f32[2048]{0:T(1024)}, u32[]{:S(2)}) copy-start(f32[2048]{0:T(1024)} %param.25) | copy-start | bytes 24580
  125.9 10.2 %copy-start.13 = (f32[2048]{0:T(1024)S(1)}, f32[2048]{0:T(1024)}, u32[]{:S(2)}) copy-start(f32[2048]{0:T(1024)} %param.24) | copy-start | bytes 24580
  132.9 3.2 %copy-start = (bf16[256,2048]{1,0:T(8,128)(2,1)S(1)}, bf16[256,2048]{1,0:T(8,128)(2,1)}, u32[]{:S(2)}) copy-start(bf16[256,2048]{1,0:T(8,128)(2,1)} %all-gather.2.cloned.1.call-done) | copy-start | bytes 3145732
  139.6 15.5 %collective-permute-start.1 = (bf16[512,2,256]{0,2,1:T(8,128)(2,1)S(1)}, bf16[512,2,256]{0,2,1:T(8,128)(2,1)S(1)}, u32[]{:S(2)}, u32[]{:S(2)}) collective-permute-start(bf16[512,2,256]{0,2,1:T(8,128)(2,1)S(1)} %pad_maximum_fusion.2), channel_id=1, source_target_pairs={{0,16},{8,24},{16,32},{24,40},{32,48},{40,56},{48,64},{56,72},{64,... | collective-permute-start | bytes 1572872 | tf_op jit(solution)/shard_map/ppermute | solution.py:155
  142.8 21.4 %collective-permute-start = (bf16[512,2,256]{0,2,1:T(8,128)(2,1)S(1)}, bf16[512,2,256]{0,2,1:T(8,128)(2,1)S(1)}, u32[]{:S(2)}, u32[]{:S(2)}) collective-permute-start(bf16[512,2,256]{0,2,1:T(8,128)(2,1)S(1)} %pad_maximum_fusion.2), channel_id=1, source_target_pairs={{0,8},{8,16},{16,24},{24,32},{32,40},{40,48},{48,56},{56,64},{64,7... | collective-permute-start | bytes 1572872 | tf_op jit(solution)/shard_map/ppermute | solution.py:155
  180.3 1.7 copy-start.12
  187.2 0.7 copy-start.6
  188.8 14.8 %copy-start.1 = (bf16[512,2,256]{2,1,0:T(2,128)(2,1)S(1)}, bf16[512,2,256]{2,1,0:T(2,128)(2,1)}, u32[]{:S(2)}) copy-start(bf16[512,2,256]{2,1,0:T(2,128)(2,1)} %param.35) | copy-start | bytes 1572868
  189.3 48.9 %copy-start.10 = (s32[1,128]{1,0:T(1,128)S(1)}, s32[1,128]{1,0:T(1,128)}, u32[]{:S(2)}) copy-start(s32[1,128]{1,0:T(1,128)} %param.23) | copy-start | bytes 1540
  190.3 47.6 %all-to-all-start = ((bf16[64,2,2176]{2,1,0:T(2,128)(2,1)}), bf16[64,2,2176]{2,1,0:T(2,128)(2,1)S(1)}, u32[]{:S(2)}, u32[]{:S(2)}) async-start(bf16[64,2,2176]{2,1,0:T(2,128)(2,1)} %reshape.262), calls=%async_computation.1 | async-start | bytes 1114112 | tf_op jit(solution)/shard_map/all_to_all | solution.py:326
  204.0 35.8 %copy-start.2 = (bf16[256,256]{1,0:T(8,128)(2,1)S(1)}, bf16[256,256]{1,0:T(8,128)(2,1)}, u32[]{:S(2)}) copy-start(bf16[256,256]{1,0:T(8,128)(2,1)} %param.19) | copy-start | bytes 393220
  204.0 35.8 %copy-start.8 = (f32[256]{0:T(256)S(1)}, f32[256]{0:T(256)}, u32[]{:S(2)}) copy-start(f32[256]{0:T(256)} %param.33) | copy-start | bytes 3076
  204.0 35.8 %copy-start.9 = (f32[256]{0:T(256)S(1)}, f32[256]{0:T(256)}, u32[]{:S(2)}) copy-start(f32[256]{0:T(256)} %param.29) | copy-start | bytes 3076
Sparse Core Ops, SparseCore 0:
  10.1 34.7 all-gather.1
  187.4 37.4 reduce-scatter.1

commit v8 on v1

--- a/solution.py
+++ b/solution.py
@@ -1,6 +1,10 @@
+import functools
+
 import jax
 import jax.numpy as jnp
 from jax import lax
+from jax.experimental import pallas as pl
+from jax.experimental.pallas import tpu as pltpu
 from jax.sharding import PartitionSpec as P
 
 HEAD_DIM = 64
@@ -9,6 +13,139 @@
 SINKS = 4
 PAGE = 4
 WINDOW = 512
+INNER = 4
+HOP_US = 3.5
+LINK_BYTES_PER_US = 45000.0
+
+
+MESH_IDS = pl.DeviceIdType.MESH
+
+
+def ring_gather_kernel(inner, outer, first_block, second_block, first_out, second_out, own_sems,
+                       *sems):
+    req_index = lax.axis_index("req")
+    tensor_index = lax.axis_index("tensor")
+    here = (req_index // inner, req_index % inner)
+    sizes = (outer, inner)
+
+    def device(shifts):
+        at = [lax.rem(here[axis] + shifts[axis] + sizes[axis], sizes[axis]) for axis in range(2)]
+        return (at[0] * inner + at[1], tensor_index)
+
+    def index(offsets):
+        return tuple(lax.rem(here[axis] + offsets[axis] + sizes[axis], sizes[axis]) for axis in range(2))
+
+    neighbours = (device((0, 1)), device((0, -1)), device((1, 0)), device((-1, 0)))
+    barrier = pltpu.get_barrier_semaphore()
+    for neighbour in neighbours:
+        pl.semaphore_signal(barrier, inc=1, device_id=neighbour, device_id_type=MESH_IDS)
+    pl.semaphore_wait(barrier, len(neighbours))
+
+    lanes = []
+    for lane, (block_ref, out_ref, first_axis) in enumerate(
+        ((first_block, first_out, 1), (second_block, second_out, 0))
+    ):
+        own = pltpu.make_async_copy(block_ref, out_ref.at[here[0], here[1]], own_sems.at[lane])
+        own.start()
+        lanes.append((block_ref, out_ref, first_axis, own, sems[4 * lane : 4 * lane + 4]))
+
+    def plans(count):
+        return [(0, 1, count // 2), (1, -1, (count - 1) // 2)]
+
+    def offsets_of(axis, offset, other_axis, other_offset):
+        pair = [0, 0]
+        pair[axis] = offset
+        pair[other_axis] = other_offset
+        return tuple(pair)
+
+    def copy_of(lane, ring, column, slot, direction, sign, step, arriving):
+        block_ref, out_ref, first_axis, _, lane_sems = lanes[lane]
+        axis = first_axis if ring == 0 else 1 - first_axis
+        piece = -sign * step if arriving else -sign * (step - 1)
+        place = offsets_of(axis, piece, 1 - axis, column)
+        target = out_ref.at[index(place)]
+        if step == 1 and (ring == 0 or column == 0):
+            source = block_ref
+        else:
+            source = target
+        first_send, first_recv, second_send, second_recv = lane_sems
+        if ring == 0:
+            send_sem, recv_sem = first_send.at[direction, step - 1], first_recv.at[direction, step - 1]
+        else:
+            send_sem = second_send.at[slot, direction, step - 1]
+            recv_sem = second_recv.at[slot, direction, step - 1]
+        return pltpu.make_async_remote_copy(
+            src_ref=source,
+            dst_ref=target,
+            send_sem=send_sem,
+            recv_sem=recv_sem,
+            device_id=device(offsets_of(axis, sign, 1 - axis, 0)),
+            device_id_type=MESH_IDS,
+        )
+
+    tasks = []
+    for lane, (block_ref, _, first_axis, _, _) in enumerate(lanes):
+        block_bytes = block_ref.shape[0] * block_ref.shape[1] * 2
+        duration = HOP_US + block_bytes / LINK_BYTES_PER_US
+        first_count = sizes[first_axis]
+        second_count = sizes[1 - first_axis]
+        columns = [(0, 0.0, None)]
+        for direction, sign, steps in plans(first_count):
+            ready = 0.0
+            for step in range(1, steps + 1):
+                need = None if step == 1 else (lane, 0, 0, 0, direction, sign, step - 1)
+                tasks.append((ready, len(tasks), (lane, 0, 0, 0, direction, sign, step), need))
+                ready += duration
+                columns.append((-sign * step, ready, (lane, 0, 0, 0, direction, sign, step)))
+        columns.sort(key=lambda entry: entry[1])
+        for slot, (column, start, need) in enumerate(columns):
+            for direction, sign, steps in plans(second_count):
+                ready = start
+                for step in range(1, steps + 1):
+                    if step > 1:
+                        need = (lane, 1, column, slot, direction, sign, step - 1)
+                    tasks.append((ready, len(tasks), (lane, 1, column, slot, direction, sign, step), need))
+                    ready += duration
+                final = (lane, 1, column, slot, direction, sign, steps)
+                if steps:
+                    tasks.append((float("inf"), len(tasks), None, final))
+                need = columns[slot][2]
+    tasks.sort(key=lambda entry: (entry[0], entry[1]))
+    sent = []
+    waited = set()
+    for _, _, send, need in tasks:
+        if need is not None and need not in waited:
+            waited.add(need)
+            copy_of(*need, True).wait_recv()
+        if send is not None:
+            copy = copy_of(*send, False)
+            copy.start()
+            sent.append(copy)
+    for _, _, _, own, _ in lanes:
+        own.wait()
+    for copy in sent:
+        copy.wait_send()
+
+
+def ring_gather(first_block, second_block, inner, outer):
+    semaphores = []
+    for first_count, second_count in ((inner, outer), (outer, inner)):
+        first_shape = (2, max(1, first_count // 2))
+        second_shape = (first_count, 2, max(1, second_count // 2))
+        semaphores += [pltpu.SemaphoreType.DMA(first_shape)] * 2
+        semaphores += [pltpu.SemaphoreType.DMA(second_shape)] * 2
+    gathered = pl.pallas_call(
+        functools.partial(ring_gather_kernel, inner, outer),
+        out_shape=tuple(
+            jax.ShapeDtypeStruct((outer, inner) + block.shape, block.dtype)
+            for block in (first_block, second_block)
+        ),
+        in_specs=[pl.BlockSpec(memory_space=pl.ANY)] * 2,
+        out_specs=(pl.BlockSpec(memory_space=pl.ANY),) * 2,
+        scratch_shapes=[pltpu.SemaphoreType.DMA((2,))] + semaphores,
+        compiler_params=pltpu.CompilerParams(collective_id=0, has_side_effects=True),
+    )(first_block, second_block)
+    return [part.reshape(outer * inner * part.shape[2], part.shape[3]) for part in gathered]
 
 
 EPSILON = 1e-05
@@ -137,16 +274,13 @@
     fc1_cols = fc1_weight.shape[1]
     dense_cols = dense_weight.shape[0]
     fc2_cols = fc2_weight.shape[0]
-    packed = jnp.concatenate(
-        [qkv_local, fc1_weight, dense_weight.T, fc2_weight.T, digits], axis=1
-    )
-    everything = lax.all_gather(packed, "req", axis=0, tiled=True)
-    edges = [0]
-    for width in (3 * head_cols, fc1_cols, dense_cols, fc2_cols, digit_cols):
-        edges.append(edges[-1] + width)
-    qkv_full, fc1_full, dense_full_t, fc2_full_t, digits_full = [
-        everything[:, edges[i] : edges[i + 1]] for i in range(5)
-    ]
+    first_pack = jnp.concatenate([qkv_local, digits], axis=1)
+    second_pack = jnp.concatenate([fc1_weight, dense_weight.T, fc2_weight.T], axis=1)
+    first_full, second_full = ring_gather(first_pack, second_pack, INNER, req_count // INNER)
+    qkv_full, digits_full = jnp.split(first_full, [3 * head_cols], axis=1)
+    fc1_full, dense_full_t, fc2_full_t = jnp.split(
+        second_full, [fc1_cols, fc1_cols + dense_cols], axis=1
+    )
     digit_table = digits_full.reshape(req_count, weight_rows * digit_cols)[:, : 2 * label_count]
     digit_table = digit_table.astype(jnp.int32)
     starts = jnp.min(

time: 321 us -> 209 us (0.65)
  waiting for transfers between devices: 234 us -> 37 us
  Pallas kernels: 0 us -> 83.5 us
  local copies, waits for them, and re-layouts: 14.5 us -> 9.13 us
  starting transfers between devices: 18.3 us -> 22.9 us
    all_gather x1 -> x0, waiting for transfers between devices: 161 us -> none  [shards(): everything = lax.all_gather(packed, 'req', axis=0, tiled=True)]
    pallas_call x0 -> x1, Pallas kernels: none -> 83.5 us  [ring_gather(): pl.pallas_call(functools.partial(ring_gather_kernel, inner, outer), out_s...]
    all_gather x1, waiting for transfers between devices: 30.4 us -> 0.02 us  [shards(): gathered = lax.all_gather(tokens, 'tensor', axis=1, tiled=True)]
    unnamed x35 -> x37, local copies, waits for them, and re-layouts: 6.12 us -> 0.91 us
    all_to_all x1, waiting for transfers between devices: 30.7 us -> 26.5 us  [shards(): lax.all_to_all(flagged.reshape(req_count, page_cap, page_width + flag_col...]
    all_to_all x1, starting transfers between devices: 12.5 us -> 16.6 us  [shards(): lax.all_to_all(flagged.reshape(req_count, page_cap, page_width + flag_col...]
  transfers between devices with their start and end apart: 6 -> 5, of which waited for: 5 -> 3; matrix products, arithmetic and copies ran while one was open for 5% -> 9% of each run, Pallas kernels for 0% -> 40%
where the time goes in v8:
time: 209 us; the launch traced here: 208 us
  Pallas kernels  83.5 us (40%)
  waiting for transfers between devices  37 us (18%)
  starting transfers between devices  22.9 us (11%)
  other arithmetic  20.6 us (10%)
  matrix products  17.7 us (8%)
  between operations  14.7 us (7%)
  local copies, waits for them, and re-layouts  9.13 us (4%)
  loops' own time  2.65 us (1%)
    pallas_call x1, Pallas kernels, ring_gather(): pl.pallas_call(functools.partial(ring_gather_kernel, inner, outer), out_s...  83.5 us
    all_to_all x1, waiting for transfers between devices, shards(): lax.all_to_all(flagged.reshape(req_count, page_cap, page_width + flag_col...  26.5 us
    all_to_all x1, starting transfers between devices, shards(): lax.all_to_all(flagged.reshape(req_count, page_cap, page_width + flag_col...  16.6 us
    ppermute x2, waiting for transfers between devices, from_behind(): lax.ppermute(value, axis, [(source, source + steps) for source in range(l...  9.77 us
    ppermute x2, starting transfers between devices, from_behind(): lax.ppermute(value, axis, [(source, source + steps) for source in range(l...  6.18 us
    dot_general x1, matrix products, shards(): lax.dot_general(hidden, fc2_full_t, contract_rows, preferred_element_type...  5.14 us
  transfers between devices with their start and end apart: 5, of which 3 were waited for; matrix products, arithmetic and copies ran while one was open for 9% of the time, Pallas kernels for 40%

profile of v8, /device:TPU:6, one launch (start us, length us, event | category | flops | bytes accessed | tf_op | source)
XLA Modules:
  0.0 208.2 jit_solution(8912775906703039093)
XLA Ops:
  10.4 1.4 pad_maximum_fusion.6.second_block
  11.8 83.5 %shard_map.176 = (bf16[16,4,32,896]{3,2,1,0:T(8,128)(2,1)}, bf16[16,4,32,1280]{3,2,1,0:T(8,128)(2,1)}) custom-call(bf16[32,896]{1,0:T(8,128)(2,1)} %pad_maximum_fusion.7.first_block, bf16[32,1280]{1,0:T(8,128)(2,1)} %pad_maximum_fusion.6.second_block), custom_call_target="tpu_custom_call" | custom-call | tf_op jit(solution)/shard_map/pallas_call | solution.py:137
  95.3 1.1 split.21
  99.0 1.8 constant_dynamic-update-slice_fusion.8
  100.9 1.9 constant_dynamic-update-slice_fusion.4
  103.4 1.5 convert_reduce_fusion
  105.0 1.6 fusion.25
  106.7 3.0 %fusion.32 = f32[256,768]{1,0:T(8,128)S(1)} fusion(bf16[2048,896]{1,0:T(8,128)(2,1)} %bitcast.53, f32[768]{0:T(1024)S(1)} %add.197, bf16[256,2048]{1,0:T(8,128)(2,1)S(1)} %copy-done, f32[2048]{0:T(1024)S(1)} %copy-done.14, f32[2048]{0:T(1024)S(1)} %copy-done.16, f32[256]{0:T(256)S(1)} %add_rsqrt_fusion, f32[256]{0:T(256)S(1)} %broadcast_multiply_fusion), kind=kOutput, calls=%fused_computation.39 | convolution fusion | flops 808648704 | bytes 5002240 | tf_op jit(solution)/shard_map/dot_general | solution.py:291
  110.2 2.6 %collective-permute-start = (bf16[512,2,256]{0,2,1:T(8,128)(2,1)S(1)}, bf16[512,2,256]{0,2,1:T(8,128)(2,1)S(1)}, u32[]{:S(2)}, u32[]{:S(2)}) collective-permute-start(bf16[512,2,256]{0,2,1:T(8,128)(2,1)S(1)} %pad_maximum_fusion.2), channel_id=1, source_target_pairs={{0,8},{8,16},{16,24},{24,32},{32,40},{40,48},{48,56},{56,64},{64,7... | collective-permute-start | bytes 1572872 | tf_op jit(solution)/shard_map/ppermute | solution.py:157
  112.8 3.5 %collective-permute-start.1 = (bf16[512,2,256]{0,2,1:T(8,128)(2,1)S(1)}, bf16[512,2,256]{0,2,1:T(8,128)(2,1)S(1)}, u32[]{:S(2)}, u32[]{:S(2)}) collective-permute-start(bf16[512,2,256]{0,2,1:T(8,128)(2,1)S(1)} %pad_maximum_fusion.2), channel_id=1, source_target_pairs={{0,16},{8,24},{16,32},{24,40},{32,48},{40,56},{48,64},{56,72},{64,... | collective-permute-start | bytes 1572872 | tf_op jit(solution)/shard_map/ppermute | solution.py:157
  116.4 1.8 constant_dynamic-update-slice_fusion
  118.2 4.2 %collective-permute-done = bf16[512,2,256]{0,2,1:T(8,128)(2,1)S(1)} collective-permute-done((bf16[512,2,256]{0,2,1:T(8,128)(2,1)S(1)}, bf16[512,2,256]{0,2,1:T(8,128)(2,1)S(1)}, u32[]{:S(2)}, u32[]{:S(2)}) %collective-permute-start) | collective-permute-done | bytes 524320 | tf_op jit(solution)/shard_map/ppermute | solution.py:157
  122.4 5.6 %collective-permute-done.1 = bf16[512,2,256]{0,2,1:T(8,128)(2,1)S(1)} collective-permute-done((bf16[512,2,256]{0,2,1:T(8,128)(2,1)S(1)}, bf16[512,2,256]{0,2,1:T(8,128)(2,1)S(1)}, u32[]{:S(2)}, u32[]{:S(2)}) %collective-permute-start.1) | collective-permute-done | bytes 524320 | tf_op jit(solution)/shard_map/ppermute | solution.py:157
  128.3 15.9 %while.11 = (s32[]{:T(128)}, bf16[4,256,64]{1,2,0:T(8,128)(2,1)S(1)}, s32[4]{0:T(128)S(1)}, bf16[256,256]{0,1:T(8,128)(2,1)S(1)}, bf16[1536,256]{0,1:T(8,128)(2,...) while((s32[]{:T(128)}, ...), condition=%wide.region_25.26_spmd.clone, body=%wide.region_22.25_spmd.clone.sunk | while | flops 112492032 | bytes 5240527 | solution.py:227
  130.4 0.9 fusion.96
  134.4 0.9 fusion.96
  138.4 0.9 fusion.96
  144.2 1.7 fusion.38
  146.0 5.1 %convolution_add_fusion = f32[256,2048]{1,0:T(8,128)} fusion(f32[256,2048]{1,0:T(8,128)S(1)} %fusion.38, bf16[2048,1280]{1,0:T(8,128)(2,1)} %bitcast.48, f32[512]{0:T(512)} %param.31, bf16[256,2048]{1,0:T(8,128)(2,1)S(1)} %copy-done, f32[2048]{0:T(1024)S(1)} %copy-done.15, f32[2048]{0:T(1024)} %param.24, f32[256]{0:T(256)S(1)} %copy-done.12, ...), kind=kOutput, calls=%fused_computation.23 | convolution fusion | flops 1078722560 | bytes 9457664 | tf_op jit(solution)/shard_map/dot_general | solution.py:373
  153.2 1.0 reshape.266
  154.2 16.6 %all-to-all-start = ((bf16[64,2,2176]{2,1,0:T(2,128)(2,1)}), bf16[64,2,2176]{2,1,0:T(2,128)(2,1)S(1)}, u32[]{:S(2)}, u32[]{:S(2)}) async-start(bf16[64,2,2176]{2,1,0:T(2,128)(2,1)} %reshape.266), calls=%async_computation.1 | async-start | bytes 1114112 | tf_op jit(solution)/shard_map/all_to_all | solution.py:325
  171.3 26.5 %all-to-all-done = bf16[64,2,2176]{2,1,0:T(2,128)(2,1)S(1)} async-done(((bf16[64,2,2176]{2,1,0:T(2,128)(2,1)}), bf16[64,2,2176]{2,1,0:T(2,128)(2,1)S(1)}, u32[]{:S(2)}, u32[]{:S(2)}) %all-to-all-start) | async-done | bytes 557088 | tf_op jit(solution)/shard_map/all_to_all | solution.py:325
  198.5 1.2 reshape.269
  199.7 1.6 add_convert_fusion
  (117 shorter events, 20.6 us)
Async XLA Ops:
  7.2 90.2 %copy-start.8 = (s32[43]{0:T(128)S(1)}, s32[43]{0:T(128)}, u32[]{:S(2)}) copy-start(s32[43]{0:T(128)} %param.21) | copy-start | bytes 520
  7.2 95.8 %copy-start.4 = (f32[3,256]{1,0:T(4,128)S(1)}, f32[3,256]{1,0:T(4,128)}, u32[]{:S(2)}) copy-start(f32[3,256]{1,0:T(4,128)} %param.27) | copy-start | bytes 9220
  7.2 95.8 %copy-start.3 = (bf16[256,2,256]{2,1,0:T(2,128)(2,1)S(1)}, bf16[256,2,256]{2,1,0:T(2,128)(2,1)}, u32[]{:S(2)}) copy-start(bf16[256,2,256]{2,1,0:T(2,128)(2,1)} %param.34) | copy-start | bytes 786436
  7.2 96.2 %all-gather.2.cloned.1.call-start = ((), (), s32[]{:S(2)}) async-start(), calls=%async_computation.2 | async-start | bytes 1179648 | tf_op jit(solution)/shard_map/all_gather | solution.py:257
  7.9 191.8 %reduce-scatter.2.cloned.1.call-start = ((), (), s32[]{:S(2)}) async-start(), calls=%async_computation.3 | async-start | bytes 2359296 | tf_op jit(solution)/shard_map/reduce_scatter | solution.py:377
  96.4 10.2 %copy-start.14 = (f32[2048]{0:T(1024)S(1)}, f32[2048]{0:T(1024)}, u32[]{:S(2)}) copy-start(f32[2048]{0:T(1024)} %param.25) | copy-start | bytes 24580
  96.4 10.2 %copy-start.16 = (f32[2048]{0:T(1024)S(1)}, f32[2048]{0:T(1024)}, u32[]{:S(2)}) copy-start(f32[2048]{0:T(1024)} %param.24) | copy-start | bytes 24580
  103.4 3.2 %copy-start = (bf16[256,2048]{1,0:T(8,128)(2,1)S(1)}, bf16[256,2048]{1,0:T(8,128)(2,1)}, u32[]{:S(2)}) copy-start(bf16[256,2048]{1,0:T(8,128)(2,1)} %all-gather.2.cloned.1.call-done) | copy-start | bytes 3145732
  105.0 4.7 %copy-start.5 = (f32[256]{0:T(256)}, f32[256]{0:T(256)S(1)}, u32[]{:S(2)}) copy-start(f32[256]{0:T(256)S(1)} %broadcast_multiply_fusion) | copy-start | bytes 3076
  106.7 3.0 %copy-start.11 = (f32[256]{0:T(256)}, f32[256]{0:T(256)S(1)}, u32[]{:S(2)}) copy-start(f32[256]{0:T(256)S(1)} %add_rsqrt_fusion) | copy-start | bytes 3076
  110.2 12.2 %collective-permute-start = (bf16[512,2,256]{0,2,1:T(8,128)(2,1)S(1)}, bf16[512,2,256]{0,2,1:T(8,128)(2,1)S(1)}, u32[]{:S(2)}, u32[]{:S(2)}) collective-permute-start(bf16[512,2,256]{0,2,1:T(8,128)(2,1)S(1)} %pad_maximum_fusion.2), channel_id=1, source_target_pairs={{0,8},{8,16},{16,24},{24,32},{32,40},{40,48},{48,56},{56,64},{64,7... | collective-permute-start | bytes 1572872 | tf_op jit(solution)/shard_map/ppermute | solution.py:157
  112.8 15.2 %collective-permute-start.1 = (bf16[512,2,256]{0,2,1:T(8,128)(2,1)S(1)}, bf16[512,2,256]{0,2,1:T(8,128)(2,1)S(1)}, u32[]{:S(2)}, u32[]{:S(2)}) collective-permute-start(bf16[512,2,256]{0,2,1:T(8,128)(2,1)S(1)} %pad_maximum_fusion.2), channel_id=1, source_target_pairs={{0,16},{8,24},{16,32},{24,40},{32,48},{40,56},{48,64},{56,72},{64,... | collective-permute-start | bytes 1572872 | tf_op jit(solution)/shard_map/ppermute | solution.py:157
  144.2 1.8 copy-start.6
  144.2 1.8 copy-start.12
  144.2 1.8 copy-start.15
  151.1 0.7 copy-start.7
  152.7 18.2 %copy-start.1 = (bf16[512,2,256]{2,1,0:T(2,128)(2,1)S(1)}, bf16[512,2,256]{2,1,0:T(2,128)(2,1)}, u32[]{:S(2)}) copy-start(bf16[512,2,256]{2,1,0:T(2,128)(2,1)} %param.35) | copy-start | bytes 1572868
  153.2 44.9 %copy-start.13 = (s32[1,128]{1,0:T(1,128)S(1)}, s32[1,128]{1,0:T(1,128)}, u32[]{:S(2)}) copy-start(s32[1,128]{1,0:T(1,128)} %param.23) | copy-start | bytes 1540
  154.2 43.5 %all-to-all-start = ((bf16[64,2,2176]{2,1,0:T(2,128)(2,1)}), bf16[64,2,2176]{2,1,0:T(2,128)(2,1)S(1)}, u32[]{:S(2)}, u32[]{:S(2)}) async-start(bf16[64,2,2176]{2,1,0:T(2,128)(2,1)} %reshape.266), calls=%async_computation.1 | async-start | bytes 1114112 | tf_op jit(solution)/shard_map/all_to_all | solution.py:325
  171.3 28.4 %copy-start.2 = (bf16[256,256]{1,0:T(8,128)(2,1)S(1)}, bf16[256,256]{1,0:T(8,128)(2,1)}, u32[]{:S(2)}) copy-start(bf16[256,256]{1,0:T(8,128)(2,1)} %param.19) | copy-start | bytes 393220
  171.3 28.4 %copy-start.9 = (f32[256]{0:T(256)S(1)}, f32[256]{0:T(256)}, u32[]{:S(2)}) copy-start(f32[256]{0:T(256)} %param.33) | copy-start | bytes 3076
  171.3 28.4 %copy-start.10 = (f32[256]{0:T(256)S(1)}, f32[256]{0:T(256)}, u32[]{:S(2)}) copy-start(f32[256]{0:T(256)} %param.29) | copy-start | bytes 3076
Sparse Core Ops, SparseCore 0:
  10.1 34.7 all-gather.1
  151.3 40.8 reduce-scatter.1

commit v9 on v8

--- a/solution.py
+++ b/solution.py
@@ -266,8 +266,12 @@
     )
     weight_rows = qkv_weight.shape[0]
     digit_cols = 128
-    digits = jnp.concatenate([earliest_rows // 128, earliest_rows % 128]).astype(jnp.bfloat16)
-    digits = jnp.pad(digits, (0, weight_rows * digit_cols - 2 * label_count)).reshape(
+    owners = page_owner[:, 0]
+    owner_count = owners.shape[0]
+    digits = jnp.concatenate([earliest_rows // 128, earliest_rows % 128, owners])
+    digits = digits.astype(jnp.bfloat16)
+    digit_used = 2 * label_count + owner_count
+    digits = jnp.pad(digits, (0, weight_rows * digit_cols - digit_used)).reshape(
         weight_rows, digit_cols
     )
     qkv_local = qkv_weight.reshape(weight_rows, 3 * head_cols)
@@ -281,10 +285,11 @@
     fc1_full, dense_full_t, fc2_full_t = jnp.split(
         second_full, [fc1_cols, fc1_cols + dense_cols], axis=1
     )
-    digit_table = digits_full.reshape(req_count, weight_rows * digit_cols)[:, : 2 * label_count]
+    digit_table = digits_full.reshape(req_count, weight_rows * digit_cols)[:, :digit_used]
     digit_table = digit_table.astype(jnp.int32)
+    owner_table = digit_table[:, 2 * label_count :]
     starts = jnp.min(
-        digit_table[:, :label_count] * 128 + digit_table[:, label_count:], axis=0
+        digit_table[:, :label_count] * 128 + digit_table[:, label_count : 2 * label_count], axis=0
     )
 
     def add_rows(portion):
@@ -307,7 +312,6 @@
     pages_here = tok_rows // PAGE
     page_width = PAGE * 2 * head_cols
     pages = key_value.reshape(pages_here, page_width)
-    owners = page_owner[:, 0]
     onehot = (owners[:, None] == jnp.arange(req_count, dtype=jnp.int32)[None, :]).astype(jnp.int32)
     earlier = jnp.cumsum(onehot, axis=0) - onehot
     earlier_count = jnp.sum(earlier * onehot, axis=1)
@@ -316,21 +320,13 @@
         jnp.bfloat16
     )
     outgoing = jnp.dot(selecting, pages, preferred_element_type=jnp.float32).astype(jnp.bfloat16)
-    filled = jnp.sum(selecting, axis=1)
-    flag_cols = 128
-    flagged = jnp.concatenate(
-        [outgoing, jnp.broadcast_to(filled[:, None], (pool_count, flag_cols)).astype(jnp.bfloat16)],
-        axis=1,
-    )
-    arrived = lax.all_to_all(
-        flagged.reshape(req_count, page_cap, page_width + flag_cols),
-        "req",
-        split_axis=0,
-        concat_axis=0,
-        tiled=True,
-    ).reshape(pool_count, page_width + flag_cols)
-    incoming = arrived[:, :page_width]
-    incoming_filled = arrived[:, page_width]
+    incoming = lax.all_to_all(
+        outgoing.reshape(req_count, page_cap, page_width), "req", split_axis=0, concat_axis=0, tiled=True
+    ).reshape(pool_count, page_width)
+    mine = jnp.sum((owner_table == req_index).astype(jnp.int32), axis=1)
+    incoming_filled = (
+        mine[:, None] > jnp.arange(page_cap, dtype=jnp.int32)[None, :]
+    ).reshape(pool_count)
     slot_ids = slot_perm[0]
     placing = (slot_ids[None, :] == jnp.arange(pool_count, dtype=jnp.int32)[:, None]) & (
         incoming_filled[None, :] > 0
@@ -364,14 +360,15 @@
         (position[:, None] - key_position[None, :] < WINDOW) | (key_position[None, :] < SINKS)
     )
     all_keys = jnp.concatenate(blocks, axis=0)
+    hidden = jax.nn.gelu(lifted + fc1_bias, approximate=True).astype(jnp.bfloat16)
+    mlp_part = lax.dot_general(
+        hidden, fc2_full_t, (((1,), (1,)), ((), ())), preferred_element_type=jnp.float32
+    )
+    queries, mlp_part = lax.optimization_barrier((queries, mlp_part))
     attended = head_attention(queries, all_keys[:, 0, :], all_keys[:, 1, :], allowed)
-    hidden = jax.nn.gelu(lifted + fc1_bias, approximate=True).astype(jnp.bfloat16)
     contract_rows = (((1,), (1,)), ((), ()))
     attn_part = lax.dot_general(
         attended, dense_full_t, contract_rows, preferred_element_type=jnp.float32
-    )
-    mlp_part = lax.dot_general(
-        hidden, fc2_full_t, contract_rows, preferred_element_type=jnp.float32
     )
     branches = attn_part + mlp_part
     summed = lax.psum_scatter(branches, "tensor", scatter_dimension=1, tiled=True)

time: 209 us -> 210 us (level)
  waiting for transfers between devices: 37 us -> 31.8 us
  matrix products: 17.7 us -> 22.7 us
    dot_general x4, matrix products: 3.54 us -> 7.29 us  [one_head(): lax.dot_general(query_cols, key_cols, (((1,), (1,)), ((), ())), preferred...]
    ppermute x2, waiting for transfers between devices: 9.77 us -> 6.49 us  [from_behind(): lax.ppermute(value, axis, [(source, source + steps) for source in range(l...]
  transfers between devices with their start and end apart: 5 -> 5, of which waited for: 3 -> 3; matrix products, arithmetic and copies ran while one was open for 9% -> 11% of each run, Pallas kernels for 40% -> 40%
where the time goes in v9:
time: 210 us
  Pallas kernels  83.5 us (40%)
  waiting for transfers between devices  31.8 us (15%)
  starting transfers between devices  22.9 us (11%)
  matrix products  22.7 us (11%)
  other arithmetic  21.3 us (10%)
  between operations  14.6 us (7%)
  local copies, waits for them, and re-layouts  10.1 us (5%)
  loops' own time  2.75 us (1%)
    pallas_call x1, Pallas kernels, ring_gather(): pl.pallas_call(functools.partial(ring_gather_kernel, inner, outer), out_s...  83.5 us
    all_to_all x1, waiting for transfers between devices, shards(): lax.all_to_all(outgoing.reshape(req_count, page_cap, page_width), 'req',...  24.6 us
    all_to_all x1, starting transfers between devices, shards(): lax.all_to_all(outgoing.reshape(req_count, page_cap, page_width), 'req',...  16.6 us
    dot_general x4, matrix products, one_head(): lax.dot_general(query_cols, key_cols, (((1,), (1,)), ((), ())), preferred...  7.29 us
    ppermute x2, waiting for transfers between devices, from_behind(): lax.ppermute(value, axis, [(source, source + steps) for source in range(l...  6.49 us
    ppermute x2, starting transfers between devices, from_behind(): lax.ppermute(value, axis, [(source, source + steps) for source in range(l...  6.18 us
    dot_general x1, matrix products, shards(): lax.dot_general(hidden, fc2_full_t, (((1,), (1,)), ((), ())), preferred_e...  5.12 us
  transfers between devices with their start and end apart: 5, of which 3 were waited for; matrix products, arithmetic and copies ran while one was open for 11% of the time, Pallas kernels for 40%

profile of v9, /device:TPU:6, one launch (start us, length us, event | category | flops | bytes accessed | tf_op | source)
XLA Modules:
  0.0 209.6 jit_solution(6180819421175826308)
XLA Ops:
  11.0 1.4 pad_maximum_fusion.5.second_block
  12.4 83.5 %shard_map.176 = (bf16[16,4,32,896]{3,2,1,0:T(8,128)(2,1)}, bf16[16,4,32,1280]{3,2,1,0:T(8,128)(2,1)}) custom-call(bf16[32,896]{1,0:T(8,128)(2,1)} %pad_maximum_fusion.6.first_block, bf16[32,1280]{1,0:T(8,128)(2,1)} %pad_maximum_fusion.5.second_block), custom_call_target="tpu_custom_call" | custom-call | tf_op jit(solution)/shard_map/pallas_call | solution.py:137
  95.9 1.1 split.21
  99.6 1.9 constant_dynamic-update-slice_fusion.8
  101.5 1.9 constant_dynamic-update-slice_fusion.4
  104.0 1.8 constant_dynamic-update-slice_fusion
  105.9 1.5 convert_reduce_fusion
  107.5 1.6 fusion.25
  109.1 3.0 %fusion.33 = f32[256,768]{1,0:T(8,128)S(1)} fusion(bf16[2048,896]{1,0:T(8,128)(2,1)} %bitcast.55, f32[768]{0:T(1024)S(1)} %add.197, bf16[256,2048]{1,0:T(8,128)(2,1)S(1)} %copy-done, f32[2048]{0:T(1024)S(1)} %copy-done.11, f32[2048]{0:T(1024)S(1)} %copy-done.12, f32[256]{0:T(256)S(1)} %add_rsqrt_fusion, f32[256]{0:T(256)S(1)} %broadcast_multiply_fusion), kind=kOutput, calls=%fused_computation.40 | convolution fusion | flops 808648704 | bytes 5002240 | tf_op jit(solution)/shard_map/dot_general | solution.py:296
  112.7 2.6 %collective-permute-start = (bf16[512,2,256]{0,2,1:T(8,128)(2,1)S(1)}, bf16[512,2,256]{0,2,1:T(8,128)(2,1)S(1)}, u32[]{:S(2)}, u32[]{:S(2)}) collective-permute-start(bf16[512,2,256]{0,2,1:T(8,128)(2,1)S(1)} %pad_maximum_fusion.1), channel_id=1, source_target_pairs={{0,8},{8,16},{16,24},{24,32},{32,40},{40,48},{48,56},{56,64},{64,7... | collective-permute-start | bytes 1572872 | tf_op jit(solution)/shard_map/ppermute | solution.py:157
  115.3 3.5 %collective-permute-start.1 = (bf16[512,2,256]{0,2,1:T(8,128)(2,1)S(1)}, bf16[512,2,256]{0,2,1:T(8,128)(2,1)S(1)}, u32[]{:S(2)}, u32[]{:S(2)}) collective-permute-start(bf16[512,2,256]{0,2,1:T(8,128)(2,1)S(1)} %pad_maximum_fusion.1), channel_id=1, source_target_pairs={{0,16},{8,24},{16,32},{24,40},{32,48},{40,56},{48,64},{56,72},{64,... | collective-permute-start | bytes 1572872 | tf_op jit(solution)/shard_map/ppermute | solution.py:157
  118.9 5.1 %fusion.29 = f32[256,2048]{1,0:T(8,128)} fusion(bf16[2048,1280]{1,0:T(8,128)(2,1)} %bitcast.49, f32[512]{0:T(512)S(1)} %copy-done.13, bf16[256,2048]{1,0:T(8,128)(2,1)S(1)} %copy-done, f32[2048]{0:T(1024)S(1)} %copy-done.11, f32[2048]{0:T(1024)S(1)} %copy-done.12, f32[256]{0:T(256)S(1)} %add_rsqrt_fusion, f32[256]{0:T(256)S(1)} %broadcast_multiply_fusion), kind=kOutput, calls=%fused_computation.35 | convolution fusion | flops 1078198272 | bytes 7360512 | tf_op jit(solution)/shard_map/dot_general | solution.py:364
  124.9 5.6 %collective-permute-done.1 = bf16[512,2,256]{0,2,1:T(8,128)(2,1)S(1)} collective-permute-done((bf16[512,2,256]{0,2,1:T(8,128)(2,1)S(1)}, bf16[512,2,256]{0,2,1:T(8,128)(2,1)S(1)}, u32[]{:S(2)}, u32[]{:S(2)}) %collective-permute-start.1) | collective-permute-done | bytes 524320 | tf_op jit(solution)/shard_map/ppermute | solution.py:157
  131.6 19.6 %while.11 = (s32[]{:T(128)}, bf16[4,256,64]{1,2,0:T(8,128)(2,1)S(1)}, s32[4]{0:T(128)S(1)}, bf16[256,256]{0,1:T(8,128)(2,1)S(1)}, bf16[1536,256]{0,1:T(8,128)(2,...) while((s32[]{:T(128)}, ...), condition=%wide.region_25.26_spmd.clone, body=%wide.region_22.25_spmd.clone.sunk | while | flops 112492032 | bytes 5240527 | solution.py:227
  132.9 1.8 fusion.95
  137.8 1.8 fusion.95
  142.7 1.8 fusion.95
  147.6 1.8 fusion.95
  151.3 3.1 %convolution_add_fusion = f32[256,2048]{1,0:T(8,128)} fusion(f32[256,2048]{1,0:T(8,128)S(1)} %copy-done.1, bf16[256,256]{0,1:T(8,128)(2,1)S(1)} %bitcast.53, bf16[2048,1280]{1,0:T(8,128)(2,1)} %bitcast.50), kind=kOutput, calls=%fused_computation.23 | convolution fusion | flops 268959744 | bytes 5373952 | tf_op jit(solution)/shard_map/dot_general | solution.py:370
  156.1 1.1 reshape.277
  157.3 16.6 %all-to-all-start = ((bf16[64,2,2048]{2,1,0:T(2,128)(2,1)}), bf16[64,2,2048]{2,1,0:T(2,128)(2,1)S(1)}, u32[]{:S(2)}, u32[]{:S(2)}) async-start(bf16[64,2,2048]{2,1,0:T(2,128)(2,1)} %reshape.277), calls=%async_computation.1 | async-start | bytes 1048576 | tf_op jit(solution)/shard_map/all_to_all | solution.py:323
  174.8 24.6 %all-to-all-done = bf16[64,2,2048]{2,1,0:T(2,128)(2,1)S(1)} async-done(((bf16[64,2,2048]{2,1,0:T(2,128)(2,1)}), bf16[64,2,2048]{2,1,0:T(2,128)(2,1)S(1)}, u32[]{:S(2)}, u32[]{:S(2)}) %all-to-all-start) | async-done | bytes 524320 | tf_op jit(solution)/shard_map/all_to_all | solution.py:323
  199.9 1.2 reshape.280
  201.1 1.6 add_convert_fusion
  (111 shorter events, 22.0 us)
Async XLA Ops:
  7.2 90.9 %copy-start.7 = (s32[43]{0:T(128)S(1)}, s32[43]{0:T(128)}, u32[]{:S(2)}) copy-start(s32[43]{0:T(128)} %param.21) | copy-start | bytes 520
  7.2 96.5 %copy-start.5 = (f32[3,256]{1,0:T(4,128)S(1)}, f32[3,256]{1,0:T(4,128)}, u32[]{:S(2)}) copy-start(f32[3,256]{1,0:T(4,128)} %param.27) | copy-start | bytes 9220
  7.2 96.5 %copy-start.4 = (bf16[256,2,256]{2,1,0:T(2,128)(2,1)S(1)}, bf16[256,2,256]{2,1,0:T(2,128)(2,1)}, u32[]{:S(2)}) copy-start(bf16[256,2,256]{2,1,0:T(2,128)(2,1)} %param.34) | copy-start | bytes 786436
  7.2 98.7 %all-gather.2.cloned.1.call-start = ((), (), s32[]{:S(2)}) async-start(), calls=%async_computation.2 | async-start | bytes 1179648 | tf_op jit(solution)/shard_map/all_gather | solution.py:257
  7.9 193.2 %reduce-scatter.2.cloned.1.call-start = ((), (), s32[]{:S(2)}) async-start(), calls=%async_computation.3 | async-start | bytes 2359296 | tf_op jit(solution)/shard_map/reduce_scatter | solution.py:374
  97.0 12.1 %copy-start.11 = (f32[2048]{0:T(1024)S(1)}, f32[2048]{0:T(1024)}, u32[]{:S(2)}) copy-start(f32[2048]{0:T(1024)} %param.25) | copy-start | bytes 24580
  97.0 12.1 %copy-start.12 = (f32[2048]{0:T(1024)S(1)}, f32[2048]{0:T(1024)}, u32[]{:S(2)}) copy-start(f32[2048]{0:T(1024)} %param.24) | copy-start | bytes 24580
  105.9 3.2 %copy-start = (bf16[256,2048]{1,0:T(8,128)(2,1)S(1)}, bf16[256,2048]{1,0:T(8,128)(2,1)}, u32[]{:S(2)}) copy-start(bf16[256,2048]{1,0:T(8,128)(2,1)} %all-gather.2.cloned.1.call-done) | copy-start | bytes 3145732
  112.5 6.4 %copy-start.13 = (f32[512]{0:T(512)S(1)}, f32[512]{0:T(512)}, u32[]{:S(2)}) copy-start(f32[512]{0:T(512)} %param.31) | copy-start | bytes 6148
  112.7 12.2 %collective-permute-start = (bf16[512,2,256]{0,2,1:T(8,128)(2,1)S(1)}, bf16[512,2,256]{0,2,1:T(8,128)(2,1)S(1)}, u32[]{:S(2)}, u32[]{:S(2)}) collective-permute-start(bf16[512,2,256]{0,2,1:T(8,128)(2,1)S(1)} %pad_maximum_fusion.1), channel_id=1, source_target_pairs={{0,8},{8,16},{16,24},{24,32},{32,40},{40,48},{48,56},{56,64},{64,7... | collective-permute-start | bytes 1572872 | tf_op jit(solution)/shard_map/ppermute | solution.py:157
  115.3 15.2 %collective-permute-start.1 = (bf16[512,2,256]{0,2,1:T(8,128)(2,1)S(1)}, bf16[512,2,256]{0,2,1:T(8,128)(2,1)S(1)}, u32[]{:S(2)}, u32[]{:S(2)}) collective-permute-start(bf16[512,2,256]{0,2,1:T(8,128)(2,1)S(1)} %pad_maximum_fusion.1), channel_id=1, source_target_pairs={{0,16},{8,24},{16,32},{24,40},{32,48},{40,56},{48,64},{56,72},{64,... | collective-permute-start | bytes 1572872 | tf_op jit(solution)/shard_map/ppermute | solution.py:157
  131.6 19.6 %copy-start.1 = (f32[256,2048]{1,0:T(8,128)S(1)}, f32[256,2048]{1,0:T(8,128)}, u32[]{:S(2)}) copy-start(f32[256,2048]{1,0:T(8,128)} %fusion.29) | copy-start | bytes 6291460
  154.4 0.7 copy-start.6
  155.4 18.9 %copy-start.2 = (bf16[512,2,256]{2,1,0:T(2,128)(2,1)S(1)}, bf16[512,2,256]{2,1,0:T(2,128)(2,1)}, u32[]{:S(2)}) copy-start(bf16[512,2,256]{2,1,0:T(2,128)(2,1)} %param.35) | copy-start | bytes 1572868
  155.8 18.9 %copy-start.10 = (s32[1,128]{1,0:T(1,128)S(1)}, s32[1,128]{1,0:T(1,128)}, u32[]{:S(2)}) copy-start(s32[1,128]{1,0:T(1,128)} %param.23) | copy-start | bytes 1540
  157.3 42.2 %all-to-all-start = ((bf16[64,2,2048]{2,1,0:T(2,128)(2,1)}), bf16[64,2,2048]{2,1,0:T(2,128)(2,1)S(1)}, u32[]{:S(2)}, u32[]{:S(2)}) async-start(bf16[64,2,2048]{2,1,0:T(2,128)(2,1)} %reshape.277), calls=%async_computation.1 | async-start | bytes 1048576 | tf_op jit(solution)/shard_map/all_to_all | solution.py:323
  174.7 26.4 %copy-start.3 = (bf16[256,256]{1,0:T(8,128)(2,1)S(1)}, bf16[256,256]{1,0:T(8,128)(2,1)}, u32[]{:S(2)}) copy-start(bf16[256,256]{1,0:T(8,128)(2,1)} %param.19) | copy-start | bytes 393220
  174.7 26.4 %copy-start.8 = (f32[256]{0:T(256)S(1)}, f32[256]{0:T(256)}, u32[]{:S(2)}) copy-start(f32[256]{0:T(256)} %param.33) | copy-start | bytes 3076
  174.7 26.4 %copy-start.9 = (f32[256]{0:T(256)S(1)}, f32[256]{0:T(256)}, u32[]{:S(2)}) copy-start(f32[256]{0:T(256)} %param.29) | copy-start | bytes 3076
Sparse Core Ops, SparseCore 0:
  10.1 34.7 all-gather.1
  154.5 40.8 reduce-scatter.1

commit v10 on v8

--- a/solution.py
+++ b/solution.py
@@ -274,12 +274,10 @@
     fc1_cols = fc1_weight.shape[1]
     dense_cols = dense_weight.shape[0]
     fc2_cols = fc2_weight.shape[0]
-    first_pack = jnp.concatenate([qkv_local, digits], axis=1)
-    second_pack = jnp.concatenate([fc1_weight, dense_weight.T, fc2_weight.T], axis=1)
-    first_full, second_full = ring_gather(first_pack, second_pack, INNER, req_count // INNER)
-    qkv_full, digits_full = jnp.split(first_full, [3 * head_cols], axis=1)
-    fc1_full, dense_full_t, fc2_full_t = jnp.split(
-        second_full, [fc1_cols, fc1_cols + dense_cols], axis=1
+    second_pack = jnp.concatenate([fc1_weight, dense_weight.T, fc2_weight.T, digits], axis=1)
+    qkv_full, second_full = ring_gather(qkv_local, second_pack, INNER, req_count // INNER)
+    fc1_full, dense_full_t, fc2_full_t, digits_full = jnp.split(
+        second_full, [fc1_cols, fc1_cols + dense_cols, fc1_cols + dense_cols + fc2_cols], axis=1
     )
     digit_table = digits_full.reshape(req_count, weight_rows * digit_cols)[:, : 2 * label_count]
     digit_table = digit_table.astype(jnp.int32)

time: 209 us -> 216 us (1.033)
  Pallas kernels: 83.5 us -> 88.4 us
  waiting for transfers between devices: 37 us -> 41.3 us
  starting transfers between devices: 22.9 us -> 20.4 us
    pallas_call x1, Pallas kernels: 83.5 us -> 88.4 us  [ring_gather(): pl.pallas_call(functools.partial(ring_gather_kernel, inner, outer), out_s...]
    all_to_all x1, waiting for transfers between devices: 26.5 us -> 29.7 us  [shards(): lax.all_to_all(flagged.reshape(req_count, page_cap, page_width + flag_col...]
  transfers between devices with their start and end apart: 5 -> 5, of which waited for: 3 -> 3; matrix products, arithmetic and copies ran while one was open for 9% -> 9% of each run, Pallas kernels for 40% -> 41%
where the time goes in v10:
time: 216 us
  Pallas kernels  88.4 us (41%)
  waiting for transfers between devices  41.3 us (19%)
  starting transfers between devices  20.4 us (9%)
  other arithmetic  20.1 us (9%)
  matrix products  17.7 us (8%)
  between operations  14.6 us (7%)
  local copies, waits for them, and re-layouts  10.3 us (5%)
  loops' own time  2.71 us (1%)
    pallas_call x1, Pallas kernels, ring_gather(): pl.pallas_call(functools.partial(ring_gather_kernel, inner, outer), out_s...  88.4 us
    all_to_all x1, waiting for transfers between devices, shards(): lax.all_to_all(flagged.reshape(req_count, page_cap, page_width + flag_col...  29.7 us
    all_to_all x1, starting transfers between devices, shards(): lax.all_to_all(flagged.reshape(req_count, page_cap, page_width + flag_col...  14.6 us
    ppermute x2, waiting for transfers between devices, from_behind(): lax.ppermute(value, axis, [(source, source + steps) for source in range(l...  10.9 us
    ppermute x2, starting transfers between devices, from_behind(): lax.ppermute(value, axis, [(source, source + steps) for source in range(l...  5.71 us
    dot_general x1, matrix products, shards(): lax.dot_general(hidden, fc2_full_t, contract_rows, preferred_element_type...  5.1 us
  transfers between devices with their start and end apart: 5, of which 3 were waited for; matrix products, arithmetic and copies ran while one was open for 9% of the time, Pallas kernels for 41%

profile of v10, /device:TPU:6, one launch (start us, length us, event | category | flops | bytes accessed | tf_op | source)
XLA Modules:
  0.0 215.6 jit_solution(18126851716725681160)
XLA Ops:
  8.0 1.4 copy.51
  11.0 1.4 pad_maximum_fusion.6.second_block
  12.5 88.4 %shard_map.176 = (bf16[16,4,32,768]{3,2,1,0:T(8,128)(2,1)}, bf16[16,4,32,1408]{3,2,1,0:T(8,128)(2,1)}) custom-call(bf16[32,768]{1,0:T(8,128)(2,1)} %bitcast.51, bf16[32,1408]{1,0:T(8,128)(2,1)} %pad_maximum_fusion.6.second_block), custom_call_target="tpu_custom_call" | custom-call | tf_op jit(solution)/shard_map/pallas_call | solution.py:137
  100.9 1.1 split.16
  104.6 1.8 constant_dynamic-update-slice_fusion.8
  106.5 1.9 constant_dynamic-update-slice_fusion.4
  109.0 1.5 convert_reduce_fusion
  110.5 1.6 fusion.23
  112.2 3.0 %convolution_add_fusion.1 = f32[256,768]{1,0:T(8,128)S(1)} fusion(bf16[2048,768]{1,0:T(8,128)(2,1)} %bitcast.64, f32[768]{0:T(1024)S(1)} %add.197, bf16[256,2048]{1,0:T(8,128)(2,1)S(1)} %copy-done, f32[2048]{0:T(1024)S(1)} %copy-done.9, f32[2048]{0:T(1024)S(1)} %copy-done.11, f32[256]{0:T(256)S(1)} %add_rsqrt_fusion, f32[256]{0:T(256)S(1)} %broadcast_multiply_fusion), kind=kOutput, calls=%fused_computation.37 | convolution fusion | flops 808648704 | bytes 5002240 | tf_op jit(solution)/shard_map/dot_general | solution.py:289
  115.7 4.4 %collective-permute-start.1 = (bf16[512,2,256]{0,2,1:T(8,128)(2,1)S(1)}, bf16[512,2,256]{0,2,1:T(8,128)(2,1)S(1)}, u32[]{:S(2)}, u32[]{:S(2)}) collective-permute-start(bf16[512,2,256]{0,2,1:T(8,128)(2,1)S(1)} %pad_maximum_fusion.2), channel_id=1, source_target_pairs={{0,16},{8,24},{16,32},{24,40},{32,48},{40,56},{48,64},{56,72},{64,... | collective-permute-start | bytes 1572872 | tf_op jit(solution)/shard_map/ppermute | solution.py:157
  120.1 1.3 collective-permute-start
  121.4 1.9 constant_dynamic-update-slice_fusion
  123.4 5.2 %collective-permute-done.1 = bf16[512,2,256]{0,2,1:T(8,128)(2,1)S(1)} collective-permute-done((bf16[512,2,256]{0,2,1:T(8,128)(2,1)S(1)}, bf16[512,2,256]{0,2,1:T(8,128)(2,1)S(1)}, u32[]{:S(2)}, u32[]{:S(2)}) %collective-permute-start.1) | collective-permute-done | bytes 524320 | tf_op jit(solution)/shard_map/ppermute | solution.py:157
  128.7 5.6 %collective-permute-done = bf16[512,2,256]{0,2,1:T(8,128)(2,1)S(1)} collective-permute-done((bf16[512,2,256]{0,2,1:T(8,128)(2,1)S(1)}, bf16[512,2,256]{0,2,1:T(8,128)(2,1)S(1)}, u32[]{:S(2)}, u32[]{:S(2)}) %collective-permute-start) | collective-permute-done | bytes 524320 | tf_op jit(solution)/shard_map/ppermute | solution.py:157
  134.5 15.9 %while.11 = (s32[]{:T(128)}, bf16[4,256,64]{1,2,0:T(8,128)(2,1)S(1)}, s32[4]{0:T(128)S(1)}, bf16[256,256]{0,1:T(8,128)(2,1)S(1)}, bf16[1536,256]{0,1:T(8,128)(2,...) while((s32[]{:T(128)}, ...), condition=%wide.region_25.26_spmd.clone, body=%wide.region_22.25_spmd.clone.sunk | while | flops 112492032 | bytes 5240535 | solution.py:227
  136.7 0.9 fusion.92
  140.6 0.9 fusion.92
  150.4 1.7 fusion.33
  152.2 5.1 %convolution_add_fusion = f32[256,2048]{1,0:T(8,128)} fusion(f32[256,2048]{1,0:T(8,128)S(1)} %fusion.33, bf16[2048,1408]{1,0:T(8,128)(2,1)} %bitcast.50, f32[512]{0:T(512)} %param.31, bf16[256,2048]{1,0:T(8,128)(2,1)S(1)} %copy-done, f32[2048]{0:T(1024)S(1)} %copy-done.10, f32[2048]{0:T(1024)} %param.24, f32[256]{0:T(256)S(1)} %add_rsqrt_fusion, ...), kind=kOutput, calls=%fused_computation.21 | convolution fusion | flops 1078722560 | bytes 9457664 | tf_op jit(solution)/shard_map/dot_general | solution.py:371
  159.4 1.0 reshape.266
  160.4 14.6 %all-to-all-start = ((bf16[64,2,2176]{2,1,0:T(2,128)(2,1)}), bf16[64,2,2176]{2,1,0:T(2,128)(2,1)S(1)}, u32[]{:S(2)}, u32[]{:S(2)}) async-start(bf16[64,2,2176]{2,1,0:T(2,128)(2,1)} %reshape.266), calls=%async_computation.1 | async-start | bytes 1114112 | tf_op jit(solution)/shard_map/all_to_all | solution.py:323
  175.5 29.7 %all-to-all-done = bf16[64,2,2176]{2,1,0:T(2,128)(2,1)S(1)} async-done(((bf16[64,2,2176]{2,1,0:T(2,128)(2,1)}), bf16[64,2,2176]{2,1,0:T(2,128)(2,1)S(1)}, u32[]{:S(2)}, u32[]{:S(2)}) %all-to-all-start) | async-done | bytes 557088 | tf_op jit(solution)/shard_map/all_to_all | solution.py:323
  205.9 1.2 reshape.269
  207.1 1.6 add_convert_fusion
  (106 shorter events, 20.7 us)
Async XLA Ops:
  7.2 95.8 %copy-start.5 = (s32[43]{0:T(128)S(1)}, s32[43]{0:T(128)}, u32[]{:S(2)}) copy-start(s32[43]{0:T(128)} %param.21) | copy-start | bytes 520
  7.2 101.4 %copy-start.3 = (bf16[256,2,256]{2,1,0:T(2,128)(2,1)S(1)}, bf16[256,2,256]{2,1,0:T(2,128)(2,1)}, u32[]{:S(2)}) copy-start(bf16[256,2,256]{2,1,0:T(2,128)(2,1)} %param.34) | copy-start | bytes 786436
  7.2 101.8 %all-gather.2.cloned.1.call-start = ((), (), s32[]{:S(2)}) async-start(), calls=%async_computation.2 | async-start | bytes 1179648 | tf_op jit(solution)/shard_map/all_gather | solution.py:257
  7.9 199.2 %reduce-scatter.2.cloned.1.call-start = ((), (), s32[]{:S(2)}) async-start(), calls=%async_computation.3 | async-start | bytes 2359296 | tf_op jit(solution)/shard_map/reduce_scatter | solution.py:375
  101.9 10.2 %copy-start.9 = (f32[2048]{0:T(1024)S(1)}, f32[2048]{0:T(1024)}, u32[]{:S(2)}) copy-start(f32[2048]{0:T(1024)} %param.25) | copy-start | bytes 24580
  102.0 10.2 %copy-start.11 = (f32[2048]{0:T(1024)S(1)}, f32[2048]{0:T(1024)}, u32[]{:S(2)}) copy-start(f32[2048]{0:T(1024)} %param.24) | copy-start | bytes 24580
  109.0 3.2 %copy-start = (bf16[256,2048]{1,0:T(8,128)(2,1)S(1)}, bf16[256,2048]{1,0:T(8,128)(2,1)}, u32[]{:S(2)}) copy-start(bf16[256,2048]{1,0:T(8,128)(2,1)} %all-gather.2.cloned.1.call-done) | copy-start | bytes 3145732
  115.7 13.0 %collective-permute-start.1 = (bf16[512,2,256]{0,2,1:T(8,128)(2,1)S(1)}, bf16[512,2,256]{0,2,1:T(8,128)(2,1)S(1)}, u32[]{:S(2)}, u32[]{:S(2)}) collective-permute-start(bf16[512,2,256]{0,2,1:T(8,128)(2,1)S(1)} %pad_maximum_fusion.2), channel_id=1, source_target_pairs={{0,16},{8,24},{16,32},{24,40},{32,48},{40,56},{48,64},{56,72},{64,... | collective-permute-start | bytes 1572872 | tf_op jit(solution)/shard_map/ppermute | solution.py:157
  120.1 14.2 %collective-permute-start = (bf16[512,2,256]{0,2,1:T(8,128)(2,1)S(1)}, bf16[512,2,256]{0,2,1:T(8,128)(2,1)S(1)}, u32[]{:S(2)}, u32[]{:S(2)}) collective-permute-start(bf16[512,2,256]{0,2,1:T(8,128)(2,1)S(1)} %pad_maximum_fusion.2), channel_id=1, source_target_pairs={{0,8},{8,16},{16,24},{24,32},{32,40},{40,48},{48,56},{56,64},{64,7... | collective-permute-start | bytes 1572872 | tf_op jit(solution)/shard_map/ppermute | solution.py:157
  150.4 1.7 copy-start.10
  157.3 0.7 copy-start.4
  158.8 16.2 %copy-start.1 = (bf16[512,2,256]{2,1,0:T(2,128)(2,1)S(1)}, bf16[512,2,256]{2,1,0:T(2,128)(2,1)}, u32[]{:S(2)}) copy-start(bf16[512,2,256]{2,1,0:T(2,128)(2,1)} %param.35) | copy-start | bytes 1572868
  159.4 46.1 %copy-start.8 = (s32[1,128]{1,0:T(1,128)S(1)}, s32[1,128]{1,0:T(1,128)}, u32[]{:S(2)}) copy-start(s32[1,128]{1,0:T(1,128)} %param.23) | copy-start | bytes 1540
  160.4 44.8 %all-to-all-start = ((bf16[64,2,2176]{2,1,0:T(2,128)(2,1)}), bf16[64,2,2176]{2,1,0:T(2,128)(2,1)S(1)}, u32[]{:S(2)}, u32[]{:S(2)}) async-start(bf16[64,2,2176]{2,1,0:T(2,128)(2,1)} %reshape.266), calls=%async_computation.1 | async-start | bytes 1114112 | tf_op jit(solution)/shard_map/all_to_all | solution.py:323
  175.4 31.6 %copy-start.2 = (bf16[256,256]{1,0:T(8,128)(2,1)S(1)}, bf16[256,256]{1,0:T(8,128)(2,1)}, u32[]{:S(2)}) copy-start(bf16[256,256]{1,0:T(8,128)(2,1)} %param.19) | copy-start | bytes 393220
  175.4 31.6 %copy-start.6 = (f32[256]{0:T(256)S(1)}, f32[256]{0:T(256)}, u32[]{:S(2)}) copy-start(f32[256]{0:T(256)} %param.33) | copy-start | bytes 3076
  175.5 31.6 %copy-start.7 = (f32[256]{0:T(256)S(1)}, f32[256]{0:T(256)}, u32[]{:S(2)}) copy-start(f32[256]{0:T(256)} %param.29) | copy-start | bytes 3076
Sparse Core Ops, SparseCore 0:
  10.1 34.7 all-gather.1
  157.4 38.8 reduce-scatter.1

commit v11 on v10

--- a/solution.py
+++ b/solution.py
@@ -274,11 +274,13 @@
     fc1_cols = fc1_weight.shape[1]
     dense_cols = dense_weight.shape[0]
     fc2_cols = fc2_weight.shape[0]
-    second_pack = jnp.concatenate([fc1_weight, dense_weight.T, fc2_weight.T, digits], axis=1)
-    qkv_full, second_full = ring_gather(qkv_local, second_pack, INNER, req_count // INNER)
-    fc1_full, dense_full_t, fc2_full_t, digits_full = jnp.split(
-        second_full, [fc1_cols, fc1_cols + dense_cols, fc1_cols + dense_cols + fc2_cols], axis=1
-    )
+    first_pack = jnp.concatenate([qkv_local, digits, dense_weight.T], axis=1)
+    second_pack = jnp.concatenate([fc1_weight, fc2_weight.T], axis=1)
+    first_full, second_full = ring_gather(first_pack, second_pack, INNER, req_count // INNER)
+    qkv_full, digits_full, dense_full_t = jnp.split(
+        first_full, [3 * head_cols, 3 * head_cols + digit_cols], axis=1
+    )
+    fc1_full, fc2_full_t = jnp.split(second_full, [fc1_cols], axis=1)
     digit_table = digits_full.reshape(req_count, weight_rows * digit_cols)[:, : 2 * label_count]
     digit_table = digit_table.astype(jnp.int32)
     starts = jnp.min(

time: 216 us -> 216 us (level)
  waiting for transfers between devices: 41.3 us -> 47.8 us
  Pallas kernels: 88.4 us -> 82.8 us
    pallas_call x1, Pallas kernels: 88.4 us -> 82.8 us  [ring_gather(): pl.pallas_call(functools.partial(ring_gather_kernel, inner, outer), out_s...]
    all_to_all x1, waiting for transfers between devices: 29.7 us -> 33.6 us  [shards(): lax.all_to_all(flagged.reshape(req_count, page_cap, page_width + flag_col...]
    all_to_all x1, starting transfers between devices: 14.6 us -> 11.5 us  [shards(): lax.all_to_all(flagged.reshape(req_count, page_cap, page_width + flag_col...]
    ppermute x2, waiting for transfers between devices: 10.9 us -> 13.6 us  [from_behind(): lax.ppermute(value, axis, [(source, source + steps) for source in range(l...]
  transfers between devices with their start and end apart: 5 -> 5, of which waited for: 3 -> 3; matrix products, arithmetic and copies ran while one was open for 9% -> 9% of each run, Pallas kernels for 41% -> 38%
where the time goes in v11:
time: 216 us
  Pallas kernels  82.8 us (38%)
  waiting for transfers between devices  47.8 us (22%)
  other arithmetic  21.5 us (10%)
  starting transfers between devices  18.6 us (9%)
  matrix products  17.8 us (8%)
  between operations  14.6 us (7%)
  local copies, waits for them, and re-layouts  9.69 us (4%)
  loops' own time  2.71 us (1%)
    pallas_call x1, Pallas kernels, ring_gather(): pl.pallas_call(functools.partial(ring_gather_kernel, inner, outer), out_s...  82.8 us
    all_to_all x1, waiting for transfers between devices, shards(): lax.all_to_all(flagged.reshape(req_count, page_cap, page_width + flag_col...  33.6 us
    ppermute x2, waiting for transfers between devices, from_behind(): lax.ppermute(value, axis, [(source, source + steps) for source in range(l...  13.6 us
    all_to_all x1, starting transfers between devices, shards(): lax.all_to_all(flagged.reshape(req_count, page_cap, page_width + flag_col...  11.5 us
    ppermute x2, starting transfers between devices, from_behind(): lax.ppermute(value, axis, [(source, source + steps) for source in range(l...  7.07 us
    dot_general x1, matrix products, shards(): lax.dot_general(hidden, fc2_full_t, contract_rows, preferred_element_type...  5.12 us
  transfers between devices with their start and end apart: 5, of which 3 were waited for; matrix products, arithmetic and copies ran while one was open for 9% of the time, Pallas kernels for 38%

profile of v11, /device:TPU:6, one launch (start us, length us, event | category | flops | bytes accessed | tf_op | source)
XLA Modules:
  0.0 215.6 jit_solution(1978830012642743023)
XLA Ops:
  10.4 1.4 pad_maximum_fusion.7.second_block
  11.8 1.4 pad_maximum_fusion.6.first_block
  13.2 82.8 %shard_map.176 = (bf16[16,4,32,1152]{3,2,1,0:T(8,128)(2,1)}, bf16[16,4,32,1024]{3,2,1,0:T(8,128)(2,1)}) custom-call(bf16[32,1152]{1,0:T(8,128)(2,1)} %pad_maximum_fusion.6.first_block, bf16[32,1024]{1,0:T(8,128)(2,1)} %pad_maximum_fusion.7.second_block), custom_call_target="tpu_custom_call" | custom-call | tf_op jit(solution)/shard_map/pallas_call | solution.py:137
  96.0 1.1 split.21
  99.7 1.8 constant_dynamic-update-slice_fusion.8
  101.6 1.9 constant_dynamic-update-slice_fusion.4
  104.1 1.5 convert_reduce_fusion
  105.6 1.6 fusion.25
  107.3 3.0 %fusion.32 = f32[256,768]{1,0:T(8,128)S(1)} fusion(bf16[2048,1152]{1,0:T(8,128)(2,1)} %bitcast.48, f32[768]{0:T(1024)S(1)} %add.197, bf16[256,2048]{1,0:T(8,128)(2,1)S(1)} %copy-done, f32[2048]{0:T(1024)S(1)} %copy-done.9, f32[2048]{0:T(1024)S(1)} %copy-done.11, f32[256]{0:T(256)S(1)} %add_rsqrt_fusion, f32[256]{0:T(256)S(1)} %broadcast_multiply_fusion), kind=kOutput, calls=%fused_computation.39 | convolution fusion | flops 808648704 | bytes 5002240 | tf_op jit(solution)/shard_map/dot_general | solution.py:291
  110.8 4.5 %collective-permute-start.1 = (bf16[512,2,256]{0,2,1:T(8,128)(2,1)S(1)}, bf16[512,2,256]{0,2,1:T(8,128)(2,1)S(1)}, u32[]{:S(2)}, u32[]{:S(2)}) collective-permute-start(bf16[512,2,256]{0,2,1:T(8,128)(2,1)S(1)} %pad_maximum_fusion.2), channel_id=1, source_target_pairs={{0,16},{8,24},{16,32},{24,40},{32,48},{40,56},{48,64},{56,72},{64,... | collective-permute-start | bytes 1572872 | tf_op jit(solution)/shard_map/ppermute | solution.py:157
  115.3 2.6 %collective-permute-start = (bf16[512,2,256]{0,2,1:T(8,128)(2,1)S(1)}, bf16[512,2,256]{0,2,1:T(8,128)(2,1)S(1)}, u32[]{:S(2)}, u32[]{:S(2)}) collective-permute-start(bf16[512,2,256]{0,2,1:T(8,128)(2,1)S(1)} %pad_maximum_fusion.2), channel_id=1, source_target_pairs={{0,8},{8,16},{16,24},{24,32},{32,40},{40,48},{48,56},{56,64},{64,7... | collective-permute-start | bytes 1572872 | tf_op jit(solution)/shard_map/ppermute | solution.py:157
  117.9 1.9 constant_dynamic-update-slice_fusion
  119.9 7.7 %collective-permute-done.1 = bf16[512,2,256]{0,2,1:T(8,128)(2,1)S(1)} collective-permute-done((bf16[512,2,256]{0,2,1:T(8,128)(2,1)S(1)}, bf16[512,2,256]{0,2,1:T(8,128)(2,1)S(1)}, u32[]{:S(2)}, u32[]{:S(2)}) %collective-permute-start.1) | collective-permute-done | bytes 524320 | tf_op jit(solution)/shard_map/ppermute | solution.py:157
  127.6 5.8 %collective-permute-done = bf16[512,2,256]{0,2,1:T(8,128)(2,1)S(1)} collective-permute-done((bf16[512,2,256]{0,2,1:T(8,128)(2,1)S(1)}, bf16[512,2,256]{0,2,1:T(8,128)(2,1)S(1)}, u32[]{:S(2)}, u32[]{:S(2)}) %collective-permute-start) | collective-permute-done | bytes 524320 | tf_op jit(solution)/shard_map/ppermute | solution.py:157
  133.7 15.9 %while.11 = (s32[]{:T(128)}, bf16[4,256,64]{1,2,0:T(8,128)(2,1)S(1)}, s32[4]{0:T(128)S(1)}, bf16[256,256]{0,1:T(8,128)(2,1)S(1)}, bf16[1536,256]{0,1:T(8,128)(2,...) while((s32[]{:T(128)}, ...), condition=%wide.region_25.26_spmd.clone, body=%wide.region_22.25_spmd.clone.sunk | while | flops 112492032 | bytes 5240535 | solution.py:227
  139.8 0.9 fusion.96
  143.8 0.9 fusion.96
  149.6 1.7 fusion.38
  151.4 5.1 %convolution_add_fusion = f32[256,2048]{1,0:T(8,128)} fusion(f32[256,2048]{1,0:T(8,128)S(1)} %fusion.38, bf16[2048,1024]{1,0:T(8,128)(2,1)} %bitcast.63, f32[512]{0:T(512)} %param.31, bf16[256,2048]{1,0:T(8,128)(2,1)S(1)} %copy-done, f32[2048]{0:T(1024)S(1)} %copy-done.10, f32[2048]{0:T(1024)} %param.24, f32[256]{0:T(256)S(1)} %add_rsqrt_fusion, ...), kind=kOutput, calls=%fused_computation.23 | convolution fusion | flops 1078722560 | bytes 9457664 | tf_op jit(solution)/shard_map/dot_general | solution.py:373
  158.6 1.0 reshape.266
  159.6 11.5 %all-to-all-start = ((bf16[64,2,2176]{2,1,0:T(2,128)(2,1)}), bf16[64,2,2176]{2,1,0:T(2,128)(2,1)S(1)}, u32[]{:S(2)}, u32[]{:S(2)}) async-start(bf16[64,2,2176]{2,1,0:T(2,128)(2,1)} %reshape.266), calls=%async_computation.1 | async-start | bytes 1114112 | tf_op jit(solution)/shard_map/all_to_all | solution.py:325
  171.6 33.6 %all-to-all-done = bf16[64,2,2176]{2,1,0:T(2,128)(2,1)S(1)} async-done(((bf16[64,2,2176]{2,1,0:T(2,128)(2,1)}), bf16[64,2,2176]{2,1,0:T(2,128)(2,1)S(1)}, u32[]{:S(2)}, u32[]{:S(2)}) %all-to-all-start) | async-done | bytes 557088 | tf_op jit(solution)/shard_map/all_to_all | solution.py:325
  205.9 1.2 reshape.269
  207.1 1.6 add_convert_fusion
  (107 shorter events, 21.5 us)
Async XLA Ops:
  7.2 90.9 %copy-start.5 = (s32[43]{0:T(128)S(1)}, s32[43]{0:T(128)}, u32[]{:S(2)}) copy-start(s32[43]{0:T(128)} %param.21) | copy-start | bytes 520
  7.2 96.5 %copy-start.3 = (bf16[256,2,256]{2,1,0:T(2,128)(2,1)S(1)}, bf16[256,2,256]{2,1,0:T(2,128)(2,1)}, u32[]{:S(2)}) copy-start(bf16[256,2,256]{2,1,0:T(2,128)(2,1)} %param.34) | copy-start | bytes 786436
  7.2 96.9 %all-gather.2.cloned.1.call-start = ((), (), s32[]{:S(2)}) async-start(), calls=%async_computation.2 | async-start | bytes 1179648 | tf_op jit(solution)/shard_map/all_gather | solution.py:257
  7.9 199.1 %reduce-scatter.2.cloned.1.call-start = ((), (), s32[]{:S(2)}) async-start(), calls=%async_computation.3 | async-start | bytes 2359296 | tf_op jit(solution)/shard_map/reduce_scatter | solution.py:377
  97.1 10.2 %copy-start.9 = (f32[2048]{0:T(1024)S(1)}, f32[2048]{0:T(1024)}, u32[]{:S(2)}) copy-start(f32[2048]{0:T(1024)} %param.25) | copy-start | bytes 24580
  97.1 10.2 %copy-start.11 = (f32[2048]{0:T(1024)S(1)}, f32[2048]{0:T(1024)}, u32[]{:S(2)}) copy-start(f32[2048]{0:T(1024)} %param.24) | copy-start | bytes 24580
  104.1 3.2 %copy-start = (bf16[256,2048]{1,0:T(8,128)(2,1)S(1)}, bf16[256,2048]{1,0:T(8,128)(2,1)}, u32[]{:S(2)}) copy-start(bf16[256,2048]{1,0:T(8,128)(2,1)} %all-gather.2.cloned.1.call-done) | copy-start | bytes 3145732
  110.8 16.8 %collective-permute-start.1 = (bf16[512,2,256]{0,2,1:T(8,128)(2,1)S(1)}, bf16[512,2,256]{0,2,1:T(8,128)(2,1)S(1)}, u32[]{:S(2)}, u32[]{:S(2)}) collective-permute-start(bf16[512,2,256]{0,2,1:T(8,128)(2,1)S(1)} %pad_maximum_fusion.2), channel_id=1, source_target_pairs={{0,16},{8,24},{16,32},{24,40},{32,48},{40,56},{48,64},{56,72},{64,... | collective-permute-start | bytes 1572872 | tf_op jit(solution)/shard_map/ppermute | solution.py:157
  115.3 18.2 %collective-permute-start = (bf16[512,2,256]{0,2,1:T(8,128)(2,1)S(1)}, bf16[512,2,256]{0,2,1:T(8,128)(2,1)S(1)}, u32[]{:S(2)}, u32[]{:S(2)}) collective-permute-start(bf16[512,2,256]{0,2,1:T(8,128)(2,1)S(1)} %pad_maximum_fusion.2), channel_id=1, source_target_pairs={{0,8},{8,16},{16,24},{24,32},{32,40},{40,48},{48,56},{56,64},{64,7... | collective-permute-start | bytes 1572872 | tf_op jit(solution)/shard_map/ppermute | solution.py:157
  149.6 1.7 copy-start.10
  156.5 0.7 copy-start.4
  158.0 13.1 %copy-start.1 = (bf16[512,2,256]{2,1,0:T(2,128)(2,1)S(1)}, bf16[512,2,256]{2,1,0:T(2,128)(2,1)}, u32[]{:S(2)}) copy-start(bf16[512,2,256]{2,1,0:T(2,128)(2,1)} %param.35) | copy-start | bytes 1572868
  158.6 46.9 %copy-start.8 = (s32[1,128]{1,0:T(1,128)S(1)}, s32[1,128]{1,0:T(1,128)}, u32[]{:S(2)}) copy-start(s32[1,128]{1,0:T(1,128)} %param.23) | copy-start | bytes 1540
  159.6 45.5 %all-to-all-start = ((bf16[64,2,2176]{2,1,0:T(2,128)(2,1)}), bf16[64,2,2176]{2,1,0:T(2,128)(2,1)S(1)}, u32[]{:S(2)}, u32[]{:S(2)}) async-start(bf16[64,2,2176]{2,1,0:T(2,128)(2,1)} %reshape.266), calls=%async_computation.1 | async-start | bytes 1114112 | tf_op jit(solution)/shard_map/all_to_all | solution.py:325
  171.5 35.5 %copy-start.2 = (bf16[256,256]{1,0:T(8,128)(2,1)S(1)}, bf16[256,256]{1,0:T(8,128)(2,1)}, u32[]{:S(2)}) copy-start(bf16[256,256]{1,0:T(8,128)(2,1)} %param.19) | copy-start | bytes 393220
  171.5 35.5 %copy-start.6 = (f32[256]{0:T(256)S(1)}, f32[256]{0:T(256)}, u32[]{:S(2)}) copy-start(f32[256]{0:T(256)} %param.33) | copy-start | bytes 3076
  171.6 35.5 %copy-start.7 = (f32[256]{0:T(256)S(1)}, f32[256]{0:T(256)}, u32[]{:S(2)}) copy-start(f32[256]{0:T(256)} %param.29) | copy-start | bytes 3076
Sparse Core Ops, SparseCore 0:
  10.1 34.7 all-gather.1
  156.6 35.5 reduce-scatter.1

commit v12 on v9

--- a/solution.py
+++ b/solution.py
@@ -360,15 +360,14 @@
         (position[:, None] - key_position[None, :] < WINDOW) | (key_position[None, :] < SINKS)
     )
     all_keys = jnp.concatenate(blocks, axis=0)
+    attended = head_attention(queries, all_keys[:, 0, :], all_keys[:, 1, :], allowed)
     hidden = jax.nn.gelu(lifted + fc1_bias, approximate=True).astype(jnp.bfloat16)
-    mlp_part = lax.dot_general(
-        hidden, fc2_full_t, (((1,), (1,)), ((), ())), preferred_element_type=jnp.float32
-    )
-    queries, mlp_part = lax.optimization_barrier((queries, mlp_part))
-    attended = head_attention(queries, all_keys[:, 0, :], all_keys[:, 1, :], allowed)
     contract_rows = (((1,), (1,)), ((), ()))
     attn_part = lax.dot_general(
         attended, dense_full_t, contract_rows, preferred_element_type=jnp.float32
+    )
+    mlp_part = lax.dot_general(
+        hidden, fc2_full_t, contract_rows, preferred_element_type=jnp.float32
     )
     branches = attn_part + mlp_part
     summed = lax.psum_scatter(branches, "tensor", scatter_dimension=1, tiled=True)

time: 210 us -> 208 us (level)
  matrix products: 22.7 us -> 17.7 us
  waiting for transfers between devices: 31.8 us -> 35.1 us
    dot_general x4, matrix products: 7.29 us -> 3.58 us  [one_head(): lax.dot_general(query_cols, key_cols, (((1,), (1,)), ((), ())), preferred...]
    ppermute x2, waiting for transfers between devices: 6.49 us -> 9.81 us  [from_behind(): lax.ppermute(value, axis, [(source, source + steps) for source in range(l...]
  transfers between devices with their start and end apart: 5 -> 5, of which waited for: 3 -> 3; matrix products, arithmetic and copies ran while one was open for 11% -> 9% of each run, Pallas kernels for 40% -> 40%
where the time goes in v12:
time: 208 us
  Pallas kernels  83.5 us (40%)
  waiting for transfers between devices  35.1 us (17%)
  starting transfers between devices  22.8 us (11%)
  other arithmetic  21.3 us (10%)
  matrix products  17.7 us (9%)
  between operations  14.7 us (7%)
  local copies, waits for them, and re-layouts  9.83 us (5%)
  loops' own time  2.7 us (1%)
    pallas_call x1, Pallas kernels, ring_gather(): pl.pallas_call(functools.partial(ring_gather_kernel, inner, outer), out_s...  83.5 us
    all_to_all x1, waiting for transfers between devices, shards(): lax.all_to_all(outgoing.reshape(req_count, page_cap, page_width), 'req',...  24.6 us
    all_to_all x1, starting transfers between devices, shards(): lax.all_to_all(outgoing.reshape(req_count, page_cap, page_width), 'req',...  16.6 us
    ppermute x2, waiting for transfers between devices, from_behind(): lax.ppermute(value, axis, [(source, source + steps) for source in range(l...  9.81 us
    ppermute x2, starting transfers between devices, from_behind(): lax.ppermute(value, axis, [(source, source + steps) for source in range(l...  6.18 us
    dot_general x1, matrix products, shards(): lax.dot_general(hidden, fc2_full_t, contract_rows, preferred_element_type...  5.11 us
  transfers between devices with their start and end apart: 5, of which 3 were waited for; matrix products, arithmetic and copies ran while one was open for 9% of the time, Pallas kernels for 40%

profile of v12, /device:TPU:6, one launch (start us, length us, event | category | flops | bytes accessed | tf_op | source)
XLA Modules:
  0.0 207.6 jit_solution(5660238287696601496)
XLA Ops:
  11.0 1.4 pad_maximum_fusion.5.second_block
  12.5 83.5 %shard_map.176 = (bf16[16,4,32,896]{3,2,1,0:T(8,128)(2,1)}, bf16[16,4,32,1280]{3,2,1,0:T(8,128)(2,1)}) custom-call(bf16[32,896]{1,0:T(8,128)(2,1)} %pad_maximum_fusion.6.first_block, bf16[32,1280]{1,0:T(8,128)(2,1)} %pad_maximum_fusion.5.second_block), custom_call_target="tpu_custom_call" | custom-call | tf_op jit(solution)/shard_map/pallas_call | solution.py:137
  96.0 1.1 split.21
  99.6 1.9 constant_dynamic-update-slice_fusion.8
  101.5 1.9 constant_dynamic-update-slice_fusion.4
  104.1 1.5 convert_reduce_fusion
  105.6 1.6 fusion.25
  107.3 3.0 %fusion.32 = f32[256,768]{1,0:T(8,128)S(1)} fusion(bf16[2048,896]{1,0:T(8,128)(2,1)} %bitcast.55, f32[768]{0:T(1024)S(1)} %add.197, bf16[256,2048]{1,0:T(8,128)(2,1)S(1)} %copy-done, f32[2048]{0:T(1024)S(1)} %copy-done.11, f32[2048]{0:T(1024)S(1)} %copy-done.12, f32[256]{0:T(256)S(1)} %add_rsqrt_fusion, f32[256]{0:T(256)S(1)} %broadcast_multiply_fusion), kind=kOutput, calls=%fused_computation.39 | convolution fusion | flops 808648704 | bytes 5002240 | tf_op jit(solution)/shard_map/dot_general | solution.py:296
  110.8 2.6 %collective-permute-start = (bf16[512,2,256]{0,2,1:T(8,128)(2,1)S(1)}, bf16[512,2,256]{0,2,1:T(8,128)(2,1)S(1)}, u32[]{:S(2)}, u32[]{:S(2)}) collective-permute-start(bf16[512,2,256]{0,2,1:T(8,128)(2,1)S(1)} %pad_maximum_fusion.1), channel_id=1, source_target_pairs={{0,8},{8,16},{16,24},{24,32},{32,40},{40,48},{48,56},{56,64},{64,7... | collective-permute-start | bytes 1572872 | tf_op jit(solution)/shard_map/ppermute | solution.py:157
  113.5 3.5 %collective-permute-start.1 = (bf16[512,2,256]{0,2,1:T(8,128)(2,1)S(1)}, bf16[512,2,256]{0,2,1:T(8,128)(2,1)S(1)}, u32[]{:S(2)}, u32[]{:S(2)}) collective-permute-start(bf16[512,2,256]{0,2,1:T(8,128)(2,1)S(1)} %pad_maximum_fusion.1), channel_id=1, source_target_pairs={{0,16},{8,24},{16,32},{24,40},{32,48},{40,56},{48,64},{56,72},{64,... | collective-permute-start | bytes 1572872 | tf_op jit(solution)/shard_map/ppermute | solution.py:157
  117.0 1.8 constant_dynamic-update-slice_fusion
  118.8 4.2 %collective-permute-done = bf16[512,2,256]{0,2,1:T(8,128)(2,1)S(1)} collective-permute-done((bf16[512,2,256]{0,2,1:T(8,128)(2,1)S(1)}, bf16[512,2,256]{0,2,1:T(8,128)(2,1)S(1)}, u32[]{:S(2)}, u32[]{:S(2)}) %collective-permute-start) | collective-permute-done | bytes 524320 | tf_op jit(solution)/shard_map/ppermute | solution.py:157
  123.0 5.6 %collective-permute-done.1 = bf16[512,2,256]{0,2,1:T(8,128)(2,1)S(1)} collective-permute-done((bf16[512,2,256]{0,2,1:T(8,128)(2,1)S(1)}, bf16[512,2,256]{0,2,1:T(8,128)(2,1)S(1)}, u32[]{:S(2)}, u32[]{:S(2)}) %collective-permute-start.1) | collective-permute-done | bytes 524320 | tf_op jit(solution)/shard_map/ppermute | solution.py:157
  128.9 15.9 %while.11 = (s32[]{:T(128)}, bf16[4,256,64]{1,2,0:T(8,128)(2,1)S(1)}, s32[4]{0:T(128)S(1)}, bf16[256,256]{0,1:T(8,128)(2,1)S(1)}, bf16[1536,256]{0,1:T(8,128)(2,...) while((s32[]{:T(128)}, ...), condition=%wide.region_25.26_spmd.clone, body=%wide.region_22.25_spmd.clone.sunk | while | flops 112492032 | bytes 5240527 | solution.py:227
  131.0 0.9 fusion.96
  135.0 0.9 fusion.96
  139.0 0.9 fusion.96
  145.5 1.8 fusion.38
  147.3 5.1 %convolution_add_fusion = f32[256,2048]{1,0:T(8,128)} fusion(f32[256,2048]{1,0:T(8,128)S(1)} %fusion.38, bf16[2048,1280]{1,0:T(8,128)(2,1)} %bitcast.50, f32[512]{0:T(512)S(1)} %copy-done.13, bf16[256,2048]{1,0:T(8,128)(2,1)S(1)} %copy-done, f32[2048]{0:T(1024)S(1)} %copy-done.11, f32[2048]{0:T(1024)S(1)} %copy-done.12, f32[256]{0:T(256)S(1)} %add_rsqrt_fusion, ...), kind=kOutput, calls=%fused_computation.23 | convolution fusion | flops 1078722560 | bytes 9457664 | tf_op jit(solution)/shard_map/dot_general | solution.py:369
  154.1 1.1 reshape.277
  155.3 16.6 %all-to-all-start = ((bf16[64,2,2048]{2,1,0:T(2,128)(2,1)}), bf16[64,2,2048]{2,1,0:T(2,128)(2,1)S(1)}, u32[]{:S(2)}, u32[]{:S(2)}) async-start(bf16[64,2,2048]{2,1,0:T(2,128)(2,1)} %reshape.277), calls=%async_computation.1 | async-start | bytes 1048576 | tf_op jit(solution)/shard_map/all_to_all | solution.py:323
  172.8 24.6 %all-to-all-done = bf16[64,2,2048]{2,1,0:T(2,128)(2,1)S(1)} async-done(((bf16[64,2,2048]{2,1,0:T(2,128)(2,1)}), bf16[64,2,2048]{2,1,0:T(2,128)(2,1)S(1)}, u32[]{:S(2)}, u32[]{:S(2)}) %all-to-all-start) | async-done | bytes 524320 | tf_op jit(solution)/shard_map/all_to_all | solution.py:323
  197.9 1.2 reshape.280
  199.1 1.6 add_convert_fusion
  (111 shorter events, 21.7 us)
Async XLA Ops:
  7.2 90.9 %copy-start.7 = (s32[43]{0:T(128)S(1)}, s32[43]{0:T(128)}, u32[]{:S(2)}) copy-start(s32[43]{0:T(128)} %param.21) | copy-start | bytes 520
  7.2 96.5 %copy-start.5 = (f32[3,256]{1,0:T(4,128)S(1)}, f32[3,256]{1,0:T(4,128)}, u32[]{:S(2)}) copy-start(f32[3,256]{1,0:T(4,128)} %param.27) | copy-start | bytes 9220
  7.2 96.5 %copy-start.3 = (bf16[256,2,256]{2,1,0:T(2,128)(2,1)S(1)}, bf16[256,2,256]{2,1,0:T(2,128)(2,1)}, u32[]{:S(2)}) copy-start(bf16[256,2,256]{2,1,0:T(2,128)(2,1)} %param.34) | copy-start | bytes 786436
  7.2 96.9 %all-gather.2.cloned.1.call-start = ((), (), s32[]{:S(2)}) async-start(), calls=%async_computation.2 | async-start | bytes 1179648 | tf_op jit(solution)/shard_map/all_gather | solution.py:257
  7.9 191.2 %reduce-scatter.2.cloned.1.call-start = ((), (), s32[]{:S(2)}) async-start(), calls=%async_computation.3 | async-start | bytes 2359296 | tf_op jit(solution)/shard_map/reduce_scatter | solution.py:373
  97.0 10.2 %copy-start.11 = (f32[2048]{0:T(1024)S(1)}, f32[2048]{0:T(1024)}, u32[]{:S(2)}) copy-start(f32[2048]{0:T(1024)} %param.25) | copy-start | bytes 24580
  97.0 10.2 %copy-start.12 = (f32[2048]{0:T(1024)S(1)}, f32[2048]{0:T(1024)}, u32[]{:S(2)}) copy-start(f32[2048]{0:T(1024)} %param.24) | copy-start | bytes 24580
  104.1 3.2 %copy-start = (bf16[256,2048]{1,0:T(8,128)(2,1)S(1)}, bf16[256,2048]{1,0:T(8,128)(2,1)}, u32[]{:S(2)}) copy-start(bf16[256,2048]{1,0:T(8,128)(2,1)} %all-gather.2.cloned.1.call-done) | copy-start | bytes 3145732
  110.8 12.2 %collective-permute-start = (bf16[512,2,256]{0,2,1:T(8,128)(2,1)S(1)}, bf16[512,2,256]{0,2,1:T(8,128)(2,1)S(1)}, u32[]{:S(2)}, u32[]{:S(2)}) collective-permute-start(bf16[512,2,256]{0,2,1:T(8,128)(2,1)S(1)} %pad_maximum_fusion.1), channel_id=1, source_target_pairs={{0,8},{8,16},{16,24},{24,32},{32,40},{40,48},{48,56},{56,64},{64,7... | collective-permute-start | bytes 1572872 | tf_op jit(solution)/shard_map/ppermute | solution.py:157
  113.5 15.2 %collective-permute-start.1 = (bf16[512,2,256]{0,2,1:T(8,128)(2,1)S(1)}, bf16[512,2,256]{0,2,1:T(8,128)(2,1)S(1)}, u32[]{:S(2)}, u32[]{:S(2)}) collective-permute-start(bf16[512,2,256]{0,2,1:T(8,128)(2,1)S(1)} %pad_maximum_fusion.1), channel_id=1, source_target_pairs={{0,16},{8,24},{16,32},{24,40},{32,48},{40,56},{48,64},{56,72},{64,... | collective-permute-start | bytes 1572872 | tf_op jit(solution)/shard_map/ppermute | solution.py:157
  144.8 0.7 copy-start.4
  144.8 2.4 %copy-start.13 = (f32[512]{0:T(512)S(1)}, f32[512]{0:T(512)}, u32[]{:S(2)}) copy-start(f32[512]{0:T(512)} %param.31) | copy-start | bytes 6148
  152.4 0.7 copy-start.6
  153.4 18.8 %copy-start.1 = (bf16[512,2,256]{2,1,0:T(2,128)(2,1)S(1)}, bf16[512,2,256]{2,1,0:T(2,128)(2,1)}, u32[]{:S(2)}) copy-start(bf16[512,2,256]{2,1,0:T(2,128)(2,1)} %param.35) | copy-start | bytes 1572868
  153.8 18.9 %copy-start.10 = (s32[1,128]{1,0:T(1,128)S(1)}, s32[1,128]{1,0:T(1,128)}, u32[]{:S(2)}) copy-start(s32[1,128]{1,0:T(1,128)} %param.23) | copy-start | bytes 1540
  155.3 42.1 %all-to-all-start = ((bf16[64,2,2048]{2,1,0:T(2,128)(2,1)}), bf16[64,2,2048]{2,1,0:T(2,128)(2,1)S(1)}, u32[]{:S(2)}, u32[]{:S(2)}) async-start(bf16[64,2,2048]{2,1,0:T(2,128)(2,1)} %reshape.277), calls=%async_computation.1 | async-start | bytes 1048576 | tf_op jit(solution)/shard_map/all_to_all | solution.py:323
  172.7 26.4 %copy-start.2 = (bf16[256,256]{1,0:T(8,128)(2,1)S(1)}, bf16[256,256]{1,0:T(8,128)(2,1)}, u32[]{:S(2)}) copy-start(bf16[256,256]{1,0:T(8,128)(2,1)} %param.19) | copy-start | bytes 393220
  172.7 26.4 %copy-start.8 = (f32[256]{0:T(256)S(1)}, f32[256]{0:T(256)}, u32[]{:S(2)}) copy-start(f32[256]{0:T(256)} %param.33) | copy-start | bytes 3076
  172.7 26.4 %copy-start.9 = (f32[256]{0:T(256)S(1)}, f32[256]{0:T(256)}, u32[]{:S(2)}) copy-start(f32[256]{0:T(256)} %param.29) | copy-start | bytes 3076
Sparse Core Ops, SparseCore 0:
  10.1 34.7 all-gather.1
  152.5 40.8 reduce-scatter.1

commit v13 on v12

--- a/solution.py
+++ b/solution.py
@@ -342,7 +342,15 @@
     local_keys = jnp.concatenate([key_value, prefix_cache], axis=0)
     blocks = [local_keys]
     for shift_by in range(1, SPAN + 1):
-        blocks.append(from_behind(local_keys, "req", shift_by))
+        blocks.append(
+            jnp.concatenate(
+                [
+                    from_behind(key_value, "req", shift_by),
+                    from_behind(prefix_cache, "req", shift_by),
+                ],
+                axis=0,
+            )
+        )
     key_segs = []
     key_poss = []
     for step_back in range(SPAN + 1):

time: 208 us -> 218 us (1.048)
  waiting for transfers between devices: 35.1 us -> 26.5 us
  matrix products: 17.7 us -> 25.1 us
  starting transfers between devices: 22.8 us -> 29.7 us
  local copies, waits for them, and re-layouts: 9.83 us -> 15 us
    ppermute x2 -> x4, starting transfers between devices: 6.18 us -> 14.6 us  [from_behind(): lax.ppermute(value, axis, [(source, source + steps) for source in range(l...]
    ppermute x2 -> x4, waiting for transfers between devices: 9.81 us -> 1.83 us  [from_behind(): lax.ppermute(value, axis, [(source, source + steps) for source in range(l...]
    dot_general x4, matrix products: 3.58 us -> 7.28 us  [one_head(): lax.dot_general(query_cols, key_cols, (((1,), (1,)), ((), ())), preferred...]
    dot_general x4, matrix products: 3.62 us -> 7.3 us  [one_head(): jnp.dot(expo.astype(jnp.bfloat16), value_cols, preferred_element_type=jnp...]
    unnamed x31 -> x57, local copies, waits for them, and re-layouts: 1.52 us -> 4.49 us
  transfers between devices with their start and end apart: 5 -> 7, of which waited for: 3 -> 2; matrix products, arithmetic and copies ran while one was open for 9% -> 12% of each run, Pallas kernels for 40% -> 38%
where the time goes in v13:
time: 218 us; the launch traced here: 217 us
  Pallas kernels  82.6 us (38%)
  starting transfers between devices  29.7 us (14%)
  waiting for transfers between devices  26.5 us (12%)
  matrix products  25.1 us (12%)
  other arithmetic  20.5 us (9%)
  local copies, waits for them, and re-layouts  15 us (7%)
  between operations  14.8 us (7%)
  loops' own time  2.71 us (1%)
    pallas_call x1, Pallas kernels, ring_gather(): pl.pallas_call(functools.partial(ring_gather_kernel, inner, outer), out_s...  82.6 us
    all_to_all x1, waiting for transfers between devices, shards(): lax.all_to_all(outgoing.reshape(req_count, page_cap, page_width), 'req',...  24.6 us
    all_to_all x1, starting transfers between devices, shards(): lax.all_to_all(outgoing.reshape(req_count, page_cap, page_width), 'req',...  15 us
    ppermute x4, starting transfers between devices, from_behind(): lax.ppermute(value, axis, [(source, source + steps) for source in range(l...  14.6 us
    dot_general x4, matrix products, one_head(): jnp.dot(expo.astype(jnp.bfloat16), value_cols, preferred_element_type=jnp...  7.3 us
    dot_general x4, matrix products, one_head(): lax.dot_general(query_cols, key_cols, (((1,), (1,)), ((), ())), preferred...  7.28 us
    dot_general x1, matrix products, shards(): lax.dot_general(hidden, fc2_full_t, contract_rows, preferred_element_type...  5.1 us
    unnamed x57, local copies, waits for them, and re-layouts  4.49 us
  transfers between devices with their start and end apart: 7, of which 2 were waited for; matrix products, arithmetic and copies ran while one was open for 12% of the time, Pallas kernels for 38%

profile of v13, /device:TPU:6, one launch (start us, length us, event | category | flops | bytes accessed | tf_op | source)
XLA Modules:
  0.0 216.9 jit_solution(11043574446608574069)
XLA Ops:
  8.3 4.2 %collective-permute-start.1 = (bf16[256,2,256]{0,2,1:T(8,128)(2,1)S(1)}, bf16[256,2,256]{0,2,1:T(8,128)(2,1)}, u32[]{:S(2)}, u32[]{:S(2)}) collective-permute-start(bf16[256,2,256]{0,2,1:T(8,128)(2,1)S(1)} %copy.37), channel_id=1, source_target_pairs={{0,8},{8,16},{16,24},{24,32},{32,40},{40,48},{48,56},{56,64},{64,7... | collective-permute-start | bytes 786440 | tf_op jit(solution)/shard_map/ppermute | solution.py:157
  12.5 4.8 %collective-permute-start.3 = (bf16[256,2,256]{0,2,1:T(8,128)(2,1)S(1)}, bf16[256,2,256]{0,2,1:T(8,128)(2,1)}, u32[]{:S(2)}, u32[]{:S(2)}) collective-permute-start(bf16[256,2,256]{0,2,1:T(8,128)(2,1)S(1)} %copy.37), channel_id=1, source_target_pairs={{0,16},{8,24},{16,32},{24,40},{32,48},{40,56},{48,64},{56,72},{64,... | collective-permute-start | bytes 786440 | tf_op jit(solution)/shard_map/ppermute | solution.py:157
  21.9 82.6 %shard_map.176 = (bf16[16,4,32,896]{3,2,1,0:T(8,128)(2,1)}, bf16[16,4,32,1280]{3,2,1,0:T(8,128)(2,1)}) custom-call(bf16[32,896]{1,0:T(8,128)(2,1)} %pad_maximum_fusion.4.first_block, bf16[32,1280]{1,0:T(8,128)(2,1)} %pad_maximum_fusion.3.second_block), custom_call_target="tpu_custom_call" | custom-call | tf_op jit(solution)/shard_map/pallas_call | solution.py:137
  108.2 1.8 constant_dynamic-update-slice_fusion.16
  110.1 1.8 constant_dynamic-update-slice_fusion.12
  115.0 3.0 %fusion.32 = f32[256,768]{1,0:T(8,128)S(1)} fusion(bf16[2048,896]{1,0:T(8,128)(2,1)} %bitcast.51, f32[768]{0:T(1024)S(1)} %add.197, bf16[256,2048]{1,0:T(8,128)(2,1)S(1)} %copy-done, f32[2048]{0:T(1024)S(1)} %copy-done.20, f32[2048]{0:T(1024)S(1)} %copy-done.22, f32[256]{0:T(256)S(1)} %add_rsqrt_fusion, f32[256]{0:T(256)S(1)} %broadcast_multiply_fusion), kind=kOutput, calls=%fused_computation.38 | convolution fusion | flops 808648704 | bytes 5002240 | tf_op jit(solution)/shard_map/dot_general | solution.py:296
  118.5 2.0 collective-permute-start
  120.5 1.9 constant_dynamic-update-slice_fusion.8
  122.4 3.6 %collective-permute-start.2 = (bf16[256,2,256]{0,2,1:T(8,128)(2,1)S(1)}, bf16[256,2,256]{0,2,1:T(8,128)(2,1)S(1)}, u32[]{:S(2)}, u32[]{:S(2)}) collective-permute-start(bf16[256,2,256]{0,2,1:T(8,128)(2,1)S(1)} %get-tuple-element.161), channel_id=1, source_target_pairs={{0,16},{8,24},{16,32},{24,40},{32,48},{40,56},{48,64},{56,72},{64,... | collective-permute-start | bytes 786440 | tf_op jit(solution)/shard_map/ppermute | solution.py:157
  128.1 1.8 collective-permute-done.2
  132.3 23.3 %while.11 = (s32[]{:T(128)}, bf16[4,256,64]{1,2,0:T(8,128)(2,1)S(1)}, s32[4]{0:T(128)S(1)}, bf16[256,256]{0,1:T(8,128)(2,1)S(1)}, bf16[1536,256]{0,1:T(8,128)(2,...) while((s32[]{:T(128)}, ...), condition=%wide.region_25.26_spmd.clone, body=%wide.region_22.25_spmd.clone.sunk | while | flops 112492032 | bytes 5241035 | solution.py:227
  133.6 1.8 fusion.95
  136.3 1.8 fusion.97
  139.4 1.8 fusion.95
  142.1 1.8 fusion.97
  145.2 1.8 fusion.95
  148.0 1.8 fusion.97
  151.1 1.8 fusion.95
  153.8 1.8 fusion.97
  156.3 1.8 fusion.38
  158.2 5.1 %convolution_add_fusion = f32[256,2048]{1,0:T(8,128)} fusion(f32[256,2048]{1,0:T(8,128)S(1)} %fusion.38, bf16[2048,1280]{1,0:T(8,128)(2,1)} %bitcast.46, f32[512]{0:T(512)S(1)} %copy-done.24, bf16[256,2048]{1,0:T(8,128)(2,1)S(1)} %copy-done, f32[2048]{0:T(1024)S(1)} %copy-done.21, f32[2048]{0:T(1024)S(1)} %copy-done.23, f32[256]{0:T(256)S(1)} %copy-done.18, ...), kind=kOutput, calls=%fused_computation.23 | convolution fusion | flops 1078722560 | bytes 9457664 | tf_op jit(solution)/shard_map/dot_general | solution.py:377
  166.1 15.0 %all-to-all-start = ((bf16[64,2,2048]{2,1,0:T(2,128)(2,1)}), bf16[64,2,2048]{2,1,0:T(2,128)(2,1)S(1)}, u32[]{:S(2)}, u32[]{:S(2)}) async-start(bf16[64,2,2048]{2,1,0:T(2,128)(2,1)} %reshape.277), calls=%async_computation.1 | async-start | bytes 1048576 | tf_op jit(solution)/shard_map/all_to_all | solution.py:323
  182.0 24.6 %all-to-all-done = bf16[64,2,2048]{2,1,0:T(2,128)(2,1)S(1)} async-done(((bf16[64,2,2048]{2,1,0:T(2,128)(2,1)}), bf16[64,2,2048]{2,1,0:T(2,128)(2,1)S(1)}, u32[]{:S(2)}, u32[]{:S(2)}) %all-to-all-start) | async-done | bytes 524320 | tf_op jit(solution)/shard_map/all_to_all | solution.py:323
  208.4 1.6 add_convert_fusion
  (140 shorter events, 29.0 us)
Async XLA Ops:
  7.2 105.8 %all-gather.2.cloned.1.call-start = ((), (), s32[]{:S(2)}) async-start(), calls=%async_computation.2 | async-start | bytes 1179648 | tf_op jit(solution)/shard_map/all_gather | solution.py:257
  8.3 98.4 %copy-start.14 = (s32[43]{0:T(128)S(1)}, s32[43]{0:T(128)}, u32[]{:S(2)}) copy-start(s32[43]{0:T(128)} %param.21) | copy-start | bytes 520
  8.3 103.8 %copy-start.10 = (f32[3,256]{1,0:T(4,128)S(1)}, f32[3,256]{1,0:T(4,128)}, u32[]{:S(2)}) copy-start(f32[3,256]{1,0:T(4,128)} %param.27) | copy-start | bytes 9220
  8.3 118.8 %collective-permute-start.1 = (bf16[256,2,256]{0,2,1:T(8,128)(2,1)S(1)}, bf16[256,2,256]{0,2,1:T(8,128)(2,1)}, u32[]{:S(2)}, u32[]{:S(2)}) collective-permute-start(bf16[256,2,256]{0,2,1:T(8,128)(2,1)S(1)} %copy.37), channel_id=1, source_target_pairs={{0,8},{8,16},{16,24},{24,32},{32,40},{40,48},{48,56},{56,64},{64,7... | collective-permute-start | bytes 786440 | tf_op jit(solution)/shard_map/ppermute | solution.py:157
  12.5 117.4 %collective-permute-start.3 = (bf16[256,2,256]{0,2,1:T(8,128)(2,1)S(1)}, bf16[256,2,256]{0,2,1:T(8,128)(2,1)}, u32[]{:S(2)}, u32[]{:S(2)}) collective-permute-start(bf16[256,2,256]{0,2,1:T(8,128)(2,1)S(1)} %copy.37), channel_id=1, source_target_pairs={{0,16},{8,24},{16,32},{24,40},{32,48},{40,56},{48,64},{56,72},{64,... | collective-permute-start | bytes 786440 | tf_op jit(solution)/shard_map/ppermute | solution.py:157
  17.4 191.0 %reduce-scatter.2.cloned.1.call-start = ((), (), s32[]{:S(2)}) async-start(), calls=%async_computation.3 | async-start | bytes 2359296 | tf_op jit(solution)/shard_map/reduce_scatter | solution.py:381
  105.6 9.3 %copy-start.20 = (f32[2048]{0:T(1024)S(1)}, f32[2048]{0:T(1024)}, u32[]{:S(2)}) copy-start(f32[2048]{0:T(1024)} %param.25) | copy-start | bytes 24580
  105.6 9.3 %copy-start.22 = (f32[2048]{0:T(1024)S(1)}, f32[2048]{0:T(1024)}, u32[]{:S(2)}) copy-start(f32[2048]{0:T(1024)} %param.24) | copy-start | bytes 24580
  108.2 9.8 %copy-start.6 = (s32[256]{0:T(256)}, s32[256]{0:T(256)S(1)}, u32[]{:S(2)}) copy-start(s32[256]{0:T(256)S(1)} %get-tuple-element.250) | copy-start | bytes 3076
  112.1 5.9 %copy-start.8 = (s32[256]{0:T(256)}, s32[256]{0:T(256)S(1)}, u32[]{:S(2)}) copy-start(s32[256]{0:T(256)S(1)} %get-tuple-element.253) | copy-start | bytes 3076
  113.0 1.6 copy-start
  114.5 3.5 %copy-start.11 = (f32[256]{0:T(256)}, f32[256]{0:T(256)S(1)}, u32[]{:S(2)}) copy-start(f32[256]{0:T(256)S(1)} %broadcast_multiply_fusion) | copy-start | bytes 3076
  115.0 3.1 %copy-start.17 = (f32[256]{0:T(256)}, f32[256]{0:T(256)S(1)}, u32[]{:S(2)}) copy-start(f32[256]{0:T(256)S(1)} %add_rsqrt_fusion) | copy-start | bytes 3076
  118.5 7.6 %collective-permute-start = (bf16[256,2,256]{0,2,1:T(8,128)(2,1)S(1)}, bf16[256,2,256]{0,2,1:T(8,128)(2,1)}, u32[]{:S(2)}, u32[]{:S(2)}) collective-permute-start(bf16[256,2,256]{0,2,1:T(8,128)(2,1)S(1)} %get-tuple-element.161), channel_id=1, source_target_pairs={{0,8},{8,16},{16,24},{24,32},{32,40},{40,48},{48,56},{56,64},{64,7... | collective-permute-start | bytes 786440 | tf_op jit(solution)/shard_map/ppermute | solution.py:157
  122.4 7.5 %collective-permute-start.2 = (bf16[256,2,256]{0,2,1:T(8,128)(2,1)S(1)}, bf16[256,2,256]{0,2,1:T(8,128)(2,1)S(1)}, u32[]{:S(2)}, u32[]{:S(2)}) collective-permute-start(bf16[256,2,256]{0,2,1:T(8,128)(2,1)S(1)} %get-tuple-element.161), channel_id=1, source_target_pairs={{0,16},{8,24},{16,32},{24,40},{32,48},{40,56},{48,64},{56,72},{64,... | collective-permute-start | bytes 786440 | tf_op jit(solution)/shard_map/ppermute | solution.py:157
  156.3 1.8 copy-start.12
  156.3 1.8 copy-start.18
  156.3 1.9 copy-start.21
  156.3 1.9 copy-start.23
  156.3 1.9 copy-start.24
  164.7 16.8 %copy-start.1 = (bf16[512,2,256]{2,1,0:T(2,128)(2,1)S(1)}, bf16[512,2,256]{2,1,0:T(2,128)(2,1)}, u32[]{:S(2)}) copy-start(bf16[512,2,256]{2,1,0:T(2,128)(2,1)} %param.35) | copy-start | bytes 1572868
  165.0 16.9 %copy-start.19 = (s32[1,128]{1,0:T(1,128)S(1)}, s32[1,128]{1,0:T(1,128)}, u32[]{:S(2)}) copy-start(s32[1,128]{1,0:T(1,128)} %param.23) | copy-start | bytes 1540
  166.1 40.5 %all-to-all-start = ((bf16[64,2,2048]{2,1,0:T(2,128)(2,1)}), bf16[64,2,2048]{2,1,0:T(2,128)(2,1)S(1)}, u32[]{:S(2)}, u32[]{:S(2)}) async-start(bf16[64,2,2048]{2,1,0:T(2,128)(2,1)} %reshape.277), calls=%async_computation.1 | async-start | bytes 1048576 | tf_op jit(solution)/shard_map/all_to_all | solution.py:323
  206.9 1.5 copy-start.2
  (8 other events, 9.7 us)
Sparse Core Ops, SparseCore 0:
  17.5 32.6 all-gather.1
  163.4 39.1 reduce-scatter.1

commit v14 on v12

--- a/solution.py
+++ b/solution.py
@@ -14,7 +14,7 @@
 PAGE = 4
 WINDOW = 512
 INNER = 4
-HOP_US = 3.5
+HOP_US = 1.5
 LINK_BYTES_PER_US = 45000.0
 
 

time: 208 us -> 216 us (1.038)
  waiting for transfers between devices: 35.1 us -> 38.4 us
  Pallas kernels: 83.5 us -> 86.3 us
    all_to_all x1, waiting for transfers between devices: 24.6 us -> 27.7 us  [shards(): lax.all_to_all(outgoing.reshape(req_count, page_cap, page_width), 'req',...]
    pallas_call x1, Pallas kernels: 83.5 us -> 86.3 us  [ring_gather(): pl.pallas_call(functools.partial(ring_gather_kernel, inner, outer), out_s...]
    all_to_all x1, starting transfers between devices: 16.6 us -> 18.8 us  [shards(): lax.all_to_all(outgoing.reshape(req_count, page_cap, page_width), 'req',...]
where the time goes in v14:
time: 216 us; the launch traced here: 215 us
  Pallas kernels  86.3 us (40%)
  waiting for transfers between devices  38.4 us (18%)
  starting transfers between devices  24 us (11%)
  other arithmetic  21.3 us (10%)
  matrix products  17.7 us (8%)
  between operations  14.7 us (7%)
  local copies, waits for them, and re-layouts  9.83 us (5%)
  loops' own time  2.7 us (1%)
    pallas_call x1, Pallas kernels, ring_gather(): pl.pallas_call(functools.partial(ring_gather_kernel, inner, outer), out_s...  86.3 us
    all_to_all x1, waiting for transfers between devices, shards(): lax.all_to_all(outgoing.reshape(req_count, page_cap, page_width), 'req',...  27.7 us
    all_to_all x1, starting transfers between devices, shards(): lax.all_to_all(outgoing.reshape(req_count, page_cap, page_width), 'req',...  18.8 us
    ppermute x2, waiting for transfers between devices, from_behind(): lax.ppermute(value, axis, [(source, source + steps) for source in range(l...  9.98 us
    ppermute x2, starting transfers between devices, from_behind(): lax.ppermute(value, axis, [(source, source + steps) for source in range(l...  5.12 us
    dot_general x1, matrix products, shards(): lax.dot_general(hidden, fc2_full_t, contract_rows, preferred_element_type...  5.1 us
  transfers between devices with their start and end apart: 5, of which 3 were waited for; matrix products, arithmetic and copies ran while one was open for 9% of the time, Pallas kernels for 40%

profile of v14, /device:TPU:6, one launch (start us, length us, event | category | flops | bytes accessed | tf_op | source)
XLA Modules:
  0.0 214.9 jit_solution(14846236103960287201)
XLA Ops:
  11.0 1.4 pad_maximum_fusion.5.second_block
  12.5 86.3 %shard_map.176 = (bf16[16,4,32,896]{3,2,1,0:T(8,128)(2,1)}, bf16[16,4,32,1280]{3,2,1,0:T(8,128)(2,1)}) custom-call(bf16[32,896]{1,0:T(8,128)(2,1)} %pad_maximum_fusion.6.first_block, bf16[32,1280]{1,0:T(8,128)(2,1)} %pad_maximum_fusion.5.second_block), custom_call_target="tpu_custom_call" | custom-call | tf_op jit(solution)/shard_map/pallas_call | solution.py:137
  98.7 1.1 split.21
  102.4 1.9 constant_dynamic-update-slice_fusion.8
  104.3 1.9 constant_dynamic-update-slice_fusion.4
  106.9 1.5 convert_reduce_fusion
  108.4 1.6 fusion.25
  110.1 3.0 %fusion.32 = f32[256,768]{1,0:T(8,128)S(1)} fusion(bf16[2048,896]{1,0:T(8,128)(2,1)} %bitcast.55, f32[768]{0:T(1024)S(1)} %add.197, bf16[256,2048]{1,0:T(8,128)(2,1)S(1)} %copy-done, f32[2048]{0:T(1024)S(1)} %copy-done.11, f32[2048]{0:T(1024)S(1)} %copy-done.12, f32[256]{0:T(256)S(1)} %add_rsqrt_fusion, f32[256]{0:T(256)S(1)} %broadcast_multiply_fusion), kind=kOutput, calls=%fused_computation.39 | convolution fusion | flops 808648704 | bytes 5002240 | tf_op jit(solution)/shard_map/dot_general | solution.py:296
  113.6 1.3 collective-permute-start
  114.9 3.8 %collective-permute-start.1 = (bf16[512,2,256]{0,2,1:T(8,128)(2,1)S(1)}, bf16[512,2,256]{0,2,1:T(8,128)(2,1)S(1)}, u32[]{:S(2)}, u32[]{:S(2)}) collective-permute-start(bf16[512,2,256]{0,2,1:T(8,128)(2,1)S(1)} %pad_maximum_fusion.1), channel_id=1, source_target_pairs={{0,16},{8,24},{16,32},{24,40},{32,48},{40,56},{48,64},{56,72},{64,... | collective-permute-start | bytes 1572872 | tf_op jit(solution)/shard_map/ppermute | solution.py:157
  118.7 1.8 constant_dynamic-update-slice_fusion
  120.6 4.3 %collective-permute-done = bf16[512,2,256]{0,2,1:T(8,128)(2,1)S(1)} collective-permute-done((bf16[512,2,256]{0,2,1:T(8,128)(2,1)S(1)}, bf16[512,2,256]{0,2,1:T(8,128)(2,1)S(1)}, u32[]{:S(2)}, u32[]{:S(2)}) %collective-permute-start) | collective-permute-done | bytes 524320 | tf_op jit(solution)/shard_map/ppermute | solution.py:157
  124.9 5.7 %collective-permute-done.1 = bf16[512,2,256]{0,2,1:T(8,128)(2,1)S(1)} collective-permute-done((bf16[512,2,256]{0,2,1:T(8,128)(2,1)S(1)}, bf16[512,2,256]{0,2,1:T(8,128)(2,1)S(1)}, u32[]{:S(2)}, u32[]{:S(2)}) %collective-permute-start.1) | collective-permute-done | bytes 524320 | tf_op jit(solution)/shard_map/ppermute | solution.py:157
  130.8 15.9 %while.11 = (s32[]{:T(128)}, bf16[4,256,64]{1,2,0:T(8,128)(2,1)S(1)}, s32[4]{0:T(128)S(1)}, bf16[256,256]{0,1:T(8,128)(2,1)S(1)}, bf16[1536,256]{0,1:T(8,128)(2,...) while((s32[]{:T(128)}, ...), condition=%wide.region_25.26_spmd.clone, body=%wide.region_22.25_spmd.clone.sunk | while | flops 112492032 | bytes 5240527 | solution.py:227
  132.9 0.9 fusion.96
  136.9 0.9 fusion.96
  140.9 0.9 fusion.96
  147.4 1.8 fusion.38
  149.2 5.1 %convolution_add_fusion = f32[256,2048]{1,0:T(8,128)} fusion(f32[256,2048]{1,0:T(8,128)S(1)} %fusion.38, bf16[2048,1280]{1,0:T(8,128)(2,1)} %bitcast.50, f32[512]{0:T(512)S(1)} %copy-done.13, bf16[256,2048]{1,0:T(8,128)(2,1)S(1)} %copy-done, f32[2048]{0:T(1024)S(1)} %copy-done.11, f32[2048]{0:T(1024)S(1)} %copy-done.12, f32[256]{0:T(256)S(1)} %add_rsqrt_fusion, ...), kind=kOutput, calls=%fused_computation.23 | convolution fusion | flops 1078722560 | bytes 9457664 | tf_op jit(solution)/shard_map/dot_general | solution.py:369
  156.0 1.1 reshape.277
  157.2 18.8 %all-to-all-start = ((bf16[64,2,2048]{2,1,0:T(2,128)(2,1)}), bf16[64,2,2048]{2,1,0:T(2,128)(2,1)S(1)}, u32[]{:S(2)}, u32[]{:S(2)}) async-start(bf16[64,2,2048]{2,1,0:T(2,128)(2,1)} %reshape.277), calls=%async_computation.1 | async-start | bytes 1048576 | tf_op jit(solution)/shard_map/all_to_all | solution.py:323
  177.0 27.7 %all-to-all-done = bf16[64,2,2048]{2,1,0:T(2,128)(2,1)S(1)} async-done(((bf16[64,2,2048]{2,1,0:T(2,128)(2,1)}), bf16[64,2,2048]{2,1,0:T(2,128)(2,1)S(1)}, u32[]{:S(2)}, u32[]{:S(2)}) %all-to-all-start) | async-done | bytes 524320 | tf_op jit(solution)/shard_map/all_to_all | solution.py:323
  205.2 1.2 reshape.280
  206.4 1.6 add_convert_fusion
  (111 shorter events, 21.8 us)
Async XLA Ops:
  7.2 93.7 %copy-start.7 = (s32[43]{0:T(128)S(1)}, s32[43]{0:T(128)}, u32[]{:S(2)}) copy-start(s32[43]{0:T(128)} %param.21) | copy-start | bytes 520
  7.2 99.2 %copy-start.5 = (f32[3,256]{1,0:T(4,128)S(1)}, f32[3,256]{1,0:T(4,128)}, u32[]{:S(2)}) copy-start(f32[3,256]{1,0:T(4,128)} %param.27) | copy-start | bytes 9220
  7.2 99.2 %copy-start.3 = (bf16[256,2,256]{2,1,0:T(2,128)(2,1)S(1)}, bf16[256,2,256]{2,1,0:T(2,128)(2,1)}, u32[]{:S(2)}) copy-start(bf16[256,2,256]{2,1,0:T(2,128)(2,1)} %param.34) | copy-start | bytes 786436
  7.2 99.7 %all-gather.2.cloned.1.call-start = ((), (), s32[]{:S(2)}) async-start(), calls=%async_computation.2 | async-start | bytes 1179648 | tf_op jit(solution)/shard_map/all_gather | solution.py:257
  7.9 198.4 %reduce-scatter.2.cloned.1.call-start = ((), (), s32[]{:S(2)}) async-start(), calls=%async_computation.3 | async-start | bytes 2359296 | tf_op jit(solution)/shard_map/reduce_scatter | solution.py:373
  99.8 10.2 %copy-start.11 = (f32[2048]{0:T(1024)S(1)}, f32[2048]{0:T(1024)}, u32[]{:S(2)}) copy-start(f32[2048]{0:T(1024)} %param.25) | copy-start | bytes 24580
  99.8 10.2 %copy-start.12 = (f32[2048]{0:T(1024)S(1)}, f32[2048]{0:T(1024)}, u32[]{:S(2)}) copy-start(f32[2048]{0:T(1024)} %param.24) | copy-start | bytes 24580
  106.9 3.2 %copy-start = (bf16[256,2048]{1,0:T(8,128)(2,1)S(1)}, bf16[256,2048]{1,0:T(8,128)(2,1)}, u32[]{:S(2)}) copy-start(bf16[256,2048]{1,0:T(8,128)(2,1)} %all-gather.2.cloned.1.call-done) | copy-start | bytes 3145732
  113.6 11.3 %collective-permute-start = (bf16[512,2,256]{0,2,1:T(8,128)(2,1)S(1)}, bf16[512,2,256]{0,2,1:T(8,128)(2,1)S(1)}, u32[]{:S(2)}, u32[]{:S(2)}) collective-permute-start(bf16[512,2,256]{0,2,1:T(8,128)(2,1)S(1)} %pad_maximum_fusion.1), channel_id=1, source_target_pairs={{0,8},{8,16},{16,24},{24,32},{32,40},{40,48},{48,56},{56,64},{64,7... | collective-permute-start | bytes 1572872 | tf_op jit(solution)/shard_map/ppermute | solution.py:157
  114.9 15.6 %collective-permute-start.1 = (bf16[512,2,256]{0,2,1:T(8,128)(2,1)S(1)}, bf16[512,2,256]{0,2,1:T(8,128)(2,1)S(1)}, u32[]{:S(2)}, u32[]{:S(2)}) collective-permute-start(bf16[512,2,256]{0,2,1:T(8,128)(2,1)S(1)} %pad_maximum_fusion.1), channel_id=1, source_target_pairs={{0,16},{8,24},{16,32},{24,40},{32,48},{40,56},{48,64},{56,72},{64,... | collective-permute-start | bytes 1572872 | tf_op jit(solution)/shard_map/ppermute | solution.py:157
  146.7 0.7 copy-start.4
  146.7 2.4 %copy-start.13 = (f32[512]{0:T(512)S(1)}, f32[512]{0:T(512)}, u32[]{:S(2)}) copy-start(f32[512]{0:T(512)} %param.31) | copy-start | bytes 6148
  154.3 0.7 copy-start.6
  155.3 21.1 %copy-start.1 = (bf16[512,2,256]{2,1,0:T(2,128)(2,1)S(1)}, bf16[512,2,256]{2,1,0:T(2,128)(2,1)}, u32[]{:S(2)}) copy-start(bf16[512,2,256]{2,1,0:T(2,128)(2,1)} %param.35) | copy-start | bytes 1572868
  155.7 21.1 %copy-start.10 = (s32[1,128]{1,0:T(1,128)S(1)}, s32[1,128]{1,0:T(1,128)}, u32[]{:S(2)}) copy-start(s32[1,128]{1,0:T(1,128)} %param.23) | copy-start | bytes 1540
  157.2 47.5 %all-to-all-start = ((bf16[64,2,2048]{2,1,0:T(2,128)(2,1)}), bf16[64,2,2048]{2,1,0:T(2,128)(2,1)S(1)}, u32[]{:S(2)}, u32[]{:S(2)}) async-start(bf16[64,2,2048]{2,1,0:T(2,128)(2,1)} %reshape.277), calls=%async_computation.1 | async-start | bytes 1048576 | tf_op jit(solution)/shard_map/all_to_all | solution.py:323
  176.8 29.6 %copy-start.2 = (bf16[256,256]{1,0:T(8,128)(2,1)S(1)}, bf16[256,256]{1,0:T(8,128)(2,1)}, u32[]{:S(2)}) copy-start(bf16[256,256]{1,0:T(8,128)(2,1)} %param.19) | copy-start | bytes 393220
  176.8 29.6 %copy-start.8 = (f32[256]{0:T(256)S(1)}, f32[256]{0:T(256)}, u32[]{:S(2)}) copy-start(f32[256]{0:T(256)} %param.33) | copy-start | bytes 3076
  176.8 29.5 %copy-start.9 = (f32[256]{0:T(256)S(1)}, f32[256]{0:T(256)}, u32[]{:S(2)}) copy-start(f32[256]{0:T(256)} %param.29) | copy-start | bytes 3076
Sparse Core Ops, SparseCore 0:
  10.1 34.7 all-gather.1
  154.4 42.9 reduce-scatter.1
